TPU v7x, 256 devices: a whole 4x4x8 slice. The times are simulated.
256 devices in a mesh: gx: 4 (over y), gy: 16 (over z, core), gz: 4 (over x).
Axes of the slice: x: 4, y: 4, z: 8, core: 2. Of those that a mesh axis runs over, the one named last changes fastest.
Arguments:
- frac: float32 [3, 4, 16, 8, 128], P(None, 'gx', 'gy', 'gz'), may hold values from 0 to 1
- velocity: float32 [3, 4, 16, 8, 128], P(None, 'gx', 'gy', 'gz'), may hold values from -2 to 2
- force_old: float32 [3, 4, 16, 8, 128], P(None, 'gx', 'gy', 'gz'), may hold values from -6 to 6
- species: int32 [4, 16, 8, 128], P('gx', 'gy', 'gz'), may hold values from 0 to 9
- cell_count: int32 [4, 16, 8], P('gx', 'gy', 'gz'), may hold values from 1 to 128, as said below
- neighbours: int32 [16, 4, 16, 8, 128], P(None, 'gx', 'gy', 'gz'), may hold values from 0 to 3455, as said below
- embed: bfloat16 [10, 64], replicated, may hold values from -6 to 6
- w_radial_in: bfloat16 [8, 64], replicated, may hold values from -2 to 2
- w_radial_out: bfloat16 [64, 192], replicated, may hold values from -0.75 to 0.75
- w_node: bfloat16 [256, 64], replicated, may hold values from -0.375 to 0.375
- w_energy: float32 [64], replicated, may hold values from -0.75 to 0.75
Outputs:
- next_frac: float32 [3, 4, 16, 8, 128], P(None, 'gx', 'gy', 'gz')
- next_velocity: float32 [3, 4, 16, 8, 128], P(None, 'gx', 'gy', 'gz')
- next_force: float32 [3, 4, 16, 8, 128], P(None, 'gx', 'gy', 'gz')
- site_energy: float32 [4, 16, 8, 128], P('gx', 'gy', 'gz')
Inputs may be any that keep to these rules, and one draw needn't show every extreme that they name: `cell_count`: in every draw at least one cell holds exactly 128 atoms; the other cells hold 1 to 128. `neighbours`: each code o * 128 + s names slot s of the cell at offset (o // 9 - 1, (o // 3) % 3 - 1, o % 3 - 1) from the receiver's cell, periodic; s is below that cell's count; no code names the receiver itself.
All inputs are finite; a program needn't handle non-finite values.
Results may differ from a plain program's by a relative error of at most 0.015.
Values may be sent and summed in bfloat16 or wider, within the bound.
No kernel may reach another device: no remote copies, remote signals or barrier semaphores. Data moves between devices by JAX's collectives and lax.ppermute only.
A program may use at most 64 MiB of HBM per device.

v0:
```python
import jax
import jax.numpy as jnp
from jax import lax
from jax.sharding import PartitionSpec as P

MASSES = (1.008, 12.011, 14.007, 15.999, 32.06, 22.99, 35.45, 39.098, 24.305, 40.078)
SQRT3 = 1.7320508075688772
HALF_SQRT3 = 0.8660254037844386
TIME_STEP = 0.5


def padded(array, sides, width):
    for axis, dim in sides:
        size, length = (lax.axis_size(axis), array.shape[dim])
        up = [(i, (i + 1) % size) for i in range(size)]
        down = [(j, i) for i, j in up]
        last = lax.slice_in_dim(array, length - width, length, axis=dim)
        leading = lax.slice_in_dim(array, 0, width, axis=dim)
        before = lax.ppermute(last, axis, up)
        after = lax.ppermute(leading, axis, down)
        array = jnp.concatenate([before, array, after], axis=dim)
    return array


def species_mass(species):
    table = jnp.asarray(MASSES, dtype=jnp.float32) / 16.0
    shape_ones = (1,) * species.ndim
    which = species[None] == jnp.arange(len(MASSES), dtype=jnp.int32).reshape((-1,) + shape_ones)
    return jnp.sum(jnp.where(which, table.reshape((-1,) + shape_ones), 0.0), axis=0)


def embed_species(species_flat, embed):
    kinds = embed.shape[0]
    onehot = (species_flat[None, :] == jnp.arange(kinds, dtype=jnp.int32)[:, None]).astype(
        jnp.bfloat16
    )
    return jnp.dot(embed.T, onehot, preferred_element_type=jnp.float32).astype(jnp.bfloat16)


def site_terms(displace, send_feat, own_feat, w_radial_in, w_radial_out, w_node, w_energy):
    basis_count = w_radial_in.shape[0]
    channels = own_feat.shape[0]
    candidates = displace.shape[1]
    block_size = displace.shape[2]
    squared = jnp.sum(displace * displace, axis=0)
    envelope = jnp.maximum(1.0 - squared, 0.0) ** 3
    centres = jnp.arange(basis_count, dtype=jnp.float32) / (basis_count - 1)
    basis_values = jnp.exp(
        -float((basis_count - 1) ** 2) * (squared[None] - centres[:, None, None]) ** 2
    )
    basis_values = basis_values.astype(jnp.bfloat16).reshape(basis_count, candidates * block_size)
    hidden = jax.nn.silu(
        jnp.dot(w_radial_in.T, basis_values, preferred_element_type=jnp.float32)
    ).astype(jnp.bfloat16)
    radial = jnp.dot(w_radial_out.T, hidden, preferred_element_type=jnp.float32)
    radial = radial.reshape(3, channels, candidates, block_size) * envelope[None, None]
    along_x = displace[0]
    along_y = displace[1]
    along_z = displace[2]
    first_order = jnp.stack([along_x, along_y, along_z])
    second_order = jnp.stack(
        [
            SQRT3 * along_x * along_y,
            SQRT3 * along_y * along_z,
            SQRT3 * along_z * along_x,
            HALF_SQRT3 * (along_x * along_x - along_y * along_y),
            0.5 * (2.0 * along_z * along_z - along_x * along_x - along_y * along_y),
        ]
    )
    carried = radial * send_feat.astype(jnp.float32)[None]
    scalar_part = jnp.sum(carried[0], axis=1)
    vector_part = jnp.sum(carried[1][None] * first_order[:, None], axis=2)
    tensor_part = jnp.sum(carried[2][None] * second_order[:, None], axis=2)
    invariant = jnp.concatenate(
        [
            scalar_part,
            jnp.sum(vector_part * vector_part, axis=0),
            jnp.sum(tensor_part * tensor_part, axis=0),
            own_feat.astype(jnp.float32),
        ],
        axis=0,
    ).astype(jnp.bfloat16)
    activity = jax.nn.silu(jnp.dot(w_node.T, invariant, preferred_element_type=jnp.float32))
    return jnp.sum(w_energy[:, None] * activity, axis=0)


def fold_axis(summed, axis_dim):
    length = summed.shape[axis_dim] - 6
    middle = lax.slice_in_dim(summed, 3, length + 3, axis=axis_dim)
    from_lower = lax.slice_in_dim(summed, 1, 2, axis=axis_dim)
    from_upper = lax.slice_in_dim(summed, length + 4, length + 5, axis=axis_dim)
    widths_low = [(0, 0)] * summed.ndim
    widths_low[axis_dim] = (0, length - 1)
    widths_high = [(0, 0)] * summed.ndim
    widths_high[axis_dim] = (length - 1, 0)
    return middle + jnp.pad(from_lower, widths_low) + jnp.pad(from_upper, widths_high)


def shards(
    frac,
    velocity,
    force_old,
    species,
    cell_count,
    neighbours,
    embed,
    w_radial_in,
    w_radial_out,
    w_node,
    w_energy,
):
    cells_x, cells_y, cells_z, capacity = species.shape
    candidates = neighbours.shape[0]
    local_slots = cells_x * cells_y * cells_z * capacity
    wide_y = cells_y + 2
    wide_z = cells_z + 2
    block_size = cells_z * capacity
    occupied_int = (
        lax.broadcasted_iota(jnp.int32, species.shape, 3) < cell_count[..., None]
    ).astype(jnp.int32)
    occupied = occupied_int.astype(jnp.float32)
    atom_mass = species_mass(species)
    half_velocity = velocity + 0.5 * TIME_STEP * force_old / atom_mass
    moved = frac + TIME_STEP * half_velocity
    ghost_moved = padded(moved, (("gx", 1), ("gy", 2), ("gz", 3)), 1)
    own_feats = embed_species(species.reshape(local_slots), embed)
    channels = own_feats.shape[0]
    moved_flat = moved.reshape(3, local_slots)
    ghost_pos_flat = ghost_moved.reshape(3, -1)
    codes = neighbours.reshape(candidates, local_slots)
    occupied_flat = occupied.reshape(local_slots)
    receiver_order = jnp.arange(local_slots, dtype=jnp.int32)
    passes = local_slots // block_size
    cell_id = receiver_order // capacity
    cell_a = (cell_id // (cells_y * cells_z))[None, :]
    cell_b = (cell_id // cells_z % cells_y)[None, :]
    cell_c = (cell_id % cells_z)[None, :]
    offset = codes // capacity
    slot_id = codes % capacity
    shift_a = offset // 9 - 1
    shift_b = offset // 3 % 3 - 1
    shift_c = offset % 3 - 1
    senders_all = (
        ((cell_a + 1 + shift_a) * wide_y + cell_b + 1 + shift_b) * wide_z + cell_c + 1 + shift_c
    ) * capacity + slot_id
    cell_shift = jnp.stack([shift_a, shift_b, shift_c]).astype(jnp.float32)
    displace_all = cell_shift + ghost_pos_flat[:, senders_all] - moved_flat[:, None, :]
    ghost_kinds = padded(species, (("gx", 0), ("gy", 1), ("gz", 2)), 1)
    sender_kinds = ghost_kinds.reshape(-1)[senders_all]

    def sender_features():
        return embed_species(sender_kinds.reshape(-1), embed).reshape(
            channels, candidates, block_size
        )

    def one_block(number, carried):
        send_feat = sender_features()

        def energy_of(shifted):
            return site_terms(
                shifted, send_feat, own_feats, w_radial_in, w_radial_out, w_node, w_energy
            )

        energy, pullback = jax.vjp(energy_of, displace_all)
        gradient = pullback(occupied_flat)[0]
        return (gradient, energy)

    start_state = (
        jnp.zeros((3, candidates, local_slots), jnp.float32),
        jnp.zeros((local_slots,), jnp.float32),
    )
    gradients, energies_ord = lax.fori_loop(0, passes, one_block, start_state)
    own_force_ord = jnp.sum(gradients, axis=1)
    sender_force = jnp.zeros((3, (cells_x + 2) * wide_y * wide_z * capacity), jnp.float32)
    sender_force = sender_force.at[:, senders_all.reshape(-1)].add(-gradients.reshape(3, -1))
    extended = sender_force.reshape(3, cells_x + 2, wide_y, wide_z, capacity)
    returned = padded(extended.astype(jnp.bfloat16), (("gx", 1), ("gy", 2), ("gz", 3)), 2).astype(
        extended.dtype
    )
    folded = fold_axis(fold_axis(fold_axis(returned, 1), 2), 3)
    total_force = own_force_ord.reshape(3, cells_x, cells_y, cells_z, capacity) + folded
    next_force = occupied * total_force
    next_velocity = occupied * (half_velocity + 0.5 * TIME_STEP * next_force / atom_mass)
    next_frac = occupied * moved
    site_energy = occupied * energies_ord.reshape(cells_x, cells_y, cells_z, capacity)
    return (next_frac, next_velocity, next_force, site_energy)


def solution(mesh):
    in_specs = (
        P(None, "gx", "gy", "gz", None),
        P(None, "gx", "gy", "gz", None),
        P(None, "gx", "gy", "gz", None),
        P("gx", "gy", "gz", None),
        P("gx", "gy", "gz"),
        P(None, "gx", "gy", "gz", None),
        P(),
        P(),
        P(),
        P(),
        P(),
    )
    out_specs = (
        P(None, "gx", "gy", "gz", None),
        P(None, "gx", "gy", "gz", None),
        P(None, "gx", "gy", "gz", None),
        P("gx", "gy", "gz", None),
    )
    return jax.shard_map(shards, mesh=mesh, in_specs=in_specs, out_specs=out_specs, check_vma=False)
```

profile of v0, /device:TPU:6, one launch (start us, length us, event | category | flops | bytes accessed | tf_op | source)
XLA Modules:
  0.0 133.5 jit_solution(25429434532969515)
XLA Ops:
  2.2 1.3 broadcast_multiply_fusion
  3.5 1.6 %collective-permute-start = (f32[3,1,1,2,128]{4,3,2,1,0:T(2,128)S(1)}, f32[3,1,1,2,128]{4,3,2,1,0:T(2,128)S(1)}, u32[]{:S(2)}, u32[]{:S(2)}) collective-permute-start(f32[3,1,1,2,128]{4,3,2,1,0:T(2,128)S(1)} %get-tuple-element.35), channel_id=1, source_target_pairs={{0,64},{64,128},{128,192},{192,0},{1,65},{65,129},{129,193},{193,1... | collective-permute-start | bytes 9224 | tf_op jit(solution)/shard_map/ppermute | solution.py:19
  5.1 1.7 %collective-permute-start.1 = (f32[3,1,1,2,128]{4,3,2,1,0:T(2,128)S(1)}, f32[3,1,1,2,128]{4,3,2,1,0:T(2,128)S(1)}, u32[]{:S(2)}, u32[]{:S(2)}) collective-permute-start(f32[3,1,1,2,128]{4,3,2,1,0:T(2,128)S(1)} %get-tuple-element.35), channel_id=1, source_target_pairs={{64,0},{128,64},{192,128},{0,192},{65,1},{129,65},{193,129},{1,193... | collective-permute-start | bytes 9224 | tf_op jit(solution)/shard_map/ppermute | solution.py:20
  7.1 2.9 %collective-permute-start.7 = (s32[1,1,2,128]{3,2,1,0:T(2,128)}, s32[1,1,2,128]{3,2,1,0:T(2,128)S(1)}, u32[]{:S(2)}, u32[]{:S(2)}) collective-permute-start(s32[1,1,2,128]{3,2,1,0:T(2,128)} %param.15), channel_id=1, source_target_pairs={{64,0},{128,64},{192,128},{0,192},{65,1},{129,65},{193,129},{1,193... | collective-permute-start | bytes 3080 | tf_op jit(solution)/shard_map/ppermute | solution.py:20
  12.3 1.5 %fusion.16 = bf16[64,256]{1,0:T(8,128)(2,1)} fusion(bf16[10,64]{1,0:T(8,128)(2,1)} %param.18, s32[256]{0:T(256)} %bitcast.129), kind=kOutput, calls=%fused_computation.36 | convolution fusion | flops 346624 | bytes 35072 | tf_op jit(solution)/shard_map/dot_general | solution.py:37
  13.8 1.8 %compare_select_fusion = s32[4096,1]{0,1:T(1,128)} fusion(s32[4096,1]{0,1:T(1,128)S(1)} %bitcast.125, s32[4096,1]{0,1:T(1,128)S(1)} %bitcast.124, s32[4096,1]{0,1:T(1,128)} %bitcast.119), kind=kLoop, calls=%fused_computation.70 | loop fusion | flops 241664 | bytes 65536 | tf_op jit(solution)/shard_map/select_n | solution.py:175
  17.5 4.2 %collective-permute-start.9 = (s32[3,1,2,128]{3,2,1,0:T(2,128)S(1)}, s32[3,1,2,128]{3,2,1,0:T(2,128)S(1)}, u32[]{:S(2)}, u32[]{:S(2)}) collective-permute-start(s32[3,1,2,128]{3,2,1,0:T(2,128)S(1)} %constant_dynamic-update-slice_fusion), channel_id=1, source_target_pairs={{4,0},{8,4},{12,8},{16,12},{20,16},{24,20},{28,24},{32,28},{36,32}... | collective-permute-start | bytes 9224 | tf_op jit(solution)/shard_map/ppermute | solution.py:20
  25.3 2.9 %collective-permute-start.3 = (f32[3,3,1,2,128]{4,3,2,1,0:T(2,128)S(1)}, f32[3,3,1,2,128]{4,3,2,1,0:T(2,128)S(1)}, u32[]{:S(2)}, u32[]{:S(2)}) collective-permute-start(f32[3,3,1,2,128]{4,3,2,1,0:T(2,128)S(1)} %pad_maximum_fusion.4), channel_id=1, source_target_pairs={{4,0},{8,4},{12,8},{16,12},{20,16},{24,20},{28,24},{32,28},{36,32}... | collective-permute-start | bytes 27656 | tf_op jit(solution)/shard_map/ppermute | solution.py:20
  29.0 23.0 %gather_fusion.1 = s32[4096]{0:T(1024)S(1)} fusion(s32[4608]{0:T(1024)S(1)} %reshape.948, s32[4096]{0:T(1024)S(1)} %broadcast_clamp_fusion), kind=kCustom, calls=%fused_computation.1 | custom fusion | bytes 49152 | tf_op jit(solution)/shard_map/gather | solution.py:149
  52.1 1.5 %collective-permute-start.4 = (f32[3,3,3,1,128]{4,3,2,1,0:T(1,128)S(1)}, f32[3,3,3,1,128]{4,3,2,1,0:T(1,128)S(1)}, u32[]{:S(2)}, u32[]{:S(2)}) collective-permute-start(f32[3,3,3,1,128]{4,3,2,1,0:T(1,128)S(1)} %get-tuple-element.65), channel_id=1, source_target_pairs={{0,1},{1,2},{2,3},{3,0},{4,5},{5,6},{6,7},{7,4},{8,9},{9,10},{10,1... | collective-permute-start | bytes 41480 | tf_op jit(solution)/shard_map/ppermute | solution.py:19
  55.9 2.6 %collective-permute-done.5 = f32[3,3,3,1,128]{4,3,2,1,0:T(1,128)S(1)} collective-permute-done((f32[3,3,3,1,128]{4,3,2,1,0:T(1,128)S(1)}, f32[3,3,3,1,128]{4,3,2,1,0:T(1,128)S(1)}, u32[]{:S(2)}, u32[]{:S(2)}) %collective-permute-start.5) | collective-permute-done | bytes 13856 | tf_op jit(solution)/shard_map/ppermute | solution.py:20
  59.3 14.2 %gather_fusion = f32[4096,3]{1,0:T(8,128)} fusion(f32[3,4608]{0,1:T(8,128)S(1)} %bitcast.112, s32[4096]{0:T(1024)S(1)} %broadcast_clamp_fusion), kind=kCustom, calls=%fused_computation | custom fusion | bytes 114688 | tf_op jit(solution)/shard_map/gather | solution.py:147
  73.4 2.2 %copy.47 = f32[16,256,3]{1,0,2:T(8,128)S(1)} copy(f32[16,256,3]{2,1,0:T(8,128)} %bitcast.114) | data formatting | bytes 98304 | tf_op jit(solution)/shard_map/gather | solution.py:147
  81.6 1.4 %multiply_reduce_fusion.2 = f32[5,64,256]{2,1,0:T(8,128)S(1)} fusion(f32[5,16,256]{2,1,0:T(8,128)S(1)} %fusion.53, f32[64,16,256]{2,1,0:T(8,128)S(1)} %get-tuple-element.51), kind=kLoop, calls=%fused_computation.5 | loop fusion | flops 2539520 | bytes 1458176 | tf_op jit(solution)/shard_map/while/body/eval_jaxpr/jvp()/reduce_sum | solution.py:73
  88.5 2.0 %copy.54 = f32[3,16,256]{0,2,1:T(8,128)} copy(f32[3,16,256]{2,1,0:T(8,128)S(1)} %get-tuple-element.59) | data formatting | bytes 98304 | tf_op jit(solution)/shard_map/neg | solution.py:175
  90.5 23.4 %scatter_custom_fusion = f32[3,4608]{0,1:T(8,128)S(1)} fusion(s32[4096]{0:T(1024)} %bitcast.126, f32[4096,3]{1,0:T(8,128)} %bitcast.115, f32[]{:T(128)} %constant.144.clone.1), kind=kCustom, calls=%fused_computation.28 | custom fusion | flops 12288 | bytes 55808 | tf_op jit(solution)/shard_map/scatter-add | solution.py:175
  115.1 1.7 %copy.50 = bf16[3,3,3,4,128]{4,3,2,1,0:T(4,128)(2,1)S(1)} copy(bf16[3,3,3,4,128]{0,4,3,2,1:T(8,128)(2,1)} %bitcast.110) | data formatting | bytes 55296 | tf_op jit(solution)/shard_map/convert_element_type | solution.py:177
  116.9 3.2 %collective-permute-start.13 = (bf16[3,2,3,4,128]{4,3,2,1,0:T(4,128)(2,1)S(1)}, bf16[3,2,3,4,128]{4,3,2,1,0:T(4,128)(2,1)S(1)}, u32[]{:S(2)}, u32[]{:S(2)}) collective-permute-start(bf16[3,2,3,4,128]{4,3,2,1,0:T(4,128)(2,1)S(1)} %get-tuple-element.64), channel_id=1, source_target_pairs={{64,0},{128,64},{192,128},{0,192},{65,1},{129,65},{193,129},{1,193... | collective-permute-start | bytes 55304 | tf_op jit(solution)/shard_map/ppermute | solution.py:20
  120.1 1.7 %collective-permute-done.12 = bf16[3,2,3,4,128]{4,3,2,1,0:T(4,128)(2,1)S(1)} collective-permute-done((bf16[3,2,3,4,128]{4,3,2,1,0:T(4,128)(2,1)S(1)}, bf16[3,2,3,4,128]{4,3,2,1,0:T(4,128)(2,1)S(1)}, u32[]{:S(2)}, u32[]{:S(2)}) %collective-permute-start.12) | collective-permute-done | bytes 18464 | tf_op jit(solution)/shard_map/ppermute | solution.py:19
  122.0 2.9 %collective-permute-start.15 = (bf16[3,7,2,4,128]{4,3,2,1,0:T(4,128)(2,1)S(1)}, bf16[3,7,2,4,128]{4,3,2,1,0:T(4,128)(2,1)S(1)}, u32[]{:S(2)}, u32[]{:S(2)}) collective-permute-start(bf16[3,7,2,4,128]{4,3,2,1,0:T(4,128)(2,1)S(1)} %get-tuple-element.62), channel_id=1, source_target_pairs={{4,0},{8,4},{12,8},{16,12},{20,16},{24,20},{28,24},{32,28},{36,32}... | collective-permute-start | bytes 129032 | tf_op jit(solution)/shard_map/ppermute | solution.py:20
  124.9 1.7 %collective-permute-done.14 = bf16[3,7,2,4,128]{4,3,2,1,0:T(4,128)(2,1)S(1)} collective-permute-done((bf16[3,7,2,4,128]{4,3,2,1,0:T(4,128)(2,1)S(1)}, bf16[3,7,2,4,128]{4,3,2,1,0:T(4,128)(2,1)S(1)}, u32[]{:S(2)}, u32[]{:S(2)}) %collective-permute-start.14) | collective-permute-done | bytes 43040 | tf_op jit(solution)/shard_map/ppermute | solution.py:19
  126.9 2.0 %collective-permute-start.17 = (bf16[3,7,7,2,128]{4,3,2,1,0:T(2,128)(2,1)S(1)}, bf16[3,7,7,2,128]{4,3,2,1,0:T(2,128)(2,1)S(1)}, u32[]{:S(2)}, u32[]{:S(2)}) collective-permute-start(bf16[3,7,7,2,128]{4,3,2,1,0:T(2,128)(2,1)S(1)} %get-tuple-element.58), channel_id=1, source_target_pairs={{1,0},{2,1},{3,2},{0,3},{5,4},{6,5},{7,6},{4,7},{9,8},{10,9},{11,1... | collective-permute-start | bytes 225800 | tf_op jit(solution)/shard_map/ppermute | solution.py:20
  129.8 1.5 %collective-permute-done.16 = bf16[3,7,7,2,128]{4,3,2,1,0:T(2,128)(2,1)S(1)} collective-permute-done((bf16[3,7,7,2,128]{4,3,2,1,0:T(2,128)(2,1)S(1)}, bf16[3,7,7,2,128]{4,3,2,1,0:T(2,128)(2,1)S(1)}, u32[]{:S(2)}, u32[]{:S(2)}) %collective-permute-start.16) | collective-permute-done | bytes 75296 | tf_op jit(solution)/shard_map/ppermute | solution.py:19
  131.3 1.3 collective-permute-done.17
  (132 shorter events, 27.9 us)
Async XLA Ops:
  0.6 76.8 %copy-start = (bf16[64,192]{1,0:T(8,128)(2,1)S(1)}, bf16[64,192]{1,0:T(8,128)(2,1)}, u32[]{:S(2)}) copy-start(bf16[64,192]{1,0:T(8,128)(2,1)} %param.20) | copy-start | bytes 73732
  3.5 21.7 %collective-permute-start = (f32[3,1,1,2,128]{4,3,2,1,0:T(2,128)S(1)}, f32[3,1,1,2,128]{4,3,2,1,0:T(2,128)S(1)}, u32[]{:S(2)}, u32[]{:S(2)}) collective-permute-start(f32[3,1,1,2,128]{4,3,2,1,0:T(2,128)S(1)} %get-tuple-element.35), channel_id=1, source_target_pairs={{0,64},{64,128},{128,192},{192,0},{1,65},{65,129},{129,193},{193,1... | collective-permute-start | bytes 9224 | tf_op jit(solution)/shard_map/ppermute | solution.py:19
  5.1 20.2 %collective-permute-start.1 = (f32[3,1,1,2,128]{4,3,2,1,0:T(2,128)S(1)}, f32[3,1,1,2,128]{4,3,2,1,0:T(2,128)S(1)}, u32[]{:S(2)}, u32[]{:S(2)}) collective-permute-start(f32[3,1,1,2,128]{4,3,2,1,0:T(2,128)S(1)} %get-tuple-element.35), channel_id=1, source_target_pairs={{64,0},{128,64},{192,128},{0,192},{65,1},{129,65},{193,129},{1,193... | collective-permute-start | bytes 9224 | tf_op jit(solution)/shard_map/ppermute | solution.py:20
  6.7 10.1 %collective-permute-start.6 = (s32[1,1,2,128]{3,2,1,0:T(2,128)}, s32[1,1,2,128]{3,2,1,0:T(2,128)S(1)}, u32[]{:S(2)}, u32[]{:S(2)}) collective-permute-start(s32[1,1,2,128]{3,2,1,0:T(2,128)} %param.15), channel_id=1, source_target_pairs={{0,64},{64,128},{128,192},{192,0},{1,65},{65,129},{129,193},{193,1... | collective-permute-start | bytes 3080 | tf_op jit(solution)/shard_map/ppermute | solution.py:19
  7.1 10.4 %collective-permute-start.7 = (s32[1,1,2,128]{3,2,1,0:T(2,128)}, s32[1,1,2,128]{3,2,1,0:T(2,128)S(1)}, u32[]{:S(2)}, u32[]{:S(2)}) collective-permute-start(s32[1,1,2,128]{3,2,1,0:T(2,128)} %param.15), channel_id=1, source_target_pairs={{64,0},{128,64},{192,128},{0,192},{65,1},{129,65},{193,129},{1,193... | collective-permute-start | bytes 3080 | tf_op jit(solution)/shard_map/ppermute | solution.py:20
  17.5 5.5 %collective-permute-start.8 = (s32[3,1,2,128]{3,2,1,0:T(2,128)S(1)}, s32[3,1,2,128]{3,2,1,0:T(2,128)S(1)}, u32[]{:S(2)}, u32[]{:S(2)}) collective-permute-start(s32[3,1,2,128]{3,2,1,0:T(2,128)S(1)} %constant_dynamic-update-slice_fusion), channel_id=1, source_target_pairs={{0,4},{4,8},{8,12},{12,16},{16,20},{20,24},{24,28},{28,32},{32,36}... | collective-permute-start | bytes 9224 | tf_op jit(solution)/shard_map/ppermute | solution.py:19
  17.5 5.6 %collective-permute-start.9 = (s32[3,1,2,128]{3,2,1,0:T(2,128)S(1)}, s32[3,1,2,128]{3,2,1,0:T(2,128)S(1)}, u32[]{:S(2)}, u32[]{:S(2)}) collective-permute-start(s32[3,1,2,128]{3,2,1,0:T(2,128)S(1)} %constant_dynamic-update-slice_fusion), channel_id=1, source_target_pairs={{4,0},{8,4},{12,8},{16,12},{20,16},{24,20},{28,24},{32,28},{36,32}... | collective-permute-start | bytes 9224 | tf_op jit(solution)/shard_map/ppermute | solution.py:20
  23.1 5.1 %collective-permute-start.10 = (s32[3,3,1,128]{3,2,1,0:T(1,128)S(1)}, s32[3,3,1,128]{3,2,1,0:T(1,128)S(1)}, u32[]{:S(2)}, u32[]{:S(2)}) collective-permute-start(s32[3,3,1,128]{3,2,1,0:T(1,128)S(1)} %get-tuple-element.72), channel_id=1, source_target_pairs={{0,1},{1,2},{2,3},{3,0},{4,5},{5,6},{6,7},{7,4},{8,9},{9,10},{10,1... | collective-permute-start | bytes 13832 | tf_op jit(solution)/shard_map/ppermute | solution.py:19
  24.1 4.8 %collective-permute-start.11 = (s32[3,3,1,128]{3,2,1,0:T(1,128)S(1)}, s32[3,3,1,128]{3,2,1,0:T(1,128)S(1)}, u32[]{:S(2)}, u32[]{:S(2)}) collective-permute-start(s32[3,3,1,128]{3,2,1,0:T(1,128)S(1)} %get-tuple-element.73), channel_id=1, source_target_pairs={{1,0},{2,1},{3,2},{0,3},{5,4},{6,5},{7,6},{4,7},{9,8},{10,9},{11,1... | collective-permute-start | bytes 13832 | tf_op jit(solution)/shard_map/ppermute | solution.py:20
  25.2 26.8 %collective-permute-start.2 = (f32[3,3,1,2,128]{4,3,2,1,0:T(2,128)S(1)}, f32[3,3,1,2,128]{4,3,2,1,0:T(2,128)S(1)}, u32[]{:S(2)}, u32[]{:S(2)}) collective-permute-start(f32[3,3,1,2,128]{4,3,2,1,0:T(2,128)S(1)} %pad_maximum_fusion.4), channel_id=1, source_target_pairs={{0,4},{4,8},{8,12},{12,16},{16,20},{20,24},{24,28},{28,32},{32,36}... | collective-permute-start | bytes 27656 | tf_op jit(solution)/shard_map/ppermute | solution.py:19
  25.3 26.8 %collective-permute-start.3 = (f32[3,3,1,2,128]{4,3,2,1,0:T(2,128)S(1)}, f32[3,3,1,2,128]{4,3,2,1,0:T(2,128)S(1)}, u32[]{:S(2)}, u32[]{:S(2)}) collective-permute-start(f32[3,3,1,2,128]{4,3,2,1,0:T(2,128)S(1)} %pad_maximum_fusion.4), channel_id=1, source_target_pairs={{4,0},{8,4},{12,8},{16,12},{20,16},{24,20},{28,24},{32,28},{36,32}... | collective-permute-start | bytes 27656 | tf_op jit(solution)/shard_map/ppermute | solution.py:20
  29.0 25.2 %copy-start.6 = (bf16[10,64]{1,0:T(8,128)(2,1)S(1)}, bf16[10,64]{1,0:T(8,128)(2,1)}, u32[]{:S(2)}) copy-start(bf16[10,64]{1,0:T(8,128)(2,1)} %param.18) | copy-start | bytes 3844
  52.1 3.8 %collective-permute-start.4 = (f32[3,3,3,1,128]{4,3,2,1,0:T(1,128)S(1)}, f32[3,3,3,1,128]{4,3,2,1,0:T(1,128)S(1)}, u32[]{:S(2)}, u32[]{:S(2)}) collective-permute-start(f32[3,3,3,1,128]{4,3,2,1,0:T(1,128)S(1)} %get-tuple-element.65), channel_id=1, source_target_pairs={{0,1},{1,2},{2,3},{3,0},{4,5},{5,6},{6,7},{7,4},{8,9},{9,10},{10,1... | collective-permute-start | bytes 41480 | tf_op jit(solution)/shard_map/ppermute | solution.py:19
  53.6 4.9 %collective-permute-start.5 = (f32[3,3,3,1,128]{4,3,2,1,0:T(1,128)S(1)}, f32[3,3,3,1,128]{4,3,2,1,0:T(1,128)S(1)}, u32[]{:S(2)}, u32[]{:S(2)}) collective-permute-start(f32[3,3,3,1,128]{4,3,2,1,0:T(1,128)S(1)} %get-tuple-element.66), channel_id=1, source_target_pairs={{1,0},{2,1},{3,2},{0,3},{5,4},{6,5},{7,6},{4,7},{9,8},{10,9},{11,1... | collective-permute-start | bytes 41480 | tf_op jit(solution)/shard_map/ppermute | solution.py:20
  113.9 15.0 %copy-start.12 = (s32[1,1,2]{2,1,0:T(1,128)S(1)}, s32[1,1,2]{2,1,0:T(1,128)}, u32[]{:S(2)}) copy-start(s32[1,1,2]{2,1,0:T(1,128)} %param.16) | copy-start | bytes 28
  113.9 18.9 %copy-start.3 = (f32[3,1,1,2,128]{4,3,2,1,0:T(2,128)S(1)}, f32[3,1,1,2,128]{4,3,2,1,0:T(2,128)}, u32[]{:S(2)}) copy-start(f32[3,1,1,2,128]{4,3,2,1,0:T(2,128)} %get-tuple-element.48) | copy-start | bytes 9220
  113.9 18.9 %copy-start.5 = (f32[2,128]{1,0:T(2,128)S(1)}, f32[2,128]{1,0:T(2,128)}, u32[]{:S(2)}) copy-start(f32[2,128]{1,0:T(2,128)} %copy-done.4) | copy-start | bytes 3076
  114.0 18.9 %copy-start.8 = (f32[2,128]{1,0:T(2,128)S(1)}, f32[2,128]{1,0:T(2,128)}, u32[]{:S(2)}) copy-start(f32[2,128]{1,0:T(2,128)} %copy-done.7) | copy-start | bytes 3076
  116.8 5.0 %collective-permute-start.12 = (bf16[3,2,3,4,128]{4,3,2,1,0:T(4,128)(2,1)S(1)}, bf16[3,2,3,4,128]{4,3,2,1,0:T(4,128)(2,1)S(1)}, u32[]{:S(2)}, u32[]{:S(2)}) collective-permute-start(bf16[3,2,3,4,128]{4,3,2,1,0:T(4,128)(2,1)S(1)} %get-tuple-element.63), channel_id=1, source_target_pairs={{0,64},{64,128},{128,192},{192,0},{1,65},{65,129},{129,193},{193,1... | collective-permute-start | bytes 55304 | tf_op jit(solution)/shard_map/ppermute | solution.py:19
  116.9 5.0 %collective-permute-start.13 = (bf16[3,2,3,4,128]{4,3,2,1,0:T(4,128)(2,1)S(1)}, bf16[3,2,3,4,128]{4,3,2,1,0:T(4,128)(2,1)S(1)}, u32[]{:S(2)}, u32[]{:S(2)}) collective-permute-start(bf16[3,2,3,4,128]{4,3,2,1,0:T(4,128)(2,1)S(1)} %get-tuple-element.64), channel_id=1, source_target_pairs={{64,0},{128,64},{192,128},{0,192},{65,1},{129,65},{193,129},{1,193... | collective-permute-start | bytes 55304 | tf_op jit(solution)/shard_map/ppermute | solution.py:20
  122.0 4.7 %collective-permute-start.14 = (bf16[3,7,2,4,128]{4,3,2,1,0:T(4,128)(2,1)S(1)}, bf16[3,7,2,4,128]{4,3,2,1,0:T(4,128)(2,1)S(1)}, u32[]{:S(2)}, u32[]{:S(2)}) collective-permute-start(bf16[3,7,2,4,128]{4,3,2,1,0:T(4,128)(2,1)S(1)} %get-tuple-element.61), channel_id=1, source_target_pairs={{0,4},{4,8},{8,12},{12,16},{16,20},{20,24},{24,28},{28,32},{32,36}... | collective-permute-start | bytes 129032 | tf_op jit(solution)/shard_map/ppermute | solution.py:19
  122.0 4.6 %collective-permute-start.15 = (bf16[3,7,2,4,128]{4,3,2,1,0:T(4,128)(2,1)S(1)}, bf16[3,7,2,4,128]{4,3,2,1,0:T(4,128)(2,1)S(1)}, u32[]{:S(2)}, u32[]{:S(2)}) collective-permute-start(bf16[3,7,2,4,128]{4,3,2,1,0:T(4,128)(2,1)S(1)} %get-tuple-element.62), channel_id=1, source_target_pairs={{4,0},{8,4},{12,8},{16,12},{20,16},{24,20},{28,24},{32,28},{36,32}... | collective-permute-start | bytes 129032 | tf_op jit(solution)/shard_map/ppermute | solution.py:20
  126.8 4.4 %collective-permute-start.16 = (bf16[3,7,7,2,128]{4,3,2,1,0:T(2,128)(2,1)S(1)}, bf16[3,7,7,2,128]{4,3,2,1,0:T(2,128)(2,1)S(1)}, u32[]{:S(2)}, u32[]{:S(2)}) collective-permute-start(bf16[3,7,7,2,128]{4,3,2,1,0:T(2,128)(2,1)S(1)} %get-tuple-element.57), channel_id=1, source_target_pairs={{0,1},{1,2},{2,3},{3,0},{4,5},{5,6},{6,7},{7,4},{8,9},{9,10},{10,1... | collective-permute-start | bytes 225800 | tf_op jit(solution)/shard_map/ppermute | solution.py:19
  126.9 5.7 %collective-permute-start.17 = (bf16[3,7,7,2,128]{4,3,2,1,0:T(2,128)(2,1)S(1)}, bf16[3,7,7,2,128]{4,3,2,1,0:T(2,128)(2,1)S(1)}, u32[]{:S(2)}, u32[]{:S(2)}) collective-permute-start(bf16[3,7,7,2,128]{4,3,2,1,0:T(2,128)(2,1)S(1)} %get-tuple-element.58), channel_id=1, source_target_pairs={{1,0},{2,1},{3,2},{0,3},{5,4},{6,5},{7,6},{4,7},{9,8},{10,9},{11,1... | collective-permute-start | bytes 225800 | tf_op jit(solution)/shard_map/ppermute | solution.py:20
  (10 other events, 31.7 us)
where the time goes:
time: 135 us; the launch traced here: 133 us
  local copies, waits for them, and re-layouts  50.4 us (37%)
  other arithmetic  39.5 us (29%)
  starting transfers between devices  26.3 us (19%)
  waiting for transfers between devices  11.3 us (8%)
  matrix products  4.74 us (4%)
    scatter-add x1, other arithmetic, shards(): sender_force.at[:, senders_all.reshape(-1)].add(-gradients.reshape(3, -1))  23.4 us
    gather x1, local copies, waits for them, and re-layouts, shards(): sender_kinds = ghost_kinds.reshape(-1)[senders_all]  23 us
    ppermute x9, starting transfers between devices, padded(): after = lax.ppermute(leading, axis, down)  21.6 us
    gather x2, local copies, waits for them, and re-layouts, shards(): ghost_pos_flat[:, senders_all]  16.4 us
    ppermute x9, waiting for transfers between devices, padded(): before = lax.ppermute(last, axis, up)  6.63 us
    ppermute x9, waiting for transfers between devices, padded(): after = lax.ppermute(leading, axis, down)  4.71 us
    ppermute x9, starting transfers between devices, padded(): before = lax.ppermute(last, axis, up)  4.62 us
    unnamed x45, local copies, waits for them, and re-layouts  4.01 us
  transfers between devices with their start and end apart: 18, of which 9 were waited for; matrix products, arithmetic and copies ran while one was open for 24% of the time, Pallas kernels for 0%

commit v1 on v0

v1 whole, which is shorter than its diff:
```python
import jax
import jax.numpy as jnp
from jax import lax
from jax.experimental import pallas as pl
from jax.experimental.pallas import tpu as pltpu
from jax.sharding import PartitionSpec as P

MASSES = (1.008, 12.011, 14.007, 15.999, 32.06, 22.99, 35.45, 39.098, 24.305, 40.078)
SQRT3 = 1.7320508075688772
HALF_SQRT3 = 0.8660254037844386
TIME_STEP = 0.5

K = 16
CAP = 128
R = 2
W = R * CAP
CH = 64
NB = 8
GROUP = 4
F32 = jnp.float32
BF16 = jnp.bfloat16


def swap(array, axis, odd):
    n = lax.axis_size(axis)
    if odd:
        pairs = [(i, (i + 1) % n if i % 2 else (i - 1) % n) for i in range(n)]
    else:
        pairs = [(i, i ^ 1) for i in range(n)]
    return lax.ppermute(array, axis, pairs)


def both(even, to_upper, to_lower, axis):
    if to_upper is to_lower:
        got_a = swap(to_upper, axis, False)
        got_b = swap(to_upper, axis, True)
    else:
        got_a = swap(jnp.where(even, to_upper, to_lower), axis, False)
        got_b = swap(jnp.where(even, to_lower, to_upper), axis, True)
    return jnp.where(even, got_b, got_a), jnp.where(even, got_a, got_b)


def species_mass(species):
    table = [m / 16.0 for m in MASSES]
    mass = jnp.zeros(species.shape, F32)
    for number, value in enumerate(table):
        mass = jnp.where(species == number, jnp.float32(jnp.float32(MASSES[number]) / jnp.float32(16.0)), mass)
    return mass


def rows8(row, width):
    return jnp.broadcast_to(row, (8, width))


def wide(ref, row, height):
    parts = [jnp.broadcast_to(ref[r, pl.ds(row, 1), :], (height, CAP)) for r in range(R)]
    return jnp.concatenate(parts, axis=1)


def core_kernel(
    count_ref, pos_ref, codes_ref, emb_ref, w1_ref, w2_ref, wn_ref, we_ref,
    ghost_ref, own_ref,
    wc_s, w2t_s, wnt_s, embt_s,
    d_s, kd_s, off_s, slot_s, ey_s, exu_s, ds_s, feat_s, q_s, m_s, gr_s, t_s, ts_s, g_s, a_s, s_s,
):
    wc_s[...] = jnp.zeros(wc_s.shape, BF16)
    wc_s[0:CH, 0:NB] = w1_ref[...].astype(F32).T.astype(BF16)
    embt = emb_ref[...].astype(F32).T.astype(BF16)
    wc_s[CH:, NB:NB + 16] = embt
    embt_s[...] = embt
    w2t_s[...] = w2_ref[...].astype(F32).T.astype(BF16)
    wnt_s[...] = wn_ref[...].astype(F32).T.astype(BF16)

    for r in range(R):
        code = codes_ref[pl.ds(r, K, stride=R), :]
        off_s[r] = code // CAP
        slot_s[r] = code % CAP
    zero8 = jnp.zeros((8, CAP), F32)

    def gather_column(col, acc):
        acc = list(acc)
        for r in range(R):
            for h in range(2):
                off = off_s[r, h * 8:(h + 1) * 8, :]
                slot = slot_s[r, h * 8:(h + 1) * 8, :]
                for dz in range(3):
                    hit = off == col * 3 + dz
                    for q in range(4):
                        row = pos_ref[pl.ds(col * 16 + (dz + r) * 4 + q, 1), :]
                        got = jnp.take_along_axis(rows8(row, CAP), slot, axis=1, mode="promise_in_bounds")
                        at = (r * 2 + h) * 4 + q
                        acc[at] = jnp.where(hit, got, acc[at])
        return tuple(acc)

    acc = lax.fori_loop(0, 9, gather_column, (zero8,) * 16)
    for r in range(R):
        own = [pos_ref[64 + (1 + r) * 4 + c:64 + (1 + r) * 4 + c + 1, :] for c in range(3)]
        for h in range(2):
            off = off_s[r, h * 8:(h + 1) * 8, :]
            shift = (off // 9 - 1, off // 3 % 3 - 1, off % 3 - 1)
            for c in range(3):
                value = shift[c].astype(F32) + acc[(r * 2 + h) * 4 + c] - rows8(own[c], CAP)
                d_s[r, c * K + h * 8:c * K + h * 8 + 8, :] = value
            kd_s[r, h * 8:h * 8 + 8, :] = acc[(r * 2 + h) * 4 + 3]

    centre = lax.broadcasted_iota(jnp.int32, (8, W), 0).astype(F32) / (NB - 1)
    kinds16 = lax.broadcasted_iota(jnp.int32, (16, W), 0).astype(F32)

    def radial_group(group, _):
        inputs = []
        for j in range(GROUP):
            k = group * GROUP + j
            x = wide(d_s, k, 8)
            y = wide(d_s, K + k, 8)
            z = wide(d_s, 2 * K + k, 8)
            xx, yy, zz = x * x, y * y, z * z
            s = xx + yy + zz
            m1 = jnp.maximum(1.0 - s, 0.0)
            env = m1 * m1 * m1
            u = s - centre
            ex = jnp.exp(-float((NB - 1) ** 2) * (u * u))
            at = pl.multiple_of(k * 8, 8)
            exu_s[pl.ds(at, 8), :] = ex * (u * (-2.0 * float((NB - 1) ** 2)))
            ex3 = env * SQRT3
            terms = (
                env, env * x, env * y, env * z, ex3 * (x * y), ex3 * (y * z), ex3 * (z * x),
                (env * HALF_SQRT3) * (xx - yy), (env * 0.5) * (2.0 * zz - xx - yy),
            )
            for m in range(9):
                ey_s[m, pl.ds(at, 8), :] = terms[m]
            kind = wide(kd_s, k, 16)
            onehot = jnp.where(kind == kinds16, 1.0, 0.0)
            inputs.append(jnp.concatenate([ex, onehot], axis=0))
        rhs = jnp.concatenate(inputs, axis=1).astype(BF16)
        lanes = pl.ds(pl.multiple_of(group * (GROUP * W), GROUP * W), GROUP * W)
        first = jnp.dot(wc_s[...], rhs, preferred_element_type=F32)
        pre = first[:CH]
        feat = first[CH:]
        sig = 0.5 * jnp.tanh(0.5 * pre) + 0.5
        hidden = (pre * sig).astype(BF16)
        ds_s[:, lanes] = sig * (1.0 + pre * (1.0 - sig))
        feat_s[:, lanes] = feat
        radial = jnp.dot(w2t_s[...], hidden, preferred_element_type=F32)
        for deg in range(3):
            q_s[deg * CH:(deg + 1) * CH, lanes] = radial[deg * CH:(deg + 1) * CH] * feat
        return 0

    lax.fori_loop(0, K // GROUP, radial_group, 0)

    def message_block(cb, _):
        base = pl.multiple_of(cb * 16, 16)
        for r in range(R):
            sums = [None] * 9
            for k in range(K):
                lo = k * W + r * CAP
                q = [q_s[pl.ds(deg * CH + base, 16), lo:lo + CAP] for deg in range(3)]
                for m in range(9):
                    weight = ey_s[m, k * 8:(k + 1) * 8, r * CAP:(r + 1) * CAP]
                    weight = jnp.concatenate([weight, weight], axis=0)
                    term = q[0 if m == 0 else 1 if m < 4 else 2] * weight
                    sums[m] = term if sums[m] is None else sums[m] + term
            for m in range(9):
                m_s[m, pl.ds(base, 16), r * CAP:(r + 1) * CAP] = sums[m]
        return 0

    lax.fori_loop(0, CH // 16, message_block, 0)

    own_kind = jnp.concatenate(
        [jnp.broadcast_to(pos_ref[64 + (1 + r) * 4 + 3:64 + (1 + r) * 4 + 4, :], (16, CAP)) for r in range(R)], axis=1
    )
    own_feat = jnp.dot(
        embt_s[...], jnp.where(own_kind == kinds16, 1.0, 0.0).astype(BF16), preferred_element_type=F32
    )
    slot_number = lax.broadcasted_iota(jnp.int32, (1, CAP), 1)
    occupied = jnp.concatenate(
        [jnp.where(slot_number < count_ref[r], 1.0, 0.0) for r in range(R)], axis=1
    )
    vec = m_s[1] * m_s[1] + m_s[2] * m_s[2] + m_s[3] * m_s[3]
    ten = m_s[4] * m_s[4] + m_s[5] * m_s[5] + m_s[6] * m_s[6] + m_s[7] * m_s[7] + m_s[8] * m_s[8]
    invariant = jnp.concatenate([m_s[0], vec, ten, own_feat], axis=0).astype(BF16)
    pre = jnp.dot(wnt_s[...], invariant, preferred_element_type=F32)
    sig = 0.5 * jnp.tanh(0.5 * pre) + 0.5
    we = jnp.concatenate([we_ref[...]] * R, axis=1)
    energy = jnp.sum(we * (pre * sig), axis=0, keepdims=True) * occupied
    gpre = we * occupied * (sig * (1.0 + pre * (1.0 - sig)))
    ginv = jnp.dot(wn_ref[0:3 * CH, :], gpre.astype(BF16), preferred_element_type=F32).astype(BF16).astype(F32)
    m_s[0] = ginv[:CH]
    gvec = 2.0 * ginv[CH:2 * CH]
    gten = 2.0 * ginv[2 * CH:]
    for m in range(1, 9):
        m_s[m] = m_s[m] * (gvec if m < 4 else gten)

    def carried_back(k, _):
        at = pl.multiple_of(k * 8, 8)
        for r in range(R):
            cols = slice(r * CAP, (r + 1) * CAP)
            lanes = pl.ds(pl.multiple_of(k * W + r * CAP, CAP), CAP)
            weight = []
            for m in range(9):
                w8 = ey_s[m, pl.ds(at, 8), cols]
                weight.append(jnp.concatenate([w8, w8], axis=0))
            sums = [None] * 9
            for cb in range(CH // 16):
                feat = feat_s[cb * 16:(cb + 1) * 16, lanes]
                q = [q_s[deg * CH + cb * 16:deg * CH + (cb + 1) * 16, lanes] for deg in range(3)]
                back = [None] * 3
                for m in range(9):
                    deg = 0 if m == 0 else 1 if m < 4 else 2
                    cot = m_s[m, cb * 16:(cb + 1) * 16, cols]
                    term = cot * q[deg]
                    sums[m] = term if sums[m] is None else sums[m] + term
                    term = cot * weight[m]
                    back[deg] = term if back[deg] is None else back[deg] + term
                for deg in range(3):
                    gr_s[deg * CH + cb * 16:deg * CH + (cb + 1) * 16, lanes] = (back[deg] * feat).astype(BF16)
            for m in range(9):
                t_s[r, m, pl.ds(at, 8), :] = sums[m][:8] + sums[m][8:]
        return 0

    lax.fori_loop(0, K, carried_back, 0)

    def radial_back(group, _):
        lanes = pl.ds(pl.multiple_of(group * (GROUP * W), GROUP * W), GROUP * W)
        ghid = jnp.dot(w2_ref[...], gr_s[:, lanes], preferred_element_type=F32)
        gpre = (ghid.astype(BF16).astype(F32) * ds_s[:, lanes]).astype(BF16)
        gbas = jnp.dot(w1_ref[...], gpre, preferred_element_type=F32).astype(BF16).astype(F32)
        for j in range(GROUP):
            at = pl.multiple_of((group * GROUP + j) * 8, 8)
            for r in range(R):
                lo = j * W + r * CAP
                ts_s[r, pl.ds(at, 8), :] = gbas[:, lo:lo + CAP] * exu_s[pl.ds(at, 8), r * CAP:(r + 1) * CAP]
        return 0

    lax.fori_loop(0, K // GROUP, radial_back, 0)

    def total(ref):
        out = ref[pl.ds(0, K, stride=8), :]
        for sub in range(1, 8):
            out = out + ref[pl.ds(sub, K, stride=8), :]
        return out

    for r in range(R):
        cols = slice(r * CAP, (r + 1) * CAP)
        x, y, z = d_s[r, 0:K, :], d_s[r, K:2 * K, :], d_s[r, 2 * K:3 * K, :]
        xx, yy, zz = x * x, y * y, z * z
        s = xx + yy + zz
        m1 = jnp.maximum(1.0 - s, 0.0)
        env = m1 * m1 * m1
        t = [total(t_s.at[r, m]) for m in range(9)]
        harm = (
            None, x, y, z, SQRT3 * (x * y), SQRT3 * (y * z), SQRT3 * (z * x),
            HALF_SQRT3 * (xx - yy), 0.5 * (2.0 * zz - xx - yy),
        )
        genv = t[0]
        for m in range(1, 9):
            genv = genv + harm[m] * t[m]
        gs2 = 2.0 * (total(ts_s.at[r]) - 3.0 * (m1 * m1) * genv)
        e = [env * v for v in t]
        gx = e[1] + SQRT3 * (y * e[4] + z * e[6]) + x * (SQRT3 * e[7] - e[8] + gs2)
        gy = e[2] + SQRT3 * (x * e[4] + z * e[5]) + y * (gs2 - SQRT3 * e[7] - e[8])
        gz = e[3] + SQRT3 * (y * e[5] + x * e[6]) + z * (2.0 * e[8] + gs2)
        for c, g in enumerate((gx, gy, gz)):
            g_s[r, c * K:(c + 1) * K, :] = g
            own_ref[r * 4 + c:r * 4 + c + 1, :] = jnp.sum(g, axis=0, keepdims=True)
        own_ref[r * 4 + 3:r * 4 + 4, :] = energy[:, cols]

    sub = lax.broadcasted_iota(jnp.int32, (8, CAP), 0)
    comp = sub % 4
    row_cell = lax.broadcasted_iota(jnp.int32, (144, CAP), 0) // 4
    slots = lax.broadcasted_iota(jnp.int32, (CAP, CAP), 0)

    def scatter_inputs(k, _):
        for r in range(R):
            cols = slice(r * CAP, (r + 1) * CAP)
            lanes = pl.ds(pl.multiple_of(k * W + r * CAP, CAP), CAP)
            off = off_s[r, pl.ds(k, 1), :]
            cell = off // 3 * 4 + off % 3 + r
            slot = slot_s[r, pl.ds(k, 1), :]
            gx, gy, gz = (rows8(g_s[r, pl.ds(c * K + k, 1), :], CAP) for c in range(3))
            mixed = jnp.where(comp == 0, gx, jnp.where(comp == 1, gy, jnp.where(comp == 2, gz, 0.0)))
            mixed = jnp.concatenate([-mixed] * 18, axis=0)
            hit = jnp.broadcast_to(cell, (144, CAP)) == row_cell
            a_s[:, lanes] = jnp.where(hit, mixed, 0.0).astype(BF16)
            s_s[:, lanes] = jnp.where(jnp.broadcast_to(slot, (CAP, CAP)) == slots, 1.0, 0.0).astype(BF16)
        return 0

    lax.fori_loop(0, K, scatter_inputs, 0)
    ghost_ref[...] = lax.dot_general(
        a_s[...], s_s[...], (((1,), (1,)), ((), ())), preferred_element_type=F32
    )


def core(count, pos, codes, embed16, w1, w2, wn, we):
    vmem = pl.BlockSpec(memory_space=pltpu.VMEM)
    scratch = [
        pltpu.VMEM((2 * CH, NB + 16), BF16),
        pltpu.VMEM((3 * CH, CH), BF16),
        pltpu.VMEM((CH, 4 * CH), BF16),
        pltpu.VMEM((CH, 16), BF16),
        pltpu.VMEM((R, 3 * K, CAP), F32),
        pltpu.VMEM((R, K, CAP), F32),
        pltpu.VMEM((R, K, CAP), jnp.int32),
        pltpu.VMEM((R, K, CAP), jnp.int32),
        pltpu.VMEM((9, 8 * K, W), F32),
        pltpu.VMEM((8 * K, W), F32),
        pltpu.VMEM((CH, K * W), F32),
        pltpu.VMEM((CH, K * W), F32),
        pltpu.VMEM((3 * CH, K * W), F32),
        pltpu.VMEM((9, CH, W), F32),
        pltpu.VMEM((3 * CH, K * W), BF16),
        pltpu.VMEM((R, 9, 8 * K, CAP), F32),
        pltpu.VMEM((R, 8 * K, CAP), F32),
        pltpu.VMEM((R, 3 * K, CAP), F32),
        pltpu.VMEM((144, K * W), BF16),
        pltpu.VMEM((CAP, K * W), BF16),
    ]
    return pl.pallas_call(
        core_kernel,
        in_specs=[pl.BlockSpec(memory_space=pltpu.SMEM)] + [vmem] * 7,
        out_specs=[vmem, vmem],
        out_shape=[jax.ShapeDtypeStruct((144, CAP), F32), jax.ShapeDtypeStruct((8, CAP), F32)],
        scratch_shapes=scratch,
        name="edges",
    )(count, pos, codes, embed16, w1, w2, wn, we)


def shards(
    frac, velocity, force_old, species, cell_count, neighbours, embed, w_radial_in, w_radial_out, w_node, w_energy
):
    even_x = lax.axis_index("gx") % 2 == 0
    even_y = lax.axis_index("gy") % 2 == 0
    even_z = lax.axis_index("gz") % 2 == 0
    occupied = (lax.broadcasted_iota(jnp.int32, species.shape, 3) < cell_count[..., None]).astype(F32)
    atom_mass = species_mass(species)
    half_velocity = velocity + 0.5 * TIME_STEP * force_old / atom_mass
    moved = frac + TIME_STEP * half_velocity
    mine = jnp.concatenate([moved, species.astype(F32)[None]], axis=0).reshape(4, R, CAP)
    mine = mine.transpose(1, 0, 2)

    low, high = both(even_z, mine[1], mine[0], "gz")
    column = jnp.concatenate([low, mine.reshape(4 * R, CAP), high], axis=0)
    low, high = both(even_y, column, column, "gy")
    plane = jnp.stack([low, column, high])
    low, high = both(even_x, plane, plane, "gx")
    pos = jnp.stack([low, plane, high]).reshape(144, CAP)

    ghost, own = core(
        cell_count.reshape(R),
        pos,
        neighbours.reshape(K * R, CAP),
        jnp.pad(embed, ((0, 16 - embed.shape[0]), (0, 0))),
        w_radial_in,
        w_radial_out,
        w_node,
        jnp.broadcast_to(w_energy[:, None], (CH, CAP)),
    )
    ghost = ghost.reshape(3, 3, 16, CAP)
    low, high = both(even_x, ghost[2], ghost[0], "gx")
    plane = ghost[1] + low + high
    low, high = both(even_y, plane[2], plane[0], "gy")
    column = (plane[1] + low + high).reshape(4, 4, CAP)
    low, high = both(even_z, column[3], column[0], "gz")
    own = own.reshape(R, 4, CAP)
    force = column[1:3] + own
    force = force + jnp.stack([low, high])
    force = force[:, :3].transpose(1, 0, 2).reshape(frac.shape)

    next_force = occupied * force
    next_velocity = occupied * (half_velocity + 0.5 * TIME_STEP * next_force / atom_mass)
    next_frac = occupied * moved
    site_energy = own[:, 3].reshape(species.shape)
    return (next_frac, next_velocity, next_force, site_energy)


def solution(mesh):
    cells = P(None, "gx", "gy", "gz", None)
    in_specs = (
        cells, cells, cells, P("gx", "gy", "gz", None), P("gx", "gy", "gz"), cells, P(), P(), P(), P(), P(),
    )
    out_specs = (cells, cells, cells, P("gx", "gy", "gz", None))
    return jax.shard_map(shards, mesh=mesh, in_specs=in_specs, out_specs=out_specs, check_vma=False)
```

time: 135 us -> 52.4 us (0.39)
  local copies, waits for them, and re-layouts: 50.4 us -> 6.37 us
  other arithmetic: 39.5 us -> 1.63 us
  Pallas kernels: 0 us -> 10.8 us
  starting transfers between devices: 26.3 us -> 15.9 us
  waiting for transfers between devices: 11.3 us -> 16.6 us
  matrix products: 4.74 us -> 0 us
    gather x3 -> x0, local copies, waits for them, and re-layouts: 39.4 us -> none  [the longest x1 23 us: shards(): sender_kinds = ghost_kinds.reshape(-1)[senders_all]]
    scatter-add x1 -> x0, other arithmetic: 23.4 us -> none  [shards(): sender_force.at[:, senders_all.reshape(-1)].add(-gradients.reshape(3, -1))]
    pallas_call x0 -> x1, Pallas kernels: none -> 10.8 us  [core(): pl.pallas_call(core_kernel, in_specs=[pl.BlockSpec(memory_space=pltpu.SME...]
    ppermute x18 -> x12, starting transfers between devices: 26.3 us -> 15.9 us  [swap(): return lax.ppermute(array, axis, pairs)]
    reduce_sum x10 -> x0, other arithmetic: 6.21 us -> none  [the longest x2 2.17 us: site_terms(): tensor_part = jnp.sum(carried[2][None] * second_order[:, None], axis=2)]
    ppermute x18 -> x12, waiting for transfers between devices: 11.3 us -> 16.6 us  [swap(): return lax.ppermute(array, axis, pairs)]
    dot_general x7 -> x0, matrix products: 4.74 us -> none  [the longest x2 1.85 us: embed_species(): jnp.dot(embed.T, onehot, preferred_element_type=jnp.float32)]
    convert_element_type x4 -> x2, other arithmetic: 2.67 us -> 0.07 us  [the longest x1 0.07 us: shards(): (lax.broadcasted_iota(jnp.int32, species.shape, 3) < cell_count[..., None...]
  transfers between devices with their start and end apart: 18 -> 12, of which waited for: 9 -> 9; matrix products, arithmetic and copies ran while one was open for 24% -> 5% of each run, Pallas kernels for 0% -> 0%
where the time goes in v1:
time: 52.4 us; the launch traced here: 52.1 us
  waiting for transfers between devices  16.6 us (32%)
  starting transfers between devices  15.9 us (30%)
  Pallas kernels  10.8 us (21%)
  local copies, waits for them, and re-layouts  6.37 us (12%)
  other arithmetic  1.63 us (3%)
  between operations  0.79 us (2%)
    ppermute x12, waiting for transfers between devices, swap(): return lax.ppermute(array, axis, pairs)  16.6 us
    ppermute x12, starting transfers between devices, swap(): return lax.ppermute(array, axis, pairs)  15.9 us
    pallas_call x1, Pallas kernels, core(): pl.pallas_call(core_kernel, in_specs=[pl.BlockSpec(memory_space=pltpu.SME...  10.8 us
    unnamed x22, local copies, waits for them, and re-layouts  4.53 us
  transfers between devices with their start and end apart: 12, of which 9 were waited for; matrix products, arithmetic and copies ran while one was open for 5% of the time, Pallas kernels for 0%

profile of v1, /device:TPU:6, one launch (start us, length us, event | category | flops | bytes accessed | tf_op | source)
XLA Modules:
  0.0 52.1 jit_solution(7929900640100410615)
XLA Ops:
  0.6 0.7 %copy-done.5 = s32[1,1,2,128]{3,2,1,0:T(2,128)S(1)} copy-done((s32[1,1,2,128]{3,2,1,0:T(2,128)S(1)}, s32[1,1,2,128]{3,2,1,0:T(2,128)}, u32[]{:S(2)}) %copy-start.5) | copy-done | bytes 1048
  1.4 0.6 %copy-done.8 = s32[1,1,2]{2,1,0:T(1,128)S(1)} copy-done((s32[1,1,2]{2,1,0:T(1,128)S(1)}, s32[1,1,2]{2,1,0:T(1,128)}, u32[]{:S(2)}) %copy-start.8) | copy-done | bytes 32
  2.1 2.3 %collective-permute-start = (f32[4,128]{1,0:T(4,128)S(1)}, f32[4,128]{1,0:T(4,128)S(1)}, u32[]{:S(2)}, u32[]{:S(2)}) collective-permute-start(f32[4,128]{1,0:T(4,128)S(1)} %get-tuple-element.37), channel_id=1, source_target_pairs={{0,3},{1,2},{2,1},{3,0},{4,7},{5,6},{6,5},{7,4},{8,11},{9,10},{10,... | collective-permute-start | bytes 6152 | tf_op jit(solution)/shard_map/ppermute | solution.py:30
  4.5 2.6 %collective-permute-done = f32[4,128]{1,0:T(4,128)S(1)} collective-permute-done((f32[4,128]{1,0:T(4,128)S(1)}, f32[4,128]{1,0:T(4,128)S(1)}, u32[]{:S(2)}, u32[]{:S(2)}) %collective-permute-start) | collective-permute-done | bytes 2080 | tf_op jit(solution)/shard_map/ppermute | solution.py:30
  7.0 1.0 %collective-permute-done.1 = f32[4,128]{1,0:T(4,128)S(1)} collective-permute-done((f32[4,128]{1,0:T(4,128)S(1)}, f32[4,128]{1,0:T(4,128)S(1)}, u32[]{:S(2)}, u32[]{:S(2)}) %collective-permute-start.1) | collective-permute-done | bytes 2080 | tf_op jit(solution)/shard_map/ppermute | solution.py:30
  8.2 5.0 %collective-permute-start.2 = (f32[16,128]{1,0:T(8,128)S(1)}, f32[16,128]{1,0:T(8,128)S(1)}, u32[]{:S(2)}, u32[]{:S(2)}) collective-permute-start(f32[16,128]{1,0:T(8,128)S(1)} %get-tuple-element.32), channel_id=1, source_target_pairs={{0,60},{4,8},{8,4},{12,16},{16,12},{20,24},{24,20},{28,32},{32,28}... | collective-permute-start | bytes 24584 | tf_op jit(solution)/shard_map/ppermute | solution.py:30
  13.1 1.4 %collective-permute-done.2 = f32[16,128]{1,0:T(8,128)S(1)} collective-permute-done((f32[16,128]{1,0:T(8,128)S(1)}, f32[16,128]{1,0:T(8,128)S(1)}, u32[]{:S(2)}, u32[]{:S(2)}) %collective-permute-start.2) | collective-permute-done | bytes 8224 | tf_op jit(solution)/shard_map/ppermute | solution.py:30
  14.5 1.7 %collective-permute-start.5 = (f32[3,16,128]{2,1,0:T(8,128)S(1)}, f32[3,16,128]{2,1,0:T(8,128)S(1)}, u32[]{:S(2)}, u32[]{:S(2)}) collective-permute-start(f32[3,16,128]{2,1,0:T(8,128)S(1)} %get-tuple-element.26), channel_id=1, source_target_pairs={{0,64},{64,0},{128,192},{192,128},{1,65},{65,1},{129,193},{193,129... | collective-permute-start | bytes 73736 | tf_op jit(solution)/shard_map/ppermute | solution.py:30
  16.2 2.2 %collective-permute-start.4 = (f32[3,16,128]{2,1,0:T(8,128)S(1)}, f32[3,16,128]{2,1,0:T(8,128)S(1)}, u32[]{:S(2)}, u32[]{:S(2)}) collective-permute-start(f32[3,16,128]{2,1,0:T(8,128)S(1)} %get-tuple-element.26), channel_id=1, source_target_pairs={{0,192},{64,128},{128,64},{192,0},{1,193},{65,129},{129,65},{193,1... | collective-permute-start | bytes 73736 | tf_op jit(solution)/shard_map/ppermute | solution.py:30
  18.3 0.7 %copy.30.wn_ref = bf16[256,64]{1,0:T(8,128)(2,1)} copy(bf16[256,64]{0,1:T(8,128)(2,1)S(1)} %copy-done) | data formatting | bytes 65536 | tf_op args[9]
  19.1 0.6 %pad.4.emb_ref = bf16[16,64]{1,0:T(8,128)(2,1)} pad(bf16[10,64]{1,0:T(8,128)(2,1)S(1)} %copy-done.4, bf16[]{:T(256)} %constant.79.clone.1), padding=0_6x0_0 | pad | bytes 3330 | tf_op jit(solution)/shard_map/jit(_pad)/pad | solution.py:351
  19.7 1.5 %collective-permute-done.4 = f32[3,16,128]{2,1,0:T(8,128)S(1)} collective-permute-done((f32[3,16,128]{2,1,0:T(8,128)S(1)}, f32[3,16,128]{2,1,0:T(8,128)S(1)}, u32[]{:S(2)}, u32[]{:S(2)}) %collective-permute-start.4) | collective-permute-done | bytes 24608 | tf_op jit(solution)/shard_map/ppermute | solution.py:30
  21.2 0.6 %pad_maximum_fusion = f32[3,3,16,128]{3,2,1,0:T(8,128)} fusion(f32[1,3,16,128]{3,2,1,0:T(8,128)S(1)} %get-tuple-element.22, f32[1,3,16,128]{3,2,1,0:T(8,128)S(1)} %get-tuple-element.25, f32[1,3,16,128]{3,2,1,0:T(8,128)S(1)} %get-tuple-element.21), kind=kLoop, calls=%fused_computation | loop fusion | flops 36864 | bytes 147456 | tf_op jit(solution)/shard_map/stack | solution.py:345
  21.8 0.7 %copy-done.7 = f32[64]{0:T(128)S(1)} copy-done((f32[64]{0:T(128)S(1)}, f32[64]{0:T(128)}, u32[]{:S(2)}) %copy-start.7) | copy-done | bytes 280
  22.5 0.7 %broadcast_in_dim.61.we_ref = f32[64,128]{1,0:T(8,128)} broadcast(f32[64]{0:T(128)S(1)} %copy-done.7), dimensions={0} | broadcast | bytes 33024 | tf_op jit(solution)/shard_map/broadcast_in_dim | solution.py:355
  23.2 10.8 %edges.1 = (f32[144,128]{1,0:T(8,128)}, f32[8,128]{1,0:T(8,128)}) custom-call(s32[2]{0:T(128)} %bitcast.75, f32[144,128]{1,0:T(8,128)} %bitcast.61, s32[32,128]{1,0:T(8,128)} %bitcast.70, bf16[16,64]{1,0:T(8,128)(2,1)} %pad.4.emb_ref, bf16[8,64]{1,0:T(8,128)(2,1)} %w1_ref.1, bf16[64,192]{1,0:T(8,128)(2,1)} %w2_ref.1, bf16[256,64]{1,0:T(8,128)(2,1)} %copy.30.wn_ref, ...), custom_call_target="tpu_custom_call" | custom-call | tf_op jit(solution)/shard_map/edges/pallas_call | solution.py:317
  34.0 0.8 %fusion.10 = (f32[48,128]{1,0:T(8,128)S(1)}, f32[48,128]{1,0:T(8,128)S(1)}, f32[48,128]{1,0:T(8,128)S(1)}) fusion(f32[144,128]{1,0:T(8,128)} %get-tuple-element.6, pred[]{:T(512)S(6)} %eq.93), kind=kLoop, calls=%fused_computation.51 | loop fusion | flops 12288 | bytes 147457 | tf_op jit(solution)/shard_map/slice | solution.py:359
  34.8 2.2 %collective-permute-start.6 = (f32[3,16,128]{2,1,0:T(8,128)S(1)}, f32[3,16,128]{2,1,0:T(8,128)S(1)}, u32[]{:S(2)}, u32[]{:S(2)}) collective-permute-start(f32[3,16,128]{2,1,0:T(8,128)S(1)} %bitcast.66), channel_id=1, source_target_pairs={{0,192},{64,128},{128,64},{192,0},{1,193},{65,129},{129,65},{193,1... | collective-permute-start | bytes 73736 | tf_op jit(solution)/shard_map/ppermute | solution.py:30
  37.0 2.9 %collective-permute-done.6 = f32[3,16,128]{2,1,0:T(8,128)S(1)} collective-permute-done((f32[3,16,128]{2,1,0:T(8,128)S(1)}, f32[3,16,128]{2,1,0:T(8,128)S(1)}, u32[]{:S(2)}, u32[]{:S(2)}) %collective-permute-start.6) | collective-permute-done | bytes 24608 | tf_op jit(solution)/shard_map/ppermute | solution.py:30
  39.8 1.0 %collective-permute-done.7 = f32[3,16,128]{2,1,0:T(8,128)S(1)} collective-permute-done((f32[3,16,128]{2,1,0:T(8,128)S(1)}, f32[3,16,128]{2,1,0:T(8,128)S(1)}, u32[]{:S(2)}, u32[]{:S(2)}) %collective-permute-start.7) | collective-permute-done | bytes 24608 | tf_op jit(solution)/shard_map/ppermute | solution.py:30
  41.2 3.9 %collective-permute-done.8 = f32[16,128]{1,0:T(8,128)S(1)} collective-permute-done((f32[16,128]{1,0:T(8,128)S(1)}, f32[16,128]{1,0:T(8,128)S(1)}, u32[]{:S(2)}, u32[]{:S(2)}) %collective-permute-start.8) | collective-permute-done | bytes 8224 | tf_op jit(solution)/shard_map/ppermute | solution.py:30
  45.2 2.1 %collective-permute-start.10 = (f32[4,128]{1,0:T(4,128)S(1)}, f32[4,128]{1,0:T(4,128)S(1)}, u32[]{:S(2)}, u32[]{:S(2)}) collective-permute-start(f32[4,128]{1,0:T(4,128)S(1)} %get-tuple-element.29), channel_id=1, source_target_pairs={{0,3},{1,2},{2,1},{3,0},{4,7},{5,6},{6,5},{7,4},{8,11},{9,10},{10,... | collective-permute-start | bytes 6152 | tf_op jit(solution)/shard_map/ppermute | solution.py:30
  48.6 1.5 %collective-permute-done.10 = f32[4,128]{1,0:T(4,128)S(1)} collective-permute-done((f32[4,128]{1,0:T(4,128)S(1)}, f32[4,128]{1,0:T(4,128)S(1)}, u32[]{:S(2)}, u32[]{:S(2)}) %collective-permute-start.10) | collective-permute-done | bytes 2080 | tf_op jit(solution)/shard_map/ppermute | solution.py:30
  50.1 0.8 %collective-permute-done.11 = f32[4,128]{1,0:T(4,128)S(1)} collective-permute-done((f32[4,128]{1,0:T(4,128)S(1)}, f32[4,128]{1,0:T(4,128)S(1)}, u32[]{:S(2)}, u32[]{:S(2)}) %collective-permute-start.11) | collective-permute-done | bytes 2080 | tf_op jit(solution)/shard_map/ppermute | solution.py:30
  (48 shorter events, 3.2 us)
Async XLA Ops:
  0.6 0.7 %copy-start.5 = (s32[1,1,2,128]{3,2,1,0:T(2,128)S(1)}, s32[1,1,2,128]{3,2,1,0:T(2,128)}, u32[]{:S(2)}) copy-start(s32[1,1,2,128]{3,2,1,0:T(2,128)} %param.14) | copy-start | bytes 3076
  1.3 0.7 %copy-start.6 = (f32[3,1,1,2,128]{4,3,2,1,0:T(2,128)S(1)}, f32[3,1,1,2,128]{4,3,2,1,0:T(2,128)}, u32[]{:S(2)}) copy-start(f32[3,1,1,2,128]{4,3,2,1,0:T(2,128)} %param.11) | copy-start | bytes 9220
  1.4 0.7 %copy-start.8 = (s32[1,1,2]{2,1,0:T(1,128)S(1)}, s32[1,1,2]{2,1,0:T(1,128)}, u32[]{:S(2)}) copy-start(s32[1,1,2]{2,1,0:T(1,128)} %param.15) | copy-start | bytes 28
  1.4 0.7 %copy-start.3 = (f32[3,1,1,2,128]{4,3,2,1,0:T(2,128)S(1)}, f32[3,1,1,2,128]{4,3,2,1,0:T(2,128)}, u32[]{:S(2)}) copy-start(f32[3,1,1,2,128]{4,3,2,1,0:T(2,128)} %param.12) | copy-start | bytes 9220
  1.4 0.7 %copy-start.2 = (f32[3,1,1,2,128]{4,3,2,1,0:T(2,128)S(1)}, f32[3,1,1,2,128]{4,3,2,1,0:T(2,128)}, u32[]{:S(2)}) copy-start(f32[3,1,1,2,128]{4,3,2,1,0:T(2,128)} %param.13) | copy-start | bytes 9220
  2.1 4.9 %collective-permute-start = (f32[4,128]{1,0:T(4,128)S(1)}, f32[4,128]{1,0:T(4,128)S(1)}, u32[]{:S(2)}, u32[]{:S(2)}) collective-permute-start(f32[4,128]{1,0:T(4,128)S(1)} %get-tuple-element.37), channel_id=1, source_target_pairs={{0,3},{1,2},{2,1},{3,0},{4,7},{5,6},{6,5},{7,4},{8,11},{9,10},{10,... | collective-permute-start | bytes 6152 | tf_op jit(solution)/shard_map/ppermute | solution.py:30
  4.4 3.6 %collective-permute-start.1 = (f32[4,128]{1,0:T(4,128)S(1)}, f32[4,128]{1,0:T(4,128)S(1)}, u32[]{:S(2)}, u32[]{:S(2)}) collective-permute-start(f32[4,128]{1,0:T(4,128)S(1)} %get-tuple-element.38), channel_id=1, source_target_pairs={{0,1},{1,0},{2,3},{3,2},{4,5},{5,4},{6,7},{7,6},{8,9},{9,8},{10,11... | collective-permute-start | bytes 6152 | tf_op jit(solution)/shard_map/ppermute | solution.py:30
  8.1 5.1 %collective-permute-start.3 = (f32[16,128]{1,0:T(8,128)S(1)}, f32[16,128]{1,0:T(8,128)S(1)}, u32[]{:S(2)}, u32[]{:S(2)}) collective-permute-start(f32[16,128]{1,0:T(8,128)S(1)} %get-tuple-element.32), channel_id=1, source_target_pairs={{0,4},{4,0},{8,12},{12,8},{16,20},{20,16},{24,28},{28,24},{32,36},... | collective-permute-start | bytes 24584 | tf_op jit(solution)/shard_map/ppermute | solution.py:30
  8.2 6.3 %collective-permute-start.2 = (f32[16,128]{1,0:T(8,128)S(1)}, f32[16,128]{1,0:T(8,128)S(1)}, u32[]{:S(2)}, u32[]{:S(2)}) collective-permute-start(f32[16,128]{1,0:T(8,128)S(1)} %get-tuple-element.32), channel_id=1, source_target_pairs={{0,60},{4,8},{8,4},{12,16},{16,12},{20,24},{24,20},{28,32},{32,28}... | collective-permute-start | bytes 24584 | tf_op jit(solution)/shard_map/ppermute | solution.py:30
  14.5 3.9 %copy-start = (bf16[256,64]{0,1:T(8,128)(2,1)S(1)}, bf16[256,64]{0,1:T(8,128)(2,1)}, u32[]{:S(2)}) copy-start(bf16[256,64]{0,1:T(8,128)(2,1)} %param.20) | copy-start | bytes 98308
  14.5 5.2 %collective-permute-start.5 = (f32[3,16,128]{2,1,0:T(8,128)S(1)}, f32[3,16,128]{2,1,0:T(8,128)S(1)}, u32[]{:S(2)}, u32[]{:S(2)}) collective-permute-start(f32[3,16,128]{2,1,0:T(8,128)S(1)} %get-tuple-element.26), channel_id=1, source_target_pairs={{0,64},{64,0},{128,192},{192,128},{1,65},{65,1},{129,193},{193,129... | collective-permute-start | bytes 73736 | tf_op jit(solution)/shard_map/ppermute | solution.py:30
  16.2 5.0 %collective-permute-start.4 = (f32[3,16,128]{2,1,0:T(8,128)S(1)}, f32[3,16,128]{2,1,0:T(8,128)S(1)}, u32[]{:S(2)}, u32[]{:S(2)}) collective-permute-start(f32[3,16,128]{2,1,0:T(8,128)S(1)} %get-tuple-element.26), channel_id=1, source_target_pairs={{0,192},{64,128},{128,64},{192,0},{1,193},{65,129},{129,65},{193,1... | collective-permute-start | bytes 73736 | tf_op jit(solution)/shard_map/ppermute | solution.py:30
  18.3 0.7 %copy-start.4 = (bf16[10,64]{1,0:T(8,128)(2,1)S(1)}, bf16[10,64]{1,0:T(8,128)(2,1)}, u32[]{:S(2)}) copy-start(bf16[10,64]{1,0:T(8,128)(2,1)} %param.17) | copy-start | bytes 3844
  21.8 0.7 %copy-start.7 = (f32[64]{0:T(128)S(1)}, f32[64]{0:T(128)}, u32[]{:S(2)}) copy-start(f32[64]{0:T(128)} %param.21) | copy-start | bytes 772
  34.8 5.0 %collective-permute-start.6 = (f32[3,16,128]{2,1,0:T(8,128)S(1)}, f32[3,16,128]{2,1,0:T(8,128)S(1)}, u32[]{:S(2)}, u32[]{:S(2)}) collective-permute-start(f32[3,16,128]{2,1,0:T(8,128)S(1)} %bitcast.66), channel_id=1, source_target_pairs={{0,192},{64,128},{128,64},{192,0},{1,193},{65,129},{129,65},{193,1... | collective-permute-start | bytes 73736 | tf_op jit(solution)/shard_map/ppermute | solution.py:30
  37.0 3.8 %collective-permute-start.7 = (f32[3,16,128]{2,1,0:T(8,128)S(1)}, f32[3,16,128]{2,1,0:T(8,128)S(1)}, u32[]{:S(2)}, u32[]{:S(2)}) collective-permute-start(f32[3,16,128]{2,1,0:T(8,128)S(1)} %bitcast.65), channel_id=1, source_target_pairs={{0,64},{64,0},{128,192},{192,128},{1,65},{65,1},{129,193},{193,129... | collective-permute-start | bytes 73736 | tf_op jit(solution)/shard_map/ppermute | solution.py:30
  40.8 4.4 %collective-permute-start.8 = (f32[16,128]{1,0:T(8,128)S(1)}, f32[16,128]{1,0:T(8,128)S(1)}, u32[]{:S(2)}, u32[]{:S(2)}) collective-permute-start(f32[16,128]{1,0:T(8,128)S(1)} %get-tuple-element.23), channel_id=1, source_target_pairs={{0,60},{4,8},{8,4},{12,16},{16,12},{20,24},{24,20},{28,32},{32,28}... | collective-permute-start | bytes 24584 | tf_op jit(solution)/shard_map/ppermute | solution.py:30
  41.2 3.9 %collective-permute-start.9 = (f32[16,128]{1,0:T(8,128)S(1)}, f32[16,128]{1,0:T(8,128)S(1)}, u32[]{:S(2)}, u32[]{:S(2)}) collective-permute-start(f32[16,128]{1,0:T(8,128)S(1)} %get-tuple-element.24), channel_id=1, source_target_pairs={{0,4},{4,0},{8,12},{12,8},{16,20},{20,16},{24,28},{28,24},{32,36},... | collective-permute-start | bytes 24584 | tf_op jit(solution)/shard_map/ppermute | solution.py:30
  45.2 4.9 %collective-permute-start.10 = (f32[4,128]{1,0:T(4,128)S(1)}, f32[4,128]{1,0:T(4,128)S(1)}, u32[]{:S(2)}, u32[]{:S(2)}) collective-permute-start(f32[4,128]{1,0:T(4,128)S(1)} %get-tuple-element.29), channel_id=1, source_target_pairs={{0,3},{1,2},{2,1},{3,0},{4,7},{5,6},{6,5},{7,4},{8,11},{9,10},{10,... | collective-permute-start | bytes 6152 | tf_op jit(solution)/shard_map/ppermute | solution.py:30
  47.3 3.6 %collective-permute-start.11 = (f32[4,128]{1,0:T(4,128)S(1)}, f32[4,128]{1,0:T(4,128)S(1)}, u32[]{:S(2)}, u32[]{:S(2)}) collective-permute-start(f32[4,128]{1,0:T(4,128)S(1)} %get-tuple-element.30), channel_id=1, source_target_pairs={{0,1},{1,0},{2,3},{3,2},{4,5},{5,4},{6,7},{7,6},{8,9},{9,8},{10,11... | collective-permute-start | bytes 6152 | tf_op jit(solution)/shard_map/ppermute | solution.py:30
  47.3 0.7 %copy-start.1 = (f32[8,128]{1,0:T(8,128)S(1)}, f32[8,128]{1,0:T(8,128)}, u32[]{:S(2)}) copy-start(f32[8,128]{1,0:T(8,128)} %get-tuple-element.7) | copy-start | bytes 12292

commit v2 on v1

v2 whole, which is shorter than its diff:
```python
import jax
import jax.numpy as jnp
from jax import lax
from jax.experimental import pallas as pl
from jax.experimental.pallas import tpu as pltpu
from jax.sharding import PartitionSpec as P

MASSES = (1.008, 12.011, 14.007, 15.999, 32.06, 22.99, 35.45, 39.098, 24.305, 40.078)
SQRT3 = 1.7320508075688772
HALF_SQRT3 = 0.8660254037844386
TIME_STEP = 0.5

K = 16
CAP = 128
R = 2
W = R * CAP
CH = 64
NB = 8
GROUP = 4
F32 = jnp.float32
BF16 = jnp.bfloat16


def swap(array, axis, odd):
    n = lax.axis_size(axis)
    if odd:
        pairs = [(i, (i + 1) % n if i % 2 else (i - 1) % n) for i in range(n)]
    else:
        pairs = [(i, i ^ 1) for i in range(n)]
    return lax.ppermute(array, axis, pairs)


def rows8(row, width):
    return jnp.broadcast_to(row, (8, width))


def wide(ref, row, height):
    parts = [jnp.broadcast_to(ref[r, pl.ds(row, 1), :], (height, CAP)) for r in range(R)]
    return jnp.concatenate(parts, axis=1)


def begin_kernel(frac_ref, vel_ref, force_ref, kind_ref, send_a_ref, send_b_ref, mine_ref, keep_ref):
    kind = kind_ref[...]
    mass = jnp.zeros((R, CAP), F32)
    for number, value in enumerate(MASSES):
        mass = jnp.where(kind == number, jnp.float32(value) / jnp.float32(16.0), mass)
    for c in range(3):
        half = vel_ref[c] + 0.5 * TIME_STEP * force_ref[c] / mass
        moved = frac_ref[c] + TIME_STEP * half
        for r in range(R):
            mine_ref[r * 4 + c:r * 4 + c + 1, :] = moved[r:r + 1]
            keep_ref[r * 4 + c:r * 4 + c + 1, :] = half[r:r + 1]
    for r in range(R):
        mine_ref[r * 4 + 3:r * 4 + 4, :] = kind[r:r + 1].astype(F32)
        keep_ref[r * 4 + 3:r * 4 + 4, :] = mass[r:r + 1]
    even = lax.axis_index("gz") % 2 == 0
    send_a_ref[...] = jnp.where(even, mine_ref[4:8, :], mine_ref[0:4, :])
    send_b_ref[...] = jnp.where(even, mine_ref[0:4, :], mine_ref[4:8, :])


def finish_kernel(count_ref, mid_ref, got_a_ref, got_b_ref, own_ref, mine_ref, keep_ref, frac_ref, vel_ref, force_ref, energy_ref):
    even = lax.axis_index("gz") % 2 == 0
    got = (
        jnp.where(even, got_b_ref[...], got_a_ref[...]),
        jnp.where(even, got_a_ref[...], got_b_ref[...]),
    )
    slot_number = lax.broadcasted_iota(jnp.int32, (1, CAP), 1)
    for r in range(R):
        occupied = jnp.where(slot_number < count_ref[r], 1.0, 0.0)
        total = mid_ref[4 * (r + 1):4 * (r + 2), :] + own_ref[r * 4:r * 4 + 4, :] + got[r]
        force = occupied * total
        keep = keep_ref[r * 4:r * 4 + 4, :]
        mine = mine_ref[r * 4:r * 4 + 4, :]
        speed = occupied * (keep + 0.5 * TIME_STEP * force / keep[3:4])
        place = occupied * mine
        for c in range(3):
            force_ref[c, r:r + 1, :] = force[c:c + 1]
            vel_ref[c, r:r + 1, :] = speed[c:c + 1]
            frac_ref[c, r:r + 1, :] = place[c:c + 1]
        energy_ref[r:r + 1, :] = own_ref[r * 4 + 3:r * 4 + 4, :]


def prepare_kernel(codes_ref, emb_ref, w1_ref, w2_ref, wnt_ref, wc_ref, w2t_ref, wn_ref, embt_ref, off_ref, slot_ref, cell_ref, pick_ref):
    wc_ref[...] = jnp.zeros(wc_ref.shape, BF16)
    wc_ref[0:CH, 0:NB] = w1_ref[...].astype(F32).T.astype(BF16)
    emb = jnp.concatenate([emb_ref[...].astype(F32), jnp.zeros((6, CH), F32)], axis=0)
    embt = emb.T.astype(BF16)
    wc_ref[CH:, NB:NB + 16] = embt
    embt_ref[...] = embt
    w2t_ref[...] = w2_ref[...].astype(F32).T.astype(BF16)
    wn_ref[...] = wnt_ref[...].astype(F32).T.astype(BF16)
    row_cell = lax.broadcasted_iota(jnp.int32, (144, CAP), 0) // 4
    slots = lax.broadcasted_iota(jnp.int32, (CAP, CAP), 0)
    for r in range(R):
        code = codes_ref[pl.ds(r, K, stride=R), :]
        off = code // CAP
        slot = code % CAP
        off_ref[r] = off
        slot_ref[r] = slot
        cell = off // 3 * 4 + off % 3 + r
        for k in range(K):
            lanes = slice(k * W + r * CAP, k * W + (r + 1) * CAP)
            cell_ref[:, lanes] = jnp.where(jnp.broadcast_to(cell[k:k + 1], (144, CAP)) == row_cell, 1.0, 0.0).astype(BF16)
            pick_ref[:, lanes] = jnp.where(jnp.broadcast_to(slot[k:k + 1], (CAP, CAP)) == slots, 1.0, 0.0).astype(BF16)


def edges_kernel(
    count_ref, we_ref, plane_ref, got_a_ref, got_b_ref,
    w1_ref, w2_ref, wnt_ref, wc_ref, w2t_ref, wn_ref, embt_ref, off_ref, slot_ref, cell_ref, pick_ref,
    mid_ref, send_a_ref, send_b_ref, own_ref,
    pos_s, d_s, kd_s, ey_s, exu_s, ds_s, feat_s, q_s, m_s, gr_s, t_s, ts_s, g_s, a_s,
):
    even = lax.axis_index("gx") % 2 == 0
    pos_s[0:48] = jnp.where(even, got_b_ref[...], got_a_ref[...])
    pos_s[48:96] = plane_ref[...]
    pos_s[96:144] = jnp.where(even, got_a_ref[...], got_b_ref[...])

    acc = [jnp.zeros((8, CAP), F32) for _ in range(16)]
    offs = [[off_ref[r, h * 8:(h + 1) * 8, :] for h in range(2)] for r in range(R)]
    slots = [[slot_ref[r, h * 8:(h + 1) * 8, :] for h in range(2)] for r in range(R)]
    for col in range(9):
        for zz in range(4):
            rows = [rows8(pos_s[col * 16 + zz * 4 + q:col * 16 + zz * 4 + q + 1, :], CAP) for q in range(4)]
            for r in range(R):
                dz = zz - r
                if not 0 <= dz <= 2:
                    continue
                for h in range(2):
                    hit = offs[r][h] == col * 3 + dz
                    for q in range(4):
                        got = jnp.take_along_axis(rows[q], slots[r][h], axis=1, mode="promise_in_bounds")
                        at = (r * 2 + h) * 4 + q
                        acc[at] = jnp.where(hit, got, acc[at])
    for r in range(R):
        own = [pos_s[64 + (1 + r) * 4 + c:64 + (1 + r) * 4 + c + 1, :] for c in range(3)]
        for h in range(2):
            off = offs[r][h]
            shift = (off // 9 - 1, off // 3 % 3 - 1, off % 3 - 1)
            for c in range(3):
                value = shift[c].astype(F32) + acc[(r * 2 + h) * 4 + c] - rows8(own[c], CAP)
                d_s[r, c * K + h * 8:c * K + h * 8 + 8, :] = value
            kd_s[r, h * 8:h * 8 + 8, :] = acc[(r * 2 + h) * 4 + 3]

    centre = lax.broadcasted_iota(jnp.int32, (8, W), 0).astype(F32) / (NB - 1)
    kinds16 = lax.broadcasted_iota(jnp.int32, (16, W), 0).astype(F32)

    def radial_group(group, _):
        inputs = []
        for j in range(GROUP):
            k = group * GROUP + j
            x = wide(d_s, k, 8)
            y = wide(d_s, K + k, 8)
            z = wide(d_s, 2 * K + k, 8)
            xx, yy, zz = x * x, y * y, z * z
            s = xx + yy + zz
            m1 = jnp.maximum(1.0 - s, 0.0)
            env = m1 * m1 * m1
            u = s - centre
            ex = jnp.exp(-float((NB - 1) ** 2) * (u * u))
            at = k * 8
            exu_s[pl.ds(at, 8), :] = ex * (u * (-2.0 * float((NB - 1) ** 2)))
            ex3 = env * SQRT3
            terms = (
                env, env * x, env * y, env * z, ex3 * (x * y), ex3 * (y * z), ex3 * (z * x),
                (env * HALF_SQRT3) * (xx - yy), (env * 0.5) * (2.0 * zz - xx - yy),
            )
            for m in range(9):
                ey_s[m, pl.ds(at, 8), :] = terms[m]
            kind = wide(kd_s, k, 16)
            onehot = jnp.where(kind == kinds16, 1.0, 0.0)
            inputs.append(jnp.concatenate([ex, onehot], axis=0))
        rhs = jnp.concatenate(inputs, axis=1).astype(BF16)
        lanes = pl.ds(group * (GROUP * W), GROUP * W)
        first = jnp.dot(wc_ref[...], rhs, preferred_element_type=F32)
        pre = first[:CH]
        feat = first[CH:]
        sig = 0.5 * jnp.tanh(0.5 * pre) + 0.5
        hidden = (pre * sig).astype(BF16)
        ds_s[:, lanes] = sig * (1.0 + pre * (1.0 - sig))
        feat_s[:, lanes] = feat
        radial = jnp.dot(w2t_ref[...], hidden, preferred_element_type=F32)
        for deg in range(3):
            q_s[deg * CH:(deg + 1) * CH, lanes] = radial[deg * CH:(deg + 1) * CH] * feat
        return 0

    for group in range(K // GROUP):
        radial_group(group, 0)

    def message_block(cb, _):
        base = cb * 16
        for r in range(R):
            sums = [None] * 9
            for k in range(K):
                lo = k * W + r * CAP
                q = [q_s[pl.ds(deg * CH + base, 16), lo:lo + CAP] for deg in range(3)]
                for m in range(9):
                    weight = ey_s[m, k * 8:(k + 1) * 8, r * CAP:(r + 1) * CAP]
                    weight = jnp.concatenate([weight, weight], axis=0)
                    term = q[0 if m == 0 else 1 if m < 4 else 2] * weight
                    sums[m] = term if sums[m] is None else sums[m] + term
            for m in range(9):
                m_s[m, pl.ds(base, 16), r * CAP:(r + 1) * CAP] = sums[m]
        return 0

    for cb in range(CH // 16):
        message_block(cb, 0)

    own_kind = jnp.concatenate(
        [jnp.broadcast_to(pos_s[64 + (1 + r) * 4 + 3:64 + (1 + r) * 4 + 4, :], (16, CAP)) for r in range(R)], axis=1
    )
    own_feat = jnp.dot(
        embt_ref[...], jnp.where(own_kind == kinds16, 1.0, 0.0).astype(BF16), preferred_element_type=F32
    )
    slot_number = lax.broadcasted_iota(jnp.int32, (1, CAP), 1)
    occupied = jnp.concatenate(
        [jnp.where(slot_number < count_ref[r], 1.0, 0.0) for r in range(R)], axis=1
    )
    vec = m_s[1] * m_s[1] + m_s[2] * m_s[2] + m_s[3] * m_s[3]
    ten = m_s[4] * m_s[4] + m_s[5] * m_s[5] + m_s[6] * m_s[6] + m_s[7] * m_s[7] + m_s[8] * m_s[8]
    invariant = jnp.concatenate([m_s[0], vec, ten, own_feat], axis=0).astype(BF16)
    pre = jnp.dot(wnt_ref[...], invariant, preferred_element_type=F32)
    sig = 0.5 * jnp.tanh(0.5 * pre) + 0.5
    we = jnp.broadcast_to(we_ref[...], (8, CH)).T[:, 0:1]
    energy = jnp.sum(we * (pre * sig), axis=0, keepdims=True) * occupied
    gpre = we * occupied * (sig * (1.0 + pre * (1.0 - sig)))
    ginv = jnp.dot(wn_ref[0:3 * CH, :], gpre.astype(BF16), preferred_element_type=F32).astype(BF16).astype(F32)
    m_s[0] = ginv[:CH]
    gvec = 2.0 * ginv[CH:2 * CH]
    gten = 2.0 * ginv[2 * CH:]
    for m in range(1, 9):
        m_s[m] = m_s[m] * (gvec if m < 4 else gten)

    def carried_back(k, _):
        at = k * 8
        for r in range(R):
            cols = slice(r * CAP, (r + 1) * CAP)
            lanes = pl.ds(k * W + r * CAP, CAP)
            weight = []
            for m in range(9):
                w8 = ey_s[m, pl.ds(at, 8), cols]
                weight.append(jnp.concatenate([w8, w8], axis=0))
            sums = [None] * 9
            for cb in range(CH // 16):
                feat = feat_s[cb * 16:(cb + 1) * 16, lanes]
                q = [q_s[deg * CH + cb * 16:deg * CH + (cb + 1) * 16, lanes] for deg in range(3)]
                back = [None] * 3
                for m in range(9):
                    deg = 0 if m == 0 else 1 if m < 4 else 2
                    cot = m_s[m, cb * 16:(cb + 1) * 16, cols]
                    term = cot * q[deg]
                    sums[m] = term if sums[m] is None else sums[m] + term
                    term = cot * weight[m]
                    back[deg] = term if back[deg] is None else back[deg] + term
                for deg in range(3):
                    gr_s[deg * CH + cb * 16:deg * CH + (cb + 1) * 16, lanes] = (back[deg] * feat).astype(BF16)
            for m in range(9):
                t_s[r, m, pl.ds(at, 8), :] = sums[m][:8] + sums[m][8:]
        return 0

    for k in range(K):
        carried_back(k, 0)

    def radial_back(group, _):
        lanes = pl.ds(group * (GROUP * W), GROUP * W)
        ghid = jnp.dot(w2_ref[...], gr_s[:, lanes], preferred_element_type=F32)
        gpre = (ghid.astype(BF16).astype(F32) * ds_s[:, lanes]).astype(BF16)
        gbas = jnp.dot(w1_ref[...], gpre, preferred_element_type=F32).astype(BF16).astype(F32)
        for j in range(GROUP):
            at = (group * GROUP + j) * 8
            for r in range(R):
                lo = j * W + r * CAP
                ts_s[r, pl.ds(at, 8), :] = gbas[:, lo:lo + CAP] * exu_s[pl.ds(at, 8), r * CAP:(r + 1) * CAP]
        return 0

    for group in range(K // GROUP):
        radial_back(group, 0)

    def total(ref):
        out = ref[pl.ds(0, K, stride=8), :]
        for sub in range(1, 8):
            out = out + ref[pl.ds(sub, K, stride=8), :]
        return out

    for r in range(R):
        cols = slice(r * CAP, (r + 1) * CAP)
        x, y, z = d_s[r, 0:K, :], d_s[r, K:2 * K, :], d_s[r, 2 * K:3 * K, :]
        xx, yy, zz = x * x, y * y, z * z
        s = xx + yy + zz
        m1 = jnp.maximum(1.0 - s, 0.0)
        env = m1 * m1 * m1
        t = [total(t_s.at[r, m]) for m in range(9)]
        harm = (
            None, x, y, z, SQRT3 * (x * y), SQRT3 * (y * z), SQRT3 * (z * x),
            HALF_SQRT3 * (xx - yy), 0.5 * (2.0 * zz - xx - yy),
        )
        genv = t[0]
        for m in range(1, 9):
            genv = genv + harm[m] * t[m]
        gs2 = 2.0 * (total(ts_s.at[r]) - 3.0 * (m1 * m1) * genv)
        e = [env * v for v in t]
        gx = e[1] + SQRT3 * (y * e[4] + z * e[6]) + x * (SQRT3 * e[7] - e[8] + gs2)
        gy = e[2] + SQRT3 * (x * e[4] + z * e[5]) + y * (gs2 - SQRT3 * e[7] - e[8])
        gz = e[3] + SQRT3 * (y * e[5] + x * e[6]) + z * (2.0 * e[8] + gs2)
        for c, g in enumerate((gx, gy, gz)):
            g_s[r, c * K:(c + 1) * K, :] = g
            own_ref[r * 4 + c:r * 4 + c + 1, :] = jnp.sum(g, axis=0, keepdims=True)
        own_ref[r * 4 + 3:r * 4 + 4, :] = energy[:, cols]

    sub = lax.broadcasted_iota(jnp.int32, (16, CAP), 0)
    comp = sub % 4
    for k in range(K):
        for r in range(R):
            lanes = slice(k * W + r * CAP, k * W + (r + 1) * CAP)
            gx, gy, gz = (jnp.broadcast_to(g_s[r, c * K + k:c * K + k + 1, :], (16, CAP)) for c in range(3))
            mixed = jnp.where(comp == 0, gx, jnp.where(comp == 1, gy, jnp.where(comp == 2, gz, 0.0)))
            mixed = (-mixed).astype(BF16)
            for j in range(9):
                a_s[j * 16:(j + 1) * 16, lanes] = cell_ref[j * 16:(j + 1) * 16, lanes] * mixed
    out = lax.dot_general(a_s[...], pick_ref[...], (((1,), (1,)), ((), ())), preferred_element_type=F32)
    mid_ref[...] = out[48:96]
    send_a_ref[...] = jnp.where(even, out[96:144], out[0:48])
    send_b_ref[...] = jnp.where(even, out[0:48], out[96:144])


VMEM = pl.BlockSpec(memory_space=pltpu.VMEM)
SMEM = pl.BlockSpec(memory_space=pltpu.SMEM)


def call(kernel, name, args, outs, hbm_outs=False, smem=0, scratch=()):
    shape = jax.ShapeDtypeStruct if hbm_outs else pltpu.VMEM
    return pl.pallas_call(
        kernel,
        in_specs=[SMEM] * smem + [VMEM] * (len(args) - smem),
        out_specs=[VMEM] * len(outs),
        out_shape=[shape(*out) for out in outs],
        scratch_shapes=list(scratch),
        name=name,
    )(*args)


def begin(frac, velocity, force_old, species):
    outs = [((4, CAP), F32), ((4, CAP), F32), ((4 * R, CAP), F32), ((4 * R, CAP), F32)]
    return call(begin_kernel, "begin", (frac, velocity, force_old, species), outs)


def prepare(codes, embed, w1, w2, wnt):
    outs = [
        ((2 * CH, NB + 16), BF16), ((3 * CH, CH), BF16), ((4 * CH, CH), BF16), ((CH, 16), BF16),
        ((R, K, CAP), jnp.int32), ((R, K, CAP), jnp.int32), ((144, K * W), BF16), ((CAP, K * W), BF16),
    ]
    return call(prepare_kernel, "prepare", (codes, embed, w1, w2, wnt), outs)


def edges(count, we, plane, got_a, got_b, w1, w2, wnt, prepared):
    scratch = [
        pltpu.VMEM((144, CAP), F32),
        pltpu.VMEM((R, 3 * K, CAP), F32),
        pltpu.VMEM((R, K, CAP), F32),
        pltpu.VMEM((9, 8 * K, W), F32),
        pltpu.VMEM((8 * K, W), F32),
        pltpu.VMEM((CH, K * W), F32),
        pltpu.VMEM((CH, K * W), F32),
        pltpu.VMEM((3 * CH, K * W), F32),
        pltpu.VMEM((9, CH, W), F32),
        pltpu.VMEM((3 * CH, K * W), BF16),
        pltpu.VMEM((R, 9, 8 * K, CAP), F32),
        pltpu.VMEM((R, 8 * K, CAP), F32),
        pltpu.VMEM((R, 3 * K, CAP), F32),
        pltpu.VMEM((144, K * W), BF16),
    ]
    outs = [((48, CAP), F32), ((48, CAP), F32), ((48, CAP), F32), ((8, CAP), F32)]
    args = (count, we, plane, got_a, got_b, w1, w2, wnt, *prepared)
    return call(edges_kernel, "edges", args, outs, smem=1, scratch=scratch)


def finish(count, column, got_a, got_b, own, mine, keep):
    outs = [((3, R, CAP), F32)] * 3 + [((R, CAP), F32)]
    return call(finish_kernel, "finish", (count, column, got_a, got_b, own, mine, keep), outs, hbm_outs=True, smem=1)


def shards(
    frac, velocity, force_old, species, cell_count, neighbours, embed, w_radial_in, w_radial_out, w_node, w_energy
):
    even_y = lax.axis_index("gy") % 2 == 0
    even_z = lax.axis_index("gz") % 2 == 0
    vectors = (3, R, CAP)
    count = cell_count.reshape(R)
    wnt = w_node.T
    send_a, send_b, mine, keep = begin(
        frac.reshape(vectors), velocity.reshape(vectors), force_old.reshape(vectors), species.reshape(R, CAP)
    )
    prepared = prepare(neighbours.reshape(K * R, CAP), embed, w_radial_in, w_radial_out, wnt)

    got_a, got_b = swap(send_a, "gz", False), swap(send_b, "gz", True)
    column = jnp.concatenate(
        [jnp.where(even_z, got_b, got_a), mine, jnp.where(even_z, got_a, got_b)], axis=0
    )
    got_a, got_b = swap(column, "gy", False), swap(column, "gy", True)
    plane = jnp.concatenate(
        [jnp.where(even_y, got_b, got_a), column, jnp.where(even_y, got_a, got_b)], axis=0
    )
    got_a, got_b = swap(plane, "gx", False), swap(plane, "gx", True)

    plane, send_a, send_b, own = edges(
        count, w_energy.reshape(1, CH), plane, got_a, got_b, w_radial_in, w_radial_out, wnt, prepared
    )
    plane = plane + swap(send_a, "gx", False) + swap(send_b, "gx", True)
    lower, column, upper = plane[0:16], plane[16:32], plane[32:48]
    send_a, send_b = jnp.where(even_y, upper, lower), jnp.where(even_y, lower, upper)
    column = column + swap(send_a, "gy", False) + swap(send_b, "gy", True)
    send_a = jnp.where(even_z, column[12:16], column[0:4])
    send_b = jnp.where(even_z, column[0:4], column[12:16])
    got_a, got_b = swap(send_a, "gz", False), swap(send_b, "gz", True)
    next_frac, next_velocity, next_force, energy = finish(count, column, got_a, got_b, own, mine, keep)
    return (
        next_frac.reshape(frac.shape),
        next_velocity.reshape(frac.shape),
        next_force.reshape(frac.shape),
        energy.reshape(species.shape),
    )


def solution(mesh):
    cells = P(None, "gx", "gy", "gz", None)
    in_specs = (
        cells, cells, cells, P("gx", "gy", "gz", None), P("gx", "gy", "gz"), cells, P(), P(), P(), P(), P(),
    )
    out_specs = (cells, cells, cells, P("gx", "gy", "gz", None))
    return jax.shard_map(shards, mesh=mesh, in_specs=in_specs, out_specs=out_specs, check_vma=False)
```

time: 52.4 us -> 52.2 us (level)
  other arithmetic: 1.63 us -> 0.04 us
  Pallas kernels: 10.8 us -> 12.1 us
  starting transfers between devices: 15.9 us -> 16.9 us
  waiting for transfers between devices: 16.6 us -> 15.8 us
    unnamed x22 -> x34, local copies, waits for them, and re-layouts: 4.53 us -> 6.23 us
    pallas_call x1 -> x4, Pallas kernels: 10.8 us -> 12.1 us  [call(): pl.pallas_call(kernel, in_specs=[SMEM] * smem + [VMEM] * (len(args) - sme...]
    ppermute x12, starting transfers between devices: 15.9 us -> 16.9 us  [swap(): return lax.ppermute(array, axis, pairs)]
    slice x1 -> x0, other arithmetic: 0.78 us -> none  [shards(): plane = ghost[1] + low + high]
    ppermute x12, waiting for transfers between devices: 16.6 us -> 15.8 us  [swap(): return lax.ppermute(array, axis, pairs)]
    broadcast_in_dim x1 -> x0, local copies, waits for them, and re-layouts: 0.68 us -> none  [shards(): jnp.broadcast_to(w_energy[:, None], (CH, CAP))]
    another operation x6 -> x0, other arithmetic: 0.68 us -> none  [the longest x3 0.66 us: shards(): pos = jnp.stack([low, plane, high]).reshape(144, CAP)]
    pad x1 -> x0, local copies, waits for them, and re-layouts: 0.6 us -> none  [shards(): jnp.pad(embed, ((0, 16 - embed.shape[0]), (0, 0)))]
  transfers between devices with their start and end apart: 12 -> 12, of which waited for: 9 -> 8; matrix products, arithmetic and copies ran while one was open for 5% -> 0% of each run, Pallas kernels for 0% -> 3%
where the time goes in v2:
time: 52.2 us; the launch traced here: 51.9 us
  starting transfers between devices  16.9 us (32%)
  waiting for transfers between devices  15.8 us (30%)
  Pallas kernels  12.1 us (23%)
  local copies, waits for them, and re-layouts  6.35 us (12%)
  between operations  0.75 us (1%)
    ppermute x12, starting transfers between devices, swap(): return lax.ppermute(array, axis, pairs)  16.9 us
    ppermute x12, waiting for transfers between devices, swap(): return lax.ppermute(array, axis, pairs)  15.8 us
    pallas_call x4, Pallas kernels, call(): pl.pallas_call(kernel, in_specs=[SMEM] * smem + [VMEM] * (len(args) - sme...  12.1 us
    unnamed x34, local copies, waits for them, and re-layouts  6.23 us
  transfers between devices with their start and end apart: 12, of which 8 were waited for; matrix products, arithmetic and copies ran while one was open for 0% of the time, Pallas kernels for 3%

profile of v2, /device:TPU:6, one launch (start us, length us, event | category | flops | bytes accessed | tf_op | source)
XLA Modules:
  0.0 51.9 jit_solution(11544866799709214851)
XLA Ops:
  0.6 0.8 %begin.1 = (f32[4,128]{1,0:T(4,128)S(1)}, f32[4,128]{1,0:T(4,128)S(1)}, f32[8,128]{1,0:T(8,128)S(1)}, f32[8,128]{1,0:T(8,128)S(1)}) custom-call(f32[3,2,128]{2,1,0:T(2,128)} %bitcast.21, f32[3,2,128]{2,1,0:T(2,128)} %bitcast.22, f32[3,2,128]{2,1,0:T(2,128)} %bitcast.23, s32[2,128]{1,0:T(2,128)} %bitcast.26), custom_call_target="tpu_custom_call" | custom-call | tf_op jit(solution)/shard_map/begin/pallas_call | solution.py:331
  1.4 2.3 %collective-permute-start = (f32[4,128]{1,0:T(4,128)S(1)}, f32[4,128]{1,0:T(4,128)S(1)}, u32[]{:S(2)}, u32[]{:S(2)}) collective-permute-start(f32[4,128]{1,0:T(4,128)S(1)} %get-tuple-element.24), channel_id=1, source_target_pairs={{0,3},{1,2},{2,1},{3,0},{4,7},{5,6},{6,5},{7,4},{8,11},{9,10},{10,... | collective-permute-start | bytes 6152 | tf_op jit(solution)/shard_map/ppermute | solution.py:30
  3.7 2.6 %collective-permute-done = f32[4,128]{1,0:T(4,128)S(1)} collective-permute-done((f32[4,128]{1,0:T(4,128)S(1)}, f32[4,128]{1,0:T(4,128)S(1)}, u32[]{:S(2)}, u32[]{:S(2)}) %collective-permute-start) | collective-permute-done | bytes 2080 | tf_op jit(solution)/shard_map/ppermute | solution.py:30
  6.3 1.0 %collective-permute-done.1 = f32[4,128]{1,0:T(4,128)S(1)} collective-permute-done((f32[4,128]{1,0:T(4,128)S(1)}, f32[4,128]{1,0:T(4,128)S(1)}, u32[]{:S(2)}, u32[]{:S(2)}) %collective-permute-start.1) | collective-permute-done | bytes 2080 | tf_op jit(solution)/shard_map/ppermute | solution.py:30
  7.4 5.0 %collective-permute-start.2 = (f32[16,128]{1,0:T(8,128)S(1)}, f32[16,128]{1,0:T(8,128)S(1)}, u32[]{:S(2)}, u32[]{:S(2)}) collective-permute-start(f32[16,128]{1,0:T(8,128)S(1)} %pad_maximum_fusion), channel_id=1, source_target_pairs={{0,60},{4,8},{8,4},{12,16},{16,12},{20,24},{24,20},{28,32},{32,28}... | collective-permute-start | bytes 24584 | tf_op jit(solution)/shard_map/ppermute | solution.py:30
  12.4 1.4 %collective-permute-done.2 = f32[16,128]{1,0:T(8,128)S(1)} collective-permute-done((f32[16,128]{1,0:T(8,128)S(1)}, f32[16,128]{1,0:T(8,128)S(1)}, u32[]{:S(2)}, u32[]{:S(2)}) %collective-permute-start.2) | collective-permute-done | bytes 8224 | tf_op jit(solution)/shard_map/ppermute | solution.py:30
  13.8 3.1 %collective-permute-start.5 = (f32[48,128]{1,0:T(8,128)S(1)}, f32[48,128]{1,0:T(8,128)S(1)}, u32[]{:S(2)}, u32[]{:S(2)}) collective-permute-start(f32[48,128]{1,0:T(8,128)S(1)} %concatenate.8.plane_ref), channel_id=1, source_target_pairs={{0,192},{64,128},{128,64},{192,0},{1,193},{65,129},{129,65},{193,1... | collective-permute-start | bytes 73736 | tf_op jit(solution)/shard_map/ppermute | solution.py:30
  17.1 1.7 %prepare.1 = (bf16[128,24]{1,0:T(8,128)(2,1)S(1)}, bf16[192,64]{1,0:T(8,128)(2,1)S(1)}, bf16[256,64]{1,0:T(8,128)(2,1)S(1)}, bf16[64,16]{1,0:T(8,128)(2,1)S(1)},...) custom-call(s32[32,128]{1,0:T(8,128)} %bitcast.20, ...), custom_call_target="tpu_custom_call" | custom-call | tf_op jit(solution)/shard_map/prepare/pallas_call | solution.py:331
  18.8 1.0 %copy-done = bf16[144,4096]{1,0:T(8,128)(2,1)} copy-done((bf16[144,4096]{1,0:T(8,128)(2,1)}, bf16[144,4096]{1,0:T(8,128)(2,1)S(1)}, u32[]{:S(2)}) %copy-start) | copy-done | bytes 1179672
  19.8 1.0 %copy-done.1 = bf16[128,4096]{1,0:T(8,128)(2,1)} copy-done((bf16[128,4096]{1,0:T(8,128)(2,1)}, bf16[128,4096]{1,0:T(8,128)(2,1)S(1)}, u32[]{:S(2)}) %copy-start.1) | copy-done | bytes 1048600
  20.8 0.6 %copy-done.2 = bf16[256,64]{1,0:T(8,128)(2,1)} copy-done((bf16[256,64]{1,0:T(8,128)(2,1)}, bf16[256,64]{1,0:T(8,128)(2,1)S(1)}, u32[]{:S(2)}) %copy-start.2) | copy-done | bytes 32792
  21.4 0.6 %copy-done.3 = bf16[192,64]{1,0:T(8,128)(2,1)} copy-done((bf16[192,64]{1,0:T(8,128)(2,1)}, bf16[192,64]{1,0:T(8,128)(2,1)S(1)}, u32[]{:S(2)}) %copy-start.3) | copy-done | bytes 24600
  22.0 0.6 %copy-done.5 = bf16[128,24]{1,0:T(8,128)(2,1)} copy-done((bf16[128,24]{1,0:T(8,128)(2,1)}, bf16[128,24]{1,0:T(8,128)(2,1)S(1)}, u32[]{:S(2)}) %copy-start.5) | copy-done | bytes 6168
  23.2 0.6 %copy-done.8 = s32[2,16,128]{2,1,0:T(8,128)} copy-done((s32[2,16,128]{2,1,0:T(8,128)}, s32[2,16,128]{2,1,0:T(8,128)S(1)}, u32[]{:S(2)}) %copy-start.8) | copy-done | bytes 16408
  24.5 8.2 %edges.1 = (f32[48,128]{1,0:T(8,128)S(1)}, f32[48,128]{1,0:T(8,128)S(1)}, f32[48,128]{1,0:T(8,128)S(1)}, f32[8,128]{1,0:T(8,128)S(1)}) custom-call(s32[2]{0:T(128)} %bitcast.24, f32[1,64]{1,0:T(1,128)} %bitcast.27, f32[48,128]{1,0:T(8,128)} %copy-done.11, f32[48,128]{1,0:T(8,128)} %copy-done.14, f32[48,128]{1,0:T(8,128)} %copy-done.13, ...), custom_call_target="tpu_custom_call" | custom-call | tf_op jit(solution)/shard_map/edges/pallas_call | solution.py:331
  32.7 2.0 %collective-permute-start.6 = (f32[48,128]{1,0:T(8,128)S(1)}, f32[48,128]{1,0:T(8,128)S(1)}, u32[]{:S(2)}, u32[]{:S(2)}) collective-permute-start(f32[48,128]{1,0:T(8,128)S(1)} %get-tuple-element.36), channel_id=1, source_target_pairs={{0,64},{64,0},{128,192},{192,128},{1,65},{65,1},{129,193},{193,129... | collective-permute-start | bytes 73736 | tf_op jit(solution)/shard_map/ppermute | solution.py:30
  34.9 1.7 %collective-permute-done.6 = f32[48,128]{1,0:T(8,128)S(1)} collective-permute-done((f32[48,128]{1,0:T(8,128)S(1)}, f32[48,128]{1,0:T(8,128)S(1)}, u32[]{:S(2)}, u32[]{:S(2)}) %collective-permute-start.6) | collective-permute-done | bytes 24608 | tf_op jit(solution)/shard_map/ppermute | solution.py:30
  36.6 3.1 %collective-permute-done.7 = f32[48,128]{1,0:T(8,128)S(1)} collective-permute-done((f32[48,128]{1,0:T(8,128)S(1)}, f32[48,128]{1,0:T(8,128)S(1)}, u32[]{:S(2)}, u32[]{:S(2)}) %collective-permute-start.7) | collective-permute-done | bytes 24608 | tf_op jit(solution)/shard_map/ppermute | solution.py:30
  39.8 1.9 %collective-permute-start.9 = (f32[16,128]{1,0:T(8,128)S(1)}, f32[16,128]{1,0:T(8,128)S(1)}, u32[]{:S(2)}, u32[]{:S(2)}) collective-permute-start(f32[16,128]{1,0:T(8,128)S(1)} %get-tuple-element.49), channel_id=1, source_target_pairs={{0,60},{4,8},{8,4},{12,16},{16,12},{20,24},{24,20},{28,32},{32,28}... | collective-permute-start | bytes 24584 | tf_op jit(solution)/shard_map/ppermute | solution.py:30
  41.7 2.5 %collective-permute-done.9 = f32[16,128]{1,0:T(8,128)S(1)} collective-permute-done((f32[16,128]{1,0:T(8,128)S(1)}, f32[16,128]{1,0:T(8,128)S(1)}, u32[]{:S(2)}, u32[]{:S(2)}) %collective-permute-start.9) | collective-permute-done | bytes 8224 | tf_op jit(solution)/shard_map/ppermute | solution.py:30
  44.2 2.1 %collective-permute-start.11 = (f32[4,128]{1,0:T(4,128)S(1)}, f32[4,128]{1,0:T(4,128)S(1)}, u32[]{:S(2)}, u32[]{:S(2)}) collective-permute-start(f32[4,128]{1,0:T(4,128)S(1)} %get-tuple-element.52), channel_id=1, source_target_pairs={{0,3},{1,2},{2,1},{3,0},{4,7},{5,6},{6,5},{7,4},{8,11},{9,10},{10,... | collective-permute-start | bytes 6152 | tf_op jit(solution)/shard_map/ppermute | solution.py:30
  46.3 2.8 %collective-permute-done.11.got_b_ref = f32[4,128]{1,0:T(4,128)S(1)} collective-permute-done((f32[4,128]{1,0:T(4,128)S(1)}, f32[4,128]{1,0:T(4,128)S(1)}, u32[]{:S(2)}, u32[]{:S(2)}) %collective-permute-start.11) | collective-permute-done | bytes 2080 | tf_op jit(solution)/shard_map/ppermute | solution.py:30
  49.1 0.8 %collective-permute-done.10.got_a_ref = f32[4,128]{1,0:T(4,128)S(1)} collective-permute-done((f32[4,128]{1,0:T(4,128)S(1)}, f32[4,128]{1,0:T(4,128)S(1)}, u32[]{:S(2)}, u32[]{:S(2)}) %collective-permute-start.10) | collective-permute-done | bytes 2080 | tf_op jit(solution)/shard_map/ppermute | solution.py:30
  50.5 1.4 %finish.1 = (f32[3,2,128]{2,1,0:T(2,128)}, f32[3,2,128]{2,1,0:T(2,128)}, f32[3,2,128]{2,1,0:T(2,128)}, f32[2,128]{1,0:T(2,128)}) custom-call(s32[2]{0:T(128)} %bitcast.25, f32[16,128]{1,0:T(8,128)} %copy-done.12, f32[4,128]{1,0:T(4,128)} %copy-done.16, f32[4,128]{1,0:T(4,128)} %copy-done.15, f32[8,128]{1,0:T(8,128)} %copy-done.10, f32[8,128]{1,0:T(8,128)} %copy-done.4, ...), custom_call_target="tpu_custom_call" | custom-call | tf_op jit(solution)/shard_map/finish/pallas_call | solution.py:331
  (46 shorter events, 2.5 us)
Async XLA Ops:
  1.4 15.7 %copy-start.9 = (f32[8,128]{1,0:T(8,128)}, f32[8,128]{1,0:T(8,128)S(1)}, u32[]{:S(2)}) copy-start(f32[8,128]{1,0:T(8,128)S(1)} %get-tuple-element.39.keep_ref) | copy-start | bytes 12292
  1.4 31.3 %copy-start.4 = (f32[8,128]{1,0:T(8,128)}, f32[8,128]{1,0:T(8,128)S(1)}, u32[]{:S(2)}) copy-start(f32[8,128]{1,0:T(8,128)S(1)} %get-tuple-element.26.mine_ref) | copy-start | bytes 12292
  1.4 4.9 %collective-permute-start = (f32[4,128]{1,0:T(4,128)S(1)}, f32[4,128]{1,0:T(4,128)S(1)}, u32[]{:S(2)}, u32[]{:S(2)}) collective-permute-start(f32[4,128]{1,0:T(4,128)S(1)} %get-tuple-element.24), channel_id=1, source_target_pairs={{0,3},{1,2},{2,1},{3,0},{4,7},{5,6},{6,5},{7,4},{8,11},{9,10},{10,... | collective-permute-start | bytes 6152 | tf_op jit(solution)/shard_map/ppermute | solution.py:30
  3.7 3.6 %collective-permute-start.1 = (f32[4,128]{1,0:T(4,128)S(1)}, f32[4,128]{1,0:T(4,128)S(1)}, u32[]{:S(2)}, u32[]{:S(2)}) collective-permute-start(f32[4,128]{1,0:T(4,128)S(1)} %get-tuple-element.25), channel_id=1, source_target_pairs={{0,1},{1,0},{2,3},{3,2},{4,5},{5,4},{6,7},{7,6},{8,9},{9,8},{10,11... | collective-permute-start | bytes 6152 | tf_op jit(solution)/shard_map/ppermute | solution.py:30
  7.3 5.1 %collective-permute-start.3 = (f32[16,128]{1,0:T(8,128)S(1)}, f32[16,128]{1,0:T(8,128)S(1)}, u32[]{:S(2)}, u32[]{:S(2)}) collective-permute-start(f32[16,128]{1,0:T(8,128)S(1)} %pad_maximum_fusion), channel_id=1, source_target_pairs={{0,4},{4,0},{8,12},{12,8},{16,20},{20,16},{24,28},{28,24},{32,36},... | collective-permute-start | bytes 24584 | tf_op jit(solution)/shard_map/ppermute | solution.py:30
  7.4 6.3 %collective-permute-start.2 = (f32[16,128]{1,0:T(8,128)S(1)}, f32[16,128]{1,0:T(8,128)S(1)}, u32[]{:S(2)}, u32[]{:S(2)}) collective-permute-start(f32[16,128]{1,0:T(8,128)S(1)} %pad_maximum_fusion), channel_id=1, source_target_pairs={{0,60},{4,8},{8,4},{12,16},{16,12},{20,24},{24,20},{28,32},{32,28}... | collective-permute-start | bytes 24584 | tf_op jit(solution)/shard_map/ppermute | solution.py:30
  13.8 10.0 %copy-start.11 = (f32[48,128]{1,0:T(8,128)}, f32[48,128]{1,0:T(8,128)S(1)}, u32[]{:S(2)}) copy-start(f32[48,128]{1,0:T(8,128)S(1)} %concatenate.8.plane_ref) | copy-start | bytes 73732
  13.8 10.0 %collective-permute-start.5 = (f32[48,128]{1,0:T(8,128)S(1)}, f32[48,128]{1,0:T(8,128)S(1)}, u32[]{:S(2)}, u32[]{:S(2)}) collective-permute-start(f32[48,128]{1,0:T(8,128)S(1)} %concatenate.8.plane_ref), channel_id=1, source_target_pairs={{0,192},{64,128},{128,64},{192,0},{1,193},{65,129},{129,65},{193,1... | collective-permute-start | bytes 73736 | tf_op jit(solution)/shard_map/ppermute | solution.py:30
  16.9 6.9 %collective-permute-start.4 = (f32[48,128]{1,0:T(8,128)S(1)}, f32[48,128]{1,0:T(8,128)S(1)}, u32[]{:S(2)}, u32[]{:S(2)}) collective-permute-start(f32[48,128]{1,0:T(8,128)S(1)} %concatenate.8.plane_ref), channel_id=1, source_target_pairs={{0,64},{64,0},{128,192},{192,128},{1,65},{65,1},{129,193},{193,129... | collective-permute-start | bytes 73736 | tf_op jit(solution)/shard_map/ppermute | solution.py:30
  18.8 1.0 %copy-start = (bf16[144,4096]{1,0:T(8,128)(2,1)}, bf16[144,4096]{1,0:T(8,128)(2,1)S(1)}, u32[]{:S(2)}) copy-start(bf16[144,4096]{1,0:T(8,128)(2,1)S(1)} %get-tuple-element.33.cell_ref) | copy-start | bytes 3538948
  19.8 1.0 %copy-start.1 = (bf16[128,4096]{1,0:T(8,128)(2,1)}, bf16[128,4096]{1,0:T(8,128)(2,1)S(1)}, u32[]{:S(2)}) copy-start(bf16[128,4096]{1,0:T(8,128)(2,1)S(1)} %get-tuple-element.34.pick_ref) | copy-start | bytes 3145732
  20.8 0.6 %copy-start.2 = (bf16[256,64]{1,0:T(8,128)(2,1)}, bf16[256,64]{1,0:T(8,128)(2,1)S(1)}, u32[]{:S(2)}) copy-start(bf16[256,64]{1,0:T(8,128)(2,1)S(1)} %get-tuple-element.29.wn_ref) | copy-start | bytes 98308
  21.4 0.6 %copy-start.3 = (bf16[192,64]{1,0:T(8,128)(2,1)}, bf16[192,64]{1,0:T(8,128)(2,1)S(1)}, u32[]{:S(2)}) copy-start(bf16[192,64]{1,0:T(8,128)(2,1)S(1)} %get-tuple-element.28.w2t_ref) | copy-start | bytes 73732
  23.8 0.6 %copy-start.13 = (f32[48,128]{1,0:T(8,128)}, f32[48,128]{1,0:T(8,128)S(1)}, u32[]{:S(2)}) copy-start(f32[48,128]{1,0:T(8,128)S(1)} %collective-permute-done.5.got_b_ref) | copy-start | bytes 73732
  23.8 0.6 %copy-start.14 = (f32[48,128]{1,0:T(8,128)}, f32[48,128]{1,0:T(8,128)S(1)}, u32[]{:S(2)}) copy-start(f32[48,128]{1,0:T(8,128)S(1)} %collective-permute-done.4.got_a_ref) | copy-start | bytes 73732
  32.7 17.2 %copy-start.10 = (f32[8,128]{1,0:T(8,128)}, f32[8,128]{1,0:T(8,128)S(1)}, u32[]{:S(2)}) copy-start(f32[8,128]{1,0:T(8,128)S(1)} %get-tuple-element.38.own_ref) | copy-start | bytes 12292
  32.7 3.9 %collective-permute-start.6 = (f32[48,128]{1,0:T(8,128)S(1)}, f32[48,128]{1,0:T(8,128)S(1)}, u32[]{:S(2)}, u32[]{:S(2)}) collective-permute-start(f32[48,128]{1,0:T(8,128)S(1)} %get-tuple-element.36), channel_id=1, source_target_pairs={{0,64},{64,0},{128,192},{192,128},{1,65},{65,1},{129,193},{193,129... | collective-permute-start | bytes 73736 | tf_op jit(solution)/shard_map/ppermute | solution.py:30
  34.7 5.0 %collective-permute-start.7 = (f32[48,128]{1,0:T(8,128)S(1)}, f32[48,128]{1,0:T(8,128)S(1)}, u32[]{:S(2)}, u32[]{:S(2)}) collective-permute-start(f32[48,128]{1,0:T(8,128)S(1)} %get-tuple-element.37), channel_id=1, source_target_pairs={{0,192},{64,128},{128,64},{192,0},{1,193},{65,129},{129,65},{193,1... | collective-permute-start | bytes 73736 | tf_op jit(solution)/shard_map/ppermute | solution.py:30
  39.7 2.0 %collective-permute-start.8 = (f32[16,128]{1,0:T(8,128)S(1)}, f32[16,128]{1,0:T(8,128)S(1)}, u32[]{:S(2)}, u32[]{:S(2)}) collective-permute-start(f32[16,128]{1,0:T(8,128)S(1)} %get-tuple-element.48), channel_id=1, source_target_pairs={{0,4},{4,0},{8,12},{12,8},{16,20},{20,16},{24,28},{28,24},{32,36},... | collective-permute-start | bytes 24584 | tf_op jit(solution)/shard_map/ppermute | solution.py:30
  39.8 4.4 %collective-permute-start.9 = (f32[16,128]{1,0:T(8,128)S(1)}, f32[16,128]{1,0:T(8,128)S(1)}, u32[]{:S(2)}, u32[]{:S(2)}) collective-permute-start(f32[16,128]{1,0:T(8,128)S(1)} %get-tuple-element.49), channel_id=1, source_target_pairs={{0,60},{4,8},{8,4},{12,16},{16,12},{20,24},{24,20},{28,32},{32,28}... | collective-permute-start | bytes 24584 | tf_op jit(solution)/shard_map/ppermute | solution.py:30
  44.2 5.7 %copy-start.12 = (f32[16,128]{1,0:T(8,128)}, f32[16,128]{1,0:T(8,128)S(1)}, u32[]{:S(2)}) copy-start(f32[16,128]{1,0:T(8,128)S(1)} %fusion.mid_ref) | copy-start | bytes 24580
  44.2 4.9 %collective-permute-start.11 = (f32[4,128]{1,0:T(4,128)S(1)}, f32[4,128]{1,0:T(4,128)S(1)}, u32[]{:S(2)}, u32[]{:S(2)}) collective-permute-start(f32[4,128]{1,0:T(4,128)S(1)} %get-tuple-element.52), channel_id=1, source_target_pairs={{0,3},{1,2},{2,1},{3,0},{4,7},{5,6},{6,5},{7,4},{8,11},{9,10},{10,... | collective-permute-start | bytes 6152 | tf_op jit(solution)/shard_map/ppermute | solution.py:30
  46.3 3.6 %collective-permute-start.10 = (f32[4,128]{1,0:T(4,128)S(1)}, f32[4,128]{1,0:T(4,128)S(1)}, u32[]{:S(2)}, u32[]{:S(2)}) collective-permute-start(f32[4,128]{1,0:T(4,128)S(1)} %get-tuple-element.53), channel_id=1, source_target_pairs={{0,1},{1,0},{2,3},{3,2},{4,5},{5,4},{6,7},{7,6},{8,9},{9,8},{10,11... | collective-permute-start | bytes 6152 | tf_op jit(solution)/shard_map/ppermute | solution.py:30
  49.1 0.8 %copy-start.15 = (f32[4,128]{1,0:T(4,128)}, f32[4,128]{1,0:T(4,128)S(1)}, u32[]{:S(2)}) copy-start(f32[4,128]{1,0:T(4,128)S(1)} %collective-permute-done.11.got_b_ref) | copy-start | bytes 6148
  (5 other events, 3.0 us)

commit v3 on v2

--- a/solution.py
+++ b/solution.py
@@ -105,8 +105,8 @@
 
 
 def edges_kernel(
-    count_ref, we_ref, plane_ref, got_a_ref, got_b_ref,
-    w1_ref, w2_ref, wnt_ref, wc_ref, w2t_ref, wn_ref, embt_ref, off_ref, slot_ref, cell_ref, pick_ref,
+    count_ref, we_ref, w1_ref, w2_ref, wnt_ref,
+    plane_ref, got_a_ref, got_b_ref, wc_ref, w2t_ref, wn_ref, embt_ref, off_ref, slot_ref, cell_ref, pick_ref,
     mid_ref, send_a_ref, send_b_ref, own_ref,
     pos_s, d_s, kd_s, ey_s, exu_s, ds_s, feat_s, q_s, m_s, gr_s, t_s, ts_s, g_s, a_s,
 ):
@@ -326,8 +326,9 @@
 SMEM = pl.BlockSpec(memory_space=pltpu.SMEM)
 
 
-def call(kernel, name, args, outs, hbm_outs=False, smem=0, scratch=()):
+def call(kernel, name, args, outs, near, hbm_outs=False, smem=0, scratch=()):
     shape = jax.ShapeDtypeStruct if hbm_outs else pltpu.VMEM
+    args = args[:near] + tuple(pltpu.with_memory_space_constraint(a, pltpu.VMEM) for a in args[near:])
     return pl.pallas_call(
         kernel,
         in_specs=[SMEM] * smem + [VMEM] * (len(args) - smem),
@@ -340,7 +341,7 @@
 
 def begin(frac, velocity, force_old, species):
     outs = [((4, CAP), F32), ((4, CAP), F32), ((4 * R, CAP), F32), ((4 * R, CAP), F32)]
-    return call(begin_kernel, "begin", (frac, velocity, force_old, species), outs)
+    return call(begin_kernel, "begin", (frac, velocity, force_old, species), outs, 4)
 
 
 def prepare(codes, embed, w1, w2, wnt):
@@ -348,7 +349,7 @@
         ((2 * CH, NB + 16), BF16), ((3 * CH, CH), BF16), ((4 * CH, CH), BF16), ((CH, 16), BF16),
         ((R, K, CAP), jnp.int32), ((R, K, CAP), jnp.int32), ((144, K * W), BF16), ((CAP, K * W), BF16),
     ]
-    return call(prepare_kernel, "prepare", (codes, embed, w1, w2, wnt), outs)
+    return call(prepare_kernel, "prepare", (codes, embed, w1, w2, wnt), outs, 5)
 
 
 def edges(count, we, plane, got_a, got_b, w1, w2, wnt, prepared):
@@ -369,13 +370,13 @@
         pltpu.VMEM((144, K * W), BF16),
     ]
     outs = [((48, CAP), F32), ((48, CAP), F32), ((48, CAP), F32), ((8, CAP), F32)]
-    args = (count, we, plane, got_a, got_b, w1, w2, wnt, *prepared)
-    return call(edges_kernel, "edges", args, outs, smem=1, scratch=scratch)
+    args = (count, we, w1, w2, wnt, plane, got_a, got_b, *prepared)
+    return call(edges_kernel, "edges", args, outs, 5, smem=1, scratch=scratch)
 
 
 def finish(count, column, got_a, got_b, own, mine, keep):
     outs = [((3, R, CAP), F32)] * 3 + [((R, CAP), F32)]
-    return call(finish_kernel, "finish", (count, column, got_a, got_b, own, mine, keep), outs, hbm_outs=True, smem=1)
+    return call(finish_kernel, "finish", (count, column, got_a, got_b, own, mine, keep), outs, 1, hbm_outs=True, smem=1)
 
 
 def shards(

time: 52.2 us -> 45 us (0.86)
  local copies, waits for them, and re-layouts: 6.35 us -> 0.11 us
  Pallas kernels: 12.1 us -> 10.9 us
  waiting for transfers between devices: 15.8 us -> 17 us
  starting transfers between devices: 16.9 us -> 16 us
    unnamed x34 -> x0, local copies, waits for them, and re-layouts: 6.23 us -> none
    ppermute x12, waiting for transfers between devices: 15.8 us -> 17 us  [swap(): return lax.ppermute(array, axis, pairs)]
    pallas_call x4, Pallas kernels: 12.1 us -> 10.9 us  [call(): pl.pallas_call(kernel, in_specs=[SMEM] * smem + [VMEM] * (len(args) - sme...]
    ppermute x12, starting transfers between devices: 16.9 us -> 16 us  [swap(): return lax.ppermute(array, axis, pairs)]
  transfers between devices with their start and end apart: 12 -> 12, of which waited for: 8 -> 10; matrix products, arithmetic and copies ran while one was open for 0% -> 0% of each run, Pallas kernels for 3% -> 4%
where the time goes in v3:
time: 45 us; the launch traced here: 44.7 us
  waiting for transfers between devices  17 us (38%)
  starting transfers between devices  16 us (36%)
  Pallas kernels  10.9 us (24%)
  between operations  0.68 us (2%)
    ppermute x12, waiting for transfers between devices, swap(): return lax.ppermute(array, axis, pairs)  17 us
    ppermute x12, starting transfers between devices, swap(): return lax.ppermute(array, axis, pairs)  16 us
    pallas_call x4, Pallas kernels, call(): pl.pallas_call(kernel, in_specs=[SMEM] * smem + [VMEM] * (len(args) - sme...  10.9 us
  transfers between devices with their start and end apart: 12, of which 10 were waited for; matrix products, arithmetic and copies ran while one was open for 0% of the time, Pallas kernels for 4%

profile of v3, /device:TPU:6, one launch (start us, length us, event | category | flops | bytes accessed | tf_op | source)
XLA Modules:
  0.0 44.7 jit_solution(8582535834009665594)
XLA Ops:
  0.6 0.8 %begin.1 = (f32[4,128]{1,0:T(4,128)S(1)}, f32[4,128]{1,0:T(4,128)S(1)}, f32[8,128]{1,0:T(8,128)S(1)}, f32[8,128]{1,0:T(8,128)S(1)}) custom-call(f32[3,2,128]{2,1,0:T(2,128)} %bitcast.21, f32[3,2,128]{2,1,0:T(2,128)} %bitcast.22, f32[3,2,128]{2,1,0:T(2,128)} %bitcast.23, s32[2,128]{1,0:T(2,128)} %bitcast.26), custom_call_target="tpu_custom_call" | custom-call | tf_op jit(solution)/shard_map/begin/pallas_call | solution.py:332
  1.4 2.3 %collective-permute-start = (f32[4,128]{1,0:T(4,128)S(1)}, f32[4,128]{1,0:T(4,128)S(1)}, u32[]{:S(2)}, u32[]{:S(2)}) collective-permute-start(f32[4,128]{1,0:T(4,128)S(1)} %get-tuple-element.24), channel_id=1, source_target_pairs={{0,3},{1,2},{2,1},{3,0},{4,7},{5,6},{6,5},{7,4},{8,11},{9,10},{10,... | collective-permute-start | bytes 6152 | tf_op jit(solution)/shard_map/ppermute | solution.py:30
  3.7 2.6 %collective-permute-done = f32[4,128]{1,0:T(4,128)S(1)} collective-permute-done((f32[4,128]{1,0:T(4,128)S(1)}, f32[4,128]{1,0:T(4,128)S(1)}, u32[]{:S(2)}, u32[]{:S(2)}) %collective-permute-start) | collective-permute-done | bytes 2080 | tf_op jit(solution)/shard_map/ppermute | solution.py:30
  6.3 1.0 %collective-permute-done.1 = f32[4,128]{1,0:T(4,128)S(1)} collective-permute-done((f32[4,128]{1,0:T(4,128)S(1)}, f32[4,128]{1,0:T(4,128)S(1)}, u32[]{:S(2)}, u32[]{:S(2)}) %collective-permute-start.1) | collective-permute-done | bytes 2080 | tf_op jit(solution)/shard_map/ppermute | solution.py:30
  7.3 0.1 collective-permute-start.3
  7.4 5.0 %collective-permute-start.2 = (f32[16,128]{1,0:T(8,128)S(1)}, f32[16,128]{1,0:T(8,128)S(1)}, u32[]{:S(2)}, u32[]{:S(2)}) collective-permute-start(f32[16,128]{1,0:T(8,128)S(1)} %pad_maximum_fusion), channel_id=1, source_target_pairs={{0,60},{4,8},{8,4},{12,16},{16,12},{20,24},{24,20},{28,32},{32,28}... | collective-permute-start | bytes 24584 | tf_op jit(solution)/shard_map/ppermute | solution.py:30
  12.3 1.4 %collective-permute-done.2 = f32[16,128]{1,0:T(8,128)S(1)} collective-permute-done((f32[16,128]{1,0:T(8,128)S(1)}, f32[16,128]{1,0:T(8,128)S(1)}, u32[]{:S(2)}, u32[]{:S(2)}) %collective-permute-start.2) | collective-permute-done | bytes 8224 | tf_op jit(solution)/shard_map/ppermute | solution.py:30
  13.7 0.1 concatenate.8.plane_ref
  13.8 3.1 %collective-permute-start.5 = (f32[48,128]{1,0:T(8,128)S(1)}, f32[48,128]{1,0:T(8,128)S(1)}, u32[]{:S(2)}, u32[]{:S(2)}) collective-permute-start(f32[48,128]{1,0:T(8,128)S(1)} %concatenate.8.plane_ref), channel_id=1, source_target_pairs={{0,192},{64,128},{128,64},{192,0},{1,193},{65,129},{129,65},{193,1... | collective-permute-start | bytes 73736 | tf_op jit(solution)/shard_map/ppermute | solution.py:30
  16.9 0.1 collective-permute-start.4
  17.1 1.7 %prepare.1 = (bf16[128,24]{1,0:T(8,128)(2,1)S(1)}, bf16[192,64]{1,0:T(8,128)(2,1)S(1)}, bf16[256,64]{1,0:T(8,128)(2,1)S(1)}, bf16[64,16]{1,0:T(8,128)(2,1)S(1)},...) custom-call(s32[32,128]{1,0:T(8,128)} %bitcast.20, ...), custom_call_target="tpu_custom_call" | custom-call | tf_op jit(solution)/shard_map/prepare/pallas_call | solution.py:332
  18.7 0.2 collective-permute-done.5.got_b_ref
  18.9 1.8 %collective-permute-done.4.got_a_ref = f32[48,128]{1,0:T(8,128)S(1)} collective-permute-done((f32[48,128]{1,0:T(8,128)S(1)}, f32[48,128]{1,0:T(8,128)S(1)}, u32[]{:S(2)}, u32[]{:S(2)}) %collective-permute-start.4) | collective-permute-done | bytes 24608 | tf_op jit(solution)/shard_map/ppermute | solution.py:30
  20.7 7.2 %edges.1 = (f32[48,128]{1,0:T(8,128)S(1)}, f32[48,128]{1,0:T(8,128)S(1)}, f32[48,128]{1,0:T(8,128)S(1)}, f32[8,128]{1,0:T(8,128)S(1)}) custom-call(s32[2]{0:T(128)} %bitcast.24, f32[1,64]{1,0:T(1,128)} %bitcast.27, bf16[8,64]{1,0:T(8,128)(2,1)} %w1_ref.3, bf16[64,192]{1,0:T(8,128)(2,1)} %w2_ref.3, bf16[64,256]{1,0:T(8,128)(2,1)} %bitcast.19, ...), custom_call_target="tpu_custom_call" | custom-call | tf_op jit(solution)/shard_map/edges/pallas_call | solution.py:332
  28.0 0.2 collective-permute-start.6
  28.2 1.2 %collective-permute-start.7 = (f32[48,128]{1,0:T(8,128)S(1)}, f32[48,128]{1,0:T(8,128)S(1)}, u32[]{:S(2)}, u32[]{:S(2)}) collective-permute-start(f32[48,128]{1,0:T(8,128)S(1)} %get-tuple-element.37), channel_id=1, source_target_pairs={{0,192},{64,128},{128,64},{192,0},{1,193},{65,129},{129,65},{193,1... | collective-permute-start | bytes 73736 | tf_op jit(solution)/shard_map/ppermute | solution.py:30
  29.4 2.5 %collective-permute-done.6 = f32[48,128]{1,0:T(8,128)S(1)} collective-permute-done((f32[48,128]{1,0:T(8,128)S(1)}, f32[48,128]{1,0:T(8,128)S(1)}, u32[]{:S(2)}, u32[]{:S(2)}) %collective-permute-start.6) | collective-permute-done | bytes 24608 | tf_op jit(solution)/shard_map/ppermute | solution.py:30
  31.9 1.3 %collective-permute-done.7 = f32[48,128]{1,0:T(8,128)S(1)} collective-permute-done((f32[48,128]{1,0:T(8,128)S(1)}, f32[48,128]{1,0:T(8,128)S(1)}, u32[]{:S(2)}, u32[]{:S(2)}) %collective-permute-start.7) | collective-permute-done | bytes 24608 | tf_op jit(solution)/shard_map/ppermute | solution.py:30
  33.4 1.8 %collective-permute-start.9 = (f32[16,128]{1,0:T(8,128)S(1)}, f32[16,128]{1,0:T(8,128)S(1)}, u32[]{:S(2)}, u32[]{:S(2)}) collective-permute-start(f32[16,128]{1,0:T(8,128)S(1)} %get-tuple-element.49), channel_id=1, source_target_pairs={{0,60},{4,8},{8,4},{12,16},{16,12},{20,24},{24,20},{28,32},{32,28}... | collective-permute-start | bytes 24584 | tf_op jit(solution)/shard_map/ppermute | solution.py:30
  35.2 2.6 %collective-permute-done.9 = f32[16,128]{1,0:T(8,128)S(1)} collective-permute-done((f32[16,128]{1,0:T(8,128)S(1)}, f32[16,128]{1,0:T(8,128)S(1)}, u32[]{:S(2)}, u32[]{:S(2)}) %collective-permute-start.9) | collective-permute-done | bytes 8224 | tf_op jit(solution)/shard_map/ppermute | solution.py:30
  37.8 2.1 %collective-permute-start.11 = (f32[4,128]{1,0:T(4,128)S(1)}, f32[4,128]{1,0:T(4,128)S(1)}, u32[]{:S(2)}, u32[]{:S(2)}) collective-permute-start(f32[4,128]{1,0:T(4,128)S(1)} %get-tuple-element.52), channel_id=1, source_target_pairs={{0,3},{1,2},{2,1},{3,0},{4,7},{5,6},{6,5},{7,4},{8,11},{9,10},{10,... | collective-permute-start | bytes 6152 | tf_op jit(solution)/shard_map/ppermute | solution.py:30
  39.9 2.8 %collective-permute-done.11.got_b_ref = f32[4,128]{1,0:T(4,128)S(1)} collective-permute-done((f32[4,128]{1,0:T(4,128)S(1)}, f32[4,128]{1,0:T(4,128)S(1)}, u32[]{:S(2)}, u32[]{:S(2)}) %collective-permute-start.11) | collective-permute-done | bytes 2080 | tf_op jit(solution)/shard_map/ppermute | solution.py:30
  42.6 0.8 %collective-permute-done.10.got_a_ref = f32[4,128]{1,0:T(4,128)S(1)} collective-permute-done((f32[4,128]{1,0:T(4,128)S(1)}, f32[4,128]{1,0:T(4,128)S(1)}, u32[]{:S(2)}, u32[]{:S(2)}) %collective-permute-start.10) | collective-permute-done | bytes 2080 | tf_op jit(solution)/shard_map/ppermute | solution.py:30
  43.4 1.3 %finish.1 = (f32[3,2,128]{2,1,0:T(2,128)}, f32[3,2,128]{2,1,0:T(2,128)}, f32[3,2,128]{2,1,0:T(2,128)}, f32[2,128]{1,0:T(2,128)}) custom-call(s32[2]{0:T(128)} %bitcast.25, f32[16,128]{1,0:T(8,128)S(1)} %fusion.mid_ref, f32[4,128]{1,0:T(4,128)S(1)} %collective-permute-done.10.got_a_ref, f32[4,128]{1,0:T(4,128)S(1)} %collective-permute-done.11.got_b_ref, ...), custom_call_target="tpu_custom_call" | custom-call | tf_op jit(solution)/shard_map/finish/pallas_call | solution.py:332
  (12 shorter events, 0.1 us)
Async XLA Ops:
  1.4 4.9 %collective-permute-start = (f32[4,128]{1,0:T(4,128)S(1)}, f32[4,128]{1,0:T(4,128)S(1)}, u32[]{:S(2)}, u32[]{:S(2)}) collective-permute-start(f32[4,128]{1,0:T(4,128)S(1)} %get-tuple-element.24), channel_id=1, source_target_pairs={{0,3},{1,2},{2,1},{3,0},{4,7},{5,6},{6,5},{7,4},{8,11},{9,10},{10,... | collective-permute-start | bytes 6152 | tf_op jit(solution)/shard_map/ppermute | solution.py:30
  3.7 3.6 %collective-permute-start.1 = (f32[4,128]{1,0:T(4,128)S(1)}, f32[4,128]{1,0:T(4,128)S(1)}, u32[]{:S(2)}, u32[]{:S(2)}) collective-permute-start(f32[4,128]{1,0:T(4,128)S(1)} %get-tuple-element.25), channel_id=1, source_target_pairs={{0,1},{1,0},{2,3},{3,2},{4,5},{5,4},{6,7},{7,6},{8,9},{9,8},{10,11... | collective-permute-start | bytes 6152 | tf_op jit(solution)/shard_map/ppermute | solution.py:30
  7.3 5.1 %collective-permute-start.3 = (f32[16,128]{1,0:T(8,128)S(1)}, f32[16,128]{1,0:T(8,128)S(1)}, u32[]{:S(2)}, u32[]{:S(2)}) collective-permute-start(f32[16,128]{1,0:T(8,128)S(1)} %pad_maximum_fusion), channel_id=1, source_target_pairs={{0,4},{4,0},{8,12},{12,8},{16,20},{20,16},{24,28},{28,24},{32,36},... | collective-permute-start | bytes 24584 | tf_op jit(solution)/shard_map/ppermute | solution.py:30
  7.4 6.3 %collective-permute-start.2 = (f32[16,128]{1,0:T(8,128)S(1)}, f32[16,128]{1,0:T(8,128)S(1)}, u32[]{:S(2)}, u32[]{:S(2)}) collective-permute-start(f32[16,128]{1,0:T(8,128)S(1)} %pad_maximum_fusion), channel_id=1, source_target_pairs={{0,60},{4,8},{8,4},{12,16},{16,12},{20,24},{24,20},{28,32},{32,28}... | collective-permute-start | bytes 24584 | tf_op jit(solution)/shard_map/ppermute | solution.py:30
  13.8 5.1 %collective-permute-start.5 = (f32[48,128]{1,0:T(8,128)S(1)}, f32[48,128]{1,0:T(8,128)S(1)}, u32[]{:S(2)}, u32[]{:S(2)}) collective-permute-start(f32[48,128]{1,0:T(8,128)S(1)} %concatenate.8.plane_ref), channel_id=1, source_target_pairs={{0,192},{64,128},{128,64},{192,0},{1,193},{65,129},{129,65},{193,1... | collective-permute-start | bytes 73736 | tf_op jit(solution)/shard_map/ppermute | solution.py:30
  16.9 3.8 %collective-permute-start.4 = (f32[48,128]{1,0:T(8,128)S(1)}, f32[48,128]{1,0:T(8,128)S(1)}, u32[]{:S(2)}, u32[]{:S(2)}) collective-permute-start(f32[48,128]{1,0:T(8,128)S(1)} %concatenate.8.plane_ref), channel_id=1, source_target_pairs={{0,64},{64,0},{128,192},{192,128},{1,65},{65,1},{129,193},{193,129... | collective-permute-start | bytes 73736 | tf_op jit(solution)/shard_map/ppermute | solution.py:30
  28.0 3.9 %collective-permute-start.6 = (f32[48,128]{1,0:T(8,128)S(1)}, f32[48,128]{1,0:T(8,128)S(1)}, u32[]{:S(2)}, u32[]{:S(2)}) collective-permute-start(f32[48,128]{1,0:T(8,128)S(1)} %get-tuple-element.36), channel_id=1, source_target_pairs={{0,64},{64,0},{128,192},{192,128},{1,65},{65,1},{129,193},{193,129... | collective-permute-start | bytes 73736 | tf_op jit(solution)/shard_map/ppermute | solution.py:30
  28.2 5.0 %collective-permute-start.7 = (f32[48,128]{1,0:T(8,128)S(1)}, f32[48,128]{1,0:T(8,128)S(1)}, u32[]{:S(2)}, u32[]{:S(2)}) collective-permute-start(f32[48,128]{1,0:T(8,128)S(1)} %get-tuple-element.37), channel_id=1, source_target_pairs={{0,192},{64,128},{128,64},{192,0},{1,193},{65,129},{129,65},{193,1... | collective-permute-start | bytes 73736 | tf_op jit(solution)/shard_map/ppermute | solution.py:30
  33.3 1.9 %collective-permute-start.8 = (f32[16,128]{1,0:T(8,128)S(1)}, f32[16,128]{1,0:T(8,128)S(1)}, u32[]{:S(2)}, u32[]{:S(2)}) collective-permute-start(f32[16,128]{1,0:T(8,128)S(1)} %get-tuple-element.48), channel_id=1, source_target_pairs={{0,4},{4,0},{8,12},{12,8},{16,20},{20,16},{24,28},{28,24},{32,36},... | collective-permute-start | bytes 24584 | tf_op jit(solution)/shard_map/ppermute | solution.py:30
  33.4 4.4 %collective-permute-start.9 = (f32[16,128]{1,0:T(8,128)S(1)}, f32[16,128]{1,0:T(8,128)S(1)}, u32[]{:S(2)}, u32[]{:S(2)}) collective-permute-start(f32[16,128]{1,0:T(8,128)S(1)} %get-tuple-element.49), channel_id=1, source_target_pairs={{0,60},{4,8},{8,4},{12,16},{16,12},{20,24},{24,20},{28,32},{32,28}... | collective-permute-start | bytes 24584 | tf_op jit(solution)/shard_map/ppermute | solution.py:30
  37.8 4.9 %collective-permute-start.11 = (f32[4,128]{1,0:T(4,128)S(1)}, f32[4,128]{1,0:T(4,128)S(1)}, u32[]{:S(2)}, u32[]{:S(2)}) collective-permute-start(f32[4,128]{1,0:T(4,128)S(1)} %get-tuple-element.52), channel_id=1, source_target_pairs={{0,3},{1,2},{2,1},{3,0},{4,7},{5,6},{6,5},{7,4},{8,11},{9,10},{10,... | collective-permute-start | bytes 6152 | tf_op jit(solution)/shard_map/ppermute | solution.py:30
  39.9 3.6 %collective-permute-start.10 = (f32[4,128]{1,0:T(4,128)S(1)}, f32[4,128]{1,0:T(4,128)S(1)}, u32[]{:S(2)}, u32[]{:S(2)}) collective-permute-start(f32[4,128]{1,0:T(4,128)S(1)} %get-tuple-element.53), channel_id=1, source_target_pairs={{0,1},{1,0},{2,3},{3,2},{4,5},{5,4},{6,7},{7,6},{8,9},{9,8},{10,11... | collective-permute-start | bytes 6152 | tf_op jit(solution)/shard_map/ppermute | solution.py:30

commit v4 on v3

--- a/solution.py
+++ b/solution.py
@@ -16,7 +16,7 @@
 W = R * CAP
 CH = 64
 NB = 8
-GROUP = 4
+GROUP = 8
 F32 = jnp.float32
 BF16 = jnp.bfloat16
 
@@ -58,29 +58,48 @@
     send_b_ref[...] = jnp.where(even, mine_ref[0:4, :], mine_ref[4:8, :])
 
 
-def finish_kernel(count_ref, mid_ref, got_a_ref, got_b_ref, own_ref, mine_ref, keep_ref, frac_ref, vel_ref, force_ref, energy_ref):
+def early_kernel(mine_ref, keep_ref, own_ref, occ_ref, speed_ref, gain_ref, frac_ref, energy_ref):
+    for r in range(R):
+        occupied = occ_ref[:, r * CAP:(r + 1) * CAP]
+        keep = keep_ref[r * 4:r * 4 + 4, :]
+        gain = occupied * (0.5 * TIME_STEP) / keep[3:4]
+        own = own_ref[r * 4:r * 4 + 4, :]
+        place = occupied * mine_ref[r * 4:r * 4 + 4, :]
+        speed_ref[r * 4:r * 4 + 4, :] = occupied * keep
+        gain_ref[r * 4:r * 4 + 4, :] = jnp.concatenate([gain, occupied, gain, occupied], axis=0)
+        for c in range(3):
+            frac_ref[c, r:r + 1, :] = place[c:c + 1]
+        energy_ref[r:r + 1, :] = own[3:4]
+
+
+def finish_kernel(mid_ref, got_a_ref, got_b_ref, own_ref, speed_ref, gain_ref, vel_ref, force_ref):
     even = lax.axis_index("gz") % 2 == 0
     got = (
         jnp.where(even, got_b_ref[...], got_a_ref[...]),
         jnp.where(even, got_a_ref[...], got_b_ref[...]),
     )
-    slot_number = lax.broadcasted_iota(jnp.int32, (1, CAP), 1)
-    for r in range(R):
-        occupied = jnp.where(slot_number < count_ref[r], 1.0, 0.0)
-        total = mid_ref[4 * (r + 1):4 * (r + 2), :] + own_ref[r * 4:r * 4 + 4, :] + got[r]
-        force = occupied * total
-        keep = keep_ref[r * 4:r * 4 + 4, :]
-        mine = mine_ref[r * 4:r * 4 + 4, :]
-        speed = occupied * (keep + 0.5 * TIME_STEP * force / keep[3:4])
-        place = occupied * mine
+    for r in range(R):
+        gain = gain_ref[r * 4:r * 4 + 1, :]
+        occupied = gain_ref[r * 4 + 1:r * 4 + 2, :]
+        force = mid_ref[4 * (r + 1):4 * (r + 2), :] + own_ref[r * 4:r * 4 + 4, :] + got[r]
+        speed = speed_ref[r * 4:r * 4 + 4, :] + gain * force
+        force = occupied * force
         for c in range(3):
             force_ref[c, r:r + 1, :] = force[c:c + 1]
             vel_ref[c, r:r + 1, :] = speed[c:c + 1]
-            frac_ref[c, r:r + 1, :] = place[c:c + 1]
-        energy_ref[r:r + 1, :] = own_ref[r * 4 + 3:r * 4 + 4, :]
-
-
-def prepare_kernel(codes_ref, emb_ref, w1_ref, w2_ref, wnt_ref, wc_ref, w2t_ref, wn_ref, embt_ref, off_ref, slot_ref, cell_ref, pick_ref):
+
+
+def prepare_kernel(
+    count_ref, codes_ref, emb_ref, w1_ref, w2_ref, wnt_ref, we_ref,
+    occ_ref, web_ref, w1c_ref, w2c_ref, wntc_ref, wc_ref, w2t_ref, wn_ref, embt_ref, off_ref, slot_ref, cell_ref, pick_ref,
+):
+    slot_number = lax.broadcasted_iota(jnp.int32, (1, CAP), 1)
+    for r in range(R):
+        occ_ref[:, r * CAP:(r + 1) * CAP] = jnp.where(slot_number < count_ref[r], 1.0, 0.0)
+    web_ref[...] = jnp.broadcast_to(we_ref[...], (CAP, CH)).T
+    w1c_ref[...] = w1_ref[...]
+    w2c_ref[...] = w2_ref[...]
+    wntc_ref[...] = wnt_ref[...]
     wc_ref[...] = jnp.zeros(wc_ref.shape, BF16)
     wc_ref[0:CH, 0:NB] = w1_ref[...].astype(F32).T.astype(BF16)
     emb = jnp.concatenate([emb_ref[...].astype(F32), jnp.zeros((6, CH), F32)], axis=0)
@@ -90,7 +109,7 @@
     w2t_ref[...] = w2_ref[...].astype(F32).T.astype(BF16)
     wn_ref[...] = wnt_ref[...].astype(F32).T.astype(BF16)
     row_cell = lax.broadcasted_iota(jnp.int32, (144, CAP), 0) // 4
-    slots = lax.broadcasted_iota(jnp.int32, (CAP, CAP), 0)
+    slots = lax.broadcasted_iota(jnp.int32, (CAP, CAP), 1).astype(F32)
     for r in range(R):
         code = codes_ref[pl.ds(r, K, stride=R), :]
         off = code // CAP
@@ -98,17 +117,17 @@
         off_ref[r] = off
         slot_ref[r] = slot
         cell = off // 3 * 4 + off % 3 + r
+        slot_rows = jnp.concatenate([slot.astype(F32), jnp.zeros((CAP - K, CAP), F32)], axis=0).T
         for k in range(K):
             lanes = slice(k * W + r * CAP, k * W + (r + 1) * CAP)
             cell_ref[:, lanes] = jnp.where(jnp.broadcast_to(cell[k:k + 1], (144, CAP)) == row_cell, 1.0, 0.0).astype(BF16)
-            pick_ref[:, lanes] = jnp.where(jnp.broadcast_to(slot[k:k + 1], (CAP, CAP)) == slots, 1.0, 0.0).astype(BF16)
+            pick_ref[lanes, :] = jnp.where(slot_rows[:, k:k + 1] == slots, 1.0, 0.0).astype(BF16)
 
 
 def edges_kernel(
-    count_ref, we_ref, w1_ref, w2_ref, wnt_ref,
-    plane_ref, got_a_ref, got_b_ref, wc_ref, w2t_ref, wn_ref, embt_ref, off_ref, slot_ref, cell_ref, pick_ref,
+    plane_ref, got_a_ref, got_b_ref, occ_ref, web_ref, w1_ref, w2_ref, wnt_ref, wc_ref, w2t_ref, wn_ref, embt_ref, off_ref, slot_ref, cell_ref, pick_ref,
     mid_ref, send_a_ref, send_b_ref, own_ref,
-    pos_s, d_s, kd_s, ey_s, exu_s, ds_s, feat_s, q_s, m_s, gr_s, t_s, ts_s, g_s, a_s,
+    pos_s, d_s, kd_s, ey_s, eyb_s, exu_s, ds_s, feat_s, q_s, qb_s, m_s, mb_s, gr_s, t_s, ts_s, g_s, a_s,
 ):
     even = lax.axis_index("gx") % 2 == 0
     pos_s[0:48] = jnp.where(even, got_b_ref[...], got_a_ref[...])
@@ -166,6 +185,7 @@
             )
             for m in range(9):
                 ey_s[m, pl.ds(at, 8), :] = terms[m]
+                eyb_s[m, k * 16:(k + 1) * 16, :] = jnp.concatenate([terms[m]] * 2, axis=0).astype(BF16)
             kind = wide(kd_s, k, 16)
             onehot = jnp.where(kind == kinds16, 1.0, 0.0)
             inputs.append(jnp.concatenate([ex, onehot], axis=0))
@@ -177,10 +197,12 @@
         sig = 0.5 * jnp.tanh(0.5 * pre) + 0.5
         hidden = (pre * sig).astype(BF16)
         ds_s[:, lanes] = sig * (1.0 + pre * (1.0 - sig))
-        feat_s[:, lanes] = feat
+        feat_s[:, lanes] = feat.astype(BF16)
         radial = jnp.dot(w2t_ref[...], hidden, preferred_element_type=F32)
         for deg in range(3):
-            q_s[deg * CH:(deg + 1) * CH, lanes] = radial[deg * CH:(deg + 1) * CH] * feat
+            carried = radial[deg * CH:(deg + 1) * CH] * feat
+            q_s[deg * CH:(deg + 1) * CH, lanes] = carried
+            qb_s[deg * CH:(deg + 1) * CH, lanes] = carried.astype(BF16)
         return 0
 
     for group in range(K // GROUP):
@@ -211,50 +233,45 @@
     own_feat = jnp.dot(
         embt_ref[...], jnp.where(own_kind == kinds16, 1.0, 0.0).astype(BF16), preferred_element_type=F32
     )
-    slot_number = lax.broadcasted_iota(jnp.int32, (1, CAP), 1)
-    occupied = jnp.concatenate(
-        [jnp.where(slot_number < count_ref[r], 1.0, 0.0) for r in range(R)], axis=1
-    )
+    occupied = occ_ref[...]
     vec = m_s[1] * m_s[1] + m_s[2] * m_s[2] + m_s[3] * m_s[3]
     ten = m_s[4] * m_s[4] + m_s[5] * m_s[5] + m_s[6] * m_s[6] + m_s[7] * m_s[7] + m_s[8] * m_s[8]
     invariant = jnp.concatenate([m_s[0], vec, ten, own_feat], axis=0).astype(BF16)
     pre = jnp.dot(wnt_ref[...], invariant, preferred_element_type=F32)
     sig = 0.5 * jnp.tanh(0.5 * pre) + 0.5
-    we = jnp.broadcast_to(we_ref[...], (8, CH)).T[:, 0:1]
+    we = jnp.concatenate([web_ref[...]] * R, axis=1)
     energy = jnp.sum(we * (pre * sig), axis=0, keepdims=True) * occupied
     gpre = we * occupied * (sig * (1.0 + pre * (1.0 - sig)))
     ginv = jnp.dot(wn_ref[0:3 * CH, :], gpre.astype(BF16), preferred_element_type=F32).astype(BF16).astype(F32)
-    m_s[0] = ginv[:CH]
+    mb_s[0] = ginv[:CH].astype(BF16)
     gvec = 2.0 * ginv[CH:2 * CH]
     gten = 2.0 * ginv[2 * CH:]
     for m in range(1, 9):
-        m_s[m] = m_s[m] * (gvec if m < 4 else gten)
+        mb_s[m] = (m_s[m] * (gvec if m < 4 else gten)).astype(BF16)
 
     def carried_back(k, _):
         at = k * 8
         for r in range(R):
             cols = slice(r * CAP, (r + 1) * CAP)
             lanes = pl.ds(k * W + r * CAP, CAP)
-            weight = []
-            for m in range(9):
-                w8 = ey_s[m, pl.ds(at, 8), cols]
-                weight.append(jnp.concatenate([w8, w8], axis=0))
+            weight = [eyb_s[m, k * 16:(k + 1) * 16, cols] for m in range(9)]
             sums = [None] * 9
             for cb in range(CH // 16):
                 feat = feat_s[cb * 16:(cb + 1) * 16, lanes]
-                q = [q_s[deg * CH + cb * 16:deg * CH + (cb + 1) * 16, lanes] for deg in range(3)]
+                q = [qb_s[deg * CH + cb * 16:deg * CH + (cb + 1) * 16, lanes] for deg in range(3)]
                 back = [None] * 3
                 for m in range(9):
                     deg = 0 if m == 0 else 1 if m < 4 else 2
-                    cot = m_s[m, cb * 16:(cb + 1) * 16, cols]
+                    cot = mb_s[m, cb * 16:(cb + 1) * 16, cols]
                     term = cot * q[deg]
                     sums[m] = term if sums[m] is None else sums[m] + term
                     term = cot * weight[m]
                     back[deg] = term if back[deg] is None else back[deg] + term
                 for deg in range(3):
-                    gr_s[deg * CH + cb * 16:deg * CH + (cb + 1) * 16, lanes] = (back[deg] * feat).astype(BF16)
+                    gr_s[deg * CH + cb * 16:deg * CH + (cb + 1) * 16, lanes] = back[deg] * feat
             for m in range(9):
-                t_s[r, m, pl.ds(at, 8), :] = sums[m][:8] + sums[m][8:]
+                both = sums[m].astype(F32)
+                t_s[r, m, pl.ds(at, 8), :] = both[:8] + both[8:]
         return 0
 
     for k in range(K):
@@ -316,24 +333,23 @@
             mixed = (-mixed).astype(BF16)
             for j in range(9):
                 a_s[j * 16:(j + 1) * 16, lanes] = cell_ref[j * 16:(j + 1) * 16, lanes] * mixed
-    out = lax.dot_general(a_s[...], pick_ref[...], (((1,), (1,)), ((), ())), preferred_element_type=F32)
+    out = jnp.dot(a_s[...], pick_ref[...], preferred_element_type=F32)
     mid_ref[...] = out[48:96]
-    send_a_ref[...] = jnp.where(even, out[96:144], out[0:48])
-    send_b_ref[...] = jnp.where(even, out[0:48], out[96:144])
+    send_a_ref[...] = jnp.where(even, out[96:144], out[0:48]).astype(BF16)
+    send_b_ref[...] = jnp.where(even, out[0:48], out[96:144]).astype(BF16)
 
 
 VMEM = pl.BlockSpec(memory_space=pltpu.VMEM)
 SMEM = pl.BlockSpec(memory_space=pltpu.SMEM)
 
 
-def call(kernel, name, args, outs, near, hbm_outs=False, smem=0, scratch=()):
-    shape = jax.ShapeDtypeStruct if hbm_outs else pltpu.VMEM
+def call(kernel, name, args, outs, near, far=0, smem=0, scratch=()):
     args = args[:near] + tuple(pltpu.with_memory_space_constraint(a, pltpu.VMEM) for a in args[near:])
     return pl.pallas_call(
         kernel,
         in_specs=[SMEM] * smem + [VMEM] * (len(args) - smem),
         out_specs=[VMEM] * len(outs),
-        out_shape=[shape(*out) for out in outs],
+        out_shape=[(pltpu.VMEM if i < len(outs) - far else jax.ShapeDtypeStruct)(*out) for i, out in enumerate(outs)],
         scratch_shapes=list(scratch),
         name=name,
     )(*args)
@@ -344,39 +360,47 @@
     return call(begin_kernel, "begin", (frac, velocity, force_old, species), outs, 4)
 
 
-def prepare(codes, embed, w1, w2, wnt):
+def prepare(count, codes, embed, w1, w2, wnt, we):
     outs = [
+        ((1, W), F32), ((CH, CAP), F32), ((NB, CH), BF16), ((CH, 3 * CH), BF16), ((CH, 4 * CH), BF16),
         ((2 * CH, NB + 16), BF16), ((3 * CH, CH), BF16), ((4 * CH, CH), BF16), ((CH, 16), BF16),
-        ((R, K, CAP), jnp.int32), ((R, K, CAP), jnp.int32), ((144, K * W), BF16), ((CAP, K * W), BF16),
+        ((R, K, CAP), jnp.int32), ((R, K, CAP), jnp.int32), ((144, K * W), BF16), ((K * W, CAP), BF16),
     ]
-    return call(prepare_kernel, "prepare", (codes, embed, w1, w2, wnt), outs, 5)
-
-
-def edges(count, we, plane, got_a, got_b, w1, w2, wnt, prepared):
+    return call(prepare_kernel, "prepare", (count, codes, embed, w1, w2, wnt, we), outs, 7, smem=1)
+
+
+def edges(plane, got_a, got_b, prepared):
     scratch = [
         pltpu.VMEM((144, CAP), F32),
         pltpu.VMEM((R, 3 * K, CAP), F32),
         pltpu.VMEM((R, K, CAP), F32),
         pltpu.VMEM((9, 8 * K, W), F32),
+        pltpu.VMEM((9, 16 * K, W), BF16),
         pltpu.VMEM((8 * K, W), F32),
         pltpu.VMEM((CH, K * W), F32),
-        pltpu.VMEM((CH, K * W), F32),
+        pltpu.VMEM((CH, K * W), BF16),
         pltpu.VMEM((3 * CH, K * W), F32),
+        pltpu.VMEM((3 * CH, K * W), BF16),
         pltpu.VMEM((9, CH, W), F32),
+        pltpu.VMEM((9, CH, W), BF16),
         pltpu.VMEM((3 * CH, K * W), BF16),
         pltpu.VMEM((R, 9, 8 * K, CAP), F32),
         pltpu.VMEM((R, 8 * K, CAP), F32),
         pltpu.VMEM((R, 3 * K, CAP), F32),
         pltpu.VMEM((144, K * W), BF16),
     ]
-    outs = [((48, CAP), F32), ((48, CAP), F32), ((48, CAP), F32), ((8, CAP), F32)]
-    args = (count, we, w1, w2, wnt, plane, got_a, got_b, *prepared)
-    return call(edges_kernel, "edges", args, outs, 5, smem=1, scratch=scratch)
-
-
-def finish(count, column, got_a, got_b, own, mine, keep):
-    outs = [((3, R, CAP), F32)] * 3 + [((R, CAP), F32)]
-    return call(finish_kernel, "finish", (count, column, got_a, got_b, own, mine, keep), outs, 1, hbm_outs=True, smem=1)
+    outs = [((48, CAP), F32), ((48, CAP), BF16), ((48, CAP), BF16), ((8, CAP), F32)]
+    return call(edges_kernel, "edges", (plane, got_a, got_b, *prepared), outs, 0, scratch=scratch)
+
+
+def early(mine, keep, own, prepared):
+    outs = [((4 * R, CAP), F32), ((4 * R, CAP), F32), ((3, R, CAP), F32), ((R, CAP), F32)]
+    return call(early_kernel, "early", (mine, keep, own, prepared[0]), outs, 0, far=2)
+
+
+def finish(column, got_a, got_b, own, speed, gain):
+    outs = [((3, R, CAP), F32)] * 2
+    return call(finish_kernel, "finish", (column, got_a, got_b, own, speed, gain), outs, 0, far=2)
 
 
 def shards(
@@ -390,7 +414,9 @@
     send_a, send_b, mine, keep = begin(
         frac.reshape(vectors), velocity.reshape(vectors), force_old.reshape(vectors), species.reshape(R, CAP)
     )
-    prepared = prepare(neighbours.reshape(K * R, CAP), embed, w_radial_in, w_radial_out, wnt)
+    prepared = prepare(
+        count, neighbours.reshape(K * R, CAP), embed, w_radial_in, w_radial_out, wnt, w_energy.reshape(1, CH)
+    )
 
     got_a, got_b = swap(send_a, "gz", False), swap(send_b, "gz", True)
     column = jnp.concatenate(
@@ -402,17 +428,16 @@
     )
     got_a, got_b = swap(plane, "gx", False), swap(plane, "gx", True)
 
-    plane, send_a, send_b, own = edges(
-        count, w_energy.reshape(1, CH), plane, got_a, got_b, w_radial_in, w_radial_out, wnt, prepared
-    )
-    plane = plane + swap(send_a, "gx", False) + swap(send_b, "gx", True)
+    plane, send_a, send_b, own = edges(plane, got_a, got_b, prepared)
+    speed, gain, next_frac, energy = early(mine, keep, own, prepared)
+    plane = plane + swap(send_a, "gx", False).astype(F32) + swap(send_b, "gx", True).astype(F32)
     lower, column, upper = plane[0:16], plane[16:32], plane[32:48]
     send_a, send_b = jnp.where(even_y, upper, lower), jnp.where(even_y, lower, upper)
     column = column + swap(send_a, "gy", False) + swap(send_b, "gy", True)
     send_a = jnp.where(even_z, column[12:16], column[0:4])
     send_b = jnp.where(even_z, column[0:4], column[12:16])
     got_a, got_b = swap(send_a, "gz", False), swap(send_b, "gz", True)
-    next_frac, next_velocity, next_force, energy = finish(count, column, got_a, got_b, own, mine, keep)
+    next_velocity, next_force = finish(column, got_a, got_b, own, speed, gain)
     return (
         next_frac.reshape(frac.shape),
         next_velocity.reshape(frac.shape),

time: 45 us -> 42.2 us (0.938)
  Pallas kernels: 10.9 us -> 9.19 us
  waiting for transfers between devices: 17 us -> 16 us
    pallas_call x4 -> x5, Pallas kernels: 10.9 us -> 9.19 us  [call(): pl.pallas_call(kernel, in_specs=[SMEM] * smem + [VMEM] * (len(args) - sme...]
    ppermute x12, waiting for transfers between devices: 17 us -> 16 us  [swap(): return lax.ppermute(array, axis, pairs)]
  transfers between devices with their start and end apart: 12 -> 12, of which waited for: 10 -> 9; matrix products, arithmetic and copies ran while one was open for 0% -> 0% of each run, Pallas kernels for 4% -> 6%
where the time goes in v4:
time: 42.2 us; the launch traced here: 42 us
  starting transfers between devices  16 us (38%)
  waiting for transfers between devices  16 us (38%)
  Pallas kernels  9.19 us (22%)
  between operations  0.69 us (2%)
    ppermute x12, waiting for transfers between devices, swap(): return lax.ppermute(array, axis, pairs)  16 us
    ppermute x12, starting transfers between devices, swap(): return lax.ppermute(array, axis, pairs)  16 us
    pallas_call x5, Pallas kernels, call(): pl.pallas_call(kernel, in_specs=[SMEM] * smem + [VMEM] * (len(args) - sme...  9.19 us
  transfers between devices with their start and end apart: 12, of which 9 were waited for; matrix products, arithmetic and copies ran while one was open for 0% of the time, Pallas kernels for 6%

profile of v4, /device:TPU:6, one launch (start us, length us, event | category | flops | bytes accessed | tf_op | source)
XLA Modules:
  0.0 42.0 jit_solution(11082366648055898234)
XLA Ops:
  0.6 0.8 %begin.1 = (f32[4,128]{1,0:T(4,128)S(1)}, f32[4,128]{1,0:T(4,128)S(1)}, f32[8,128]{1,0:T(8,128)S(1)}, f32[8,128]{1,0:T(8,128)S(1)}) custom-call(f32[3,2,128]{2,1,0:T(2,128)} %bitcast.20, f32[3,2,128]{2,1,0:T(2,128)} %bitcast.21, f32[3,2,128]{2,1,0:T(2,128)} %bitcast.22, s32[2,128]{1,0:T(2,128)} %bitcast.23), custom_call_target="tpu_custom_call" | custom-call | tf_op jit(solution)/shard_map/begin/pallas_call | solution.py:348
  1.4 2.3 %collective-permute-start = (f32[4,128]{1,0:T(4,128)S(1)}, f32[4,128]{1,0:T(4,128)S(1)}, u32[]{:S(2)}, u32[]{:S(2)}) collective-permute-start(f32[4,128]{1,0:T(4,128)S(1)} %get-tuple-element.33), channel_id=1, source_target_pairs={{0,3},{1,2},{2,1},{3,0},{4,7},{5,6},{6,5},{7,4},{8,11},{9,10},{10,... | collective-permute-start | bytes 6152 | tf_op jit(solution)/shard_map/ppermute | solution.py:30
  3.7 2.6 %collective-permute-done = f32[4,128]{1,0:T(4,128)S(1)} collective-permute-done((f32[4,128]{1,0:T(4,128)S(1)}, f32[4,128]{1,0:T(4,128)S(1)}, u32[]{:S(2)}, u32[]{:S(2)}) %collective-permute-start) | collective-permute-done | bytes 2080 | tf_op jit(solution)/shard_map/ppermute | solution.py:30
  6.3 1.0 %collective-permute-done.1 = f32[4,128]{1,0:T(4,128)S(1)} collective-permute-done((f32[4,128]{1,0:T(4,128)S(1)}, f32[4,128]{1,0:T(4,128)S(1)}, u32[]{:S(2)}, u32[]{:S(2)}) %collective-permute-start.1) | collective-permute-done | bytes 2080 | tf_op jit(solution)/shard_map/ppermute | solution.py:30
  7.4 5.0 %collective-permute-start.2 = (f32[16,128]{1,0:T(8,128)S(1)}, f32[16,128]{1,0:T(8,128)S(1)}, u32[]{:S(2)}, u32[]{:S(2)}) collective-permute-start(f32[16,128]{1,0:T(8,128)S(1)} %pad_maximum_fusion), channel_id=1, source_target_pairs={{0,60},{4,8},{8,4},{12,16},{16,12},{20,24},{24,20},{28,32},{32,28}... | collective-permute-start | bytes 24584 | tf_op jit(solution)/shard_map/ppermute | solution.py:30
  12.3 1.4 %collective-permute-done.2 = f32[16,128]{1,0:T(8,128)S(1)} collective-permute-done((f32[16,128]{1,0:T(8,128)S(1)}, f32[16,128]{1,0:T(8,128)S(1)}, u32[]{:S(2)}, u32[]{:S(2)}) %collective-permute-start.2) | collective-permute-done | bytes 8224 | tf_op jit(solution)/shard_map/ppermute | solution.py:30
  13.7 0.1 concatenate.8.plane_ref
  13.8 3.1 %collective-permute-start.5 = (f32[48,128]{1,0:T(8,128)S(1)}, f32[48,128]{1,0:T(8,128)S(1)}, u32[]{:S(2)}, u32[]{:S(2)}) collective-permute-start(f32[48,128]{1,0:T(8,128)S(1)} %concatenate.8.plane_ref), channel_id=1, source_target_pairs={{0,192},{64,128},{128,64},{192,0},{1,193},{65,129},{129,65},{193,1... | collective-permute-start | bytes 73736 | tf_op jit(solution)/shard_map/ppermute | solution.py:30
  16.9 0.1 collective-permute-start.4
  17.1 1.9 %prepare.1 = (f32[1,256]{1,0:T(1,128)S(1)}, f32[64,128]{1,0:T(8,128)S(1)}, bf16[8,64]{1,0:T(8,128)(2,1)S(1)}, bf16[64,192]{1,0:T(8,128)(2,1)S(1)}, bf16[64,256]{...) custom-call(s32[2]{0:T(128)} %bitcast.24, ...), custom_call_target="tpu_custom_call" | custom-call | tf_op jit(solution)/shard_map/prepare/pallas_call | solution.py:348
  19.0 1.8 %collective-permute-done.4.got_a_ref = f32[48,128]{1,0:T(8,128)S(1)} collective-permute-done((f32[48,128]{1,0:T(8,128)S(1)}, f32[48,128]{1,0:T(8,128)S(1)}, u32[]{:S(2)}, u32[]{:S(2)}) %collective-permute-start.4) | collective-permute-done | bytes 24608 | tf_op jit(solution)/shard_map/ppermute | solution.py:30
  20.7 5.3 %edges.1 = (f32[48,128]{1,0:T(8,128)S(1)}, bf16[48,128]{1,0:T(8,128)(2,1)S(1)}, bf16[48,128]{1,0:T(8,128)(2,1)S(1)}, f32[8,128]{1,0:T(8,128)S(1)}) custom-call(f32[48,128]{1,0:T(8,128)S(1)} %concatenate.8.plane_ref, f32[48,128]{1,0:T(8,128)S(1)} %collective-permute-done.4.got_a_ref, f32[48,128]{1,0:T(8,128)S(1)} %collective-permute-done.5.got_b_ref, ...), custom_call_target="tpu_custom_call" | custom-call | tf_op jit(solution)/shard_map/edges/pallas_call | solution.py:348
  26.1 0.2 collective-permute-start.6
  26.3 1.2 %collective-permute-start.7 = (bf16[48,128]{1,0:T(8,128)(2,1)S(1)}, bf16[48,128]{1,0:T(8,128)(2,1)S(1)}, u32[]{:S(2)}, u32[]{:S(2)}) collective-permute-start(bf16[48,128]{1,0:T(8,128)(2,1)S(1)} %get-tuple-element.52), channel_id=1, source_target_pairs={{0,192},{64,128},{128,64},{192,0},{1,193},{65,129},{129,65},{193,1... | collective-permute-start | bytes 36872 | tf_op jit(solution)/shard_map/ppermute | solution.py:30
  27.5 2.4 %collective-permute-done.6 = bf16[48,128]{1,0:T(8,128)(2,1)S(1)} collective-permute-done((bf16[48,128]{1,0:T(8,128)(2,1)S(1)}, bf16[48,128]{1,0:T(8,128)(2,1)S(1)}, u32[]{:S(2)}, u32[]{:S(2)}) %collective-permute-start.6) | collective-permute-done | bytes 12320 | tf_op jit(solution)/shard_map/ppermute | solution.py:30
  29.9 1.4 %collective-permute-done.7 = bf16[48,128]{1,0:T(8,128)(2,1)S(1)} collective-permute-done((bf16[48,128]{1,0:T(8,128)(2,1)S(1)}, bf16[48,128]{1,0:T(8,128)(2,1)S(1)}, u32[]{:S(2)}, u32[]{:S(2)}) %collective-permute-start.7) | collective-permute-done | bytes 12320 | tf_op jit(solution)/shard_map/ppermute | solution.py:30
  31.3 0.1 collective-permute-start.8
  31.4 1.8 %collective-permute-start.9 = (f32[16,128]{1,0:T(8,128)S(1)}, f32[16,128]{1,0:T(8,128)S(1)}, u32[]{:S(2)}, u32[]{:S(2)}) collective-permute-start(f32[16,128]{1,0:T(8,128)S(1)} %get-tuple-element.63), channel_id=1, source_target_pairs={{0,60},{4,8},{8,4},{12,16},{16,12},{20,24},{24,20},{28,32},{32,28}... | collective-permute-start | bytes 24584 | tf_op jit(solution)/shard_map/ppermute | solution.py:30
  33.2 2.6 %collective-permute-done.9 = f32[16,128]{1,0:T(8,128)S(1)} collective-permute-done((f32[16,128]{1,0:T(8,128)S(1)}, f32[16,128]{1,0:T(8,128)S(1)}, u32[]{:S(2)}, u32[]{:S(2)}) %collective-permute-start.9) | collective-permute-done | bytes 8224 | tf_op jit(solution)/shard_map/ppermute | solution.py:30
  35.8 2.1 %collective-permute-start.11 = (f32[4,128]{1,0:T(4,128)S(1)}, f32[4,128]{1,0:T(4,128)S(1)}, u32[]{:S(2)}, u32[]{:S(2)}) collective-permute-start(f32[4,128]{1,0:T(4,128)S(1)} %get-tuple-element.66), channel_id=1, source_target_pairs={{0,3},{1,2},{2,1},{3,0},{4,7},{5,6},{6,5},{7,4},{8,11},{9,10},{10,... | collective-permute-start | bytes 6152 | tf_op jit(solution)/shard_map/ppermute | solution.py:30
  37.9 0.6 %early.1 = (f32[8,128]{1,0:T(8,128)S(1)}, f32[8,128]{1,0:T(8,128)S(1)}, f32[3,2,128]{2,1,0:T(2,128)}, f32[2,128]{1,0:T(2,128)}) custom-call(f32[8,128]{1,0:T(8,128)S(1)} %get-tuple-element.31.mine_ref, f32[8,128]{1,0:T(8,128)S(1)} %get-tuple-element.32.keep_ref, f32[8,128]{1,0:T(8,128)S(1)} %get-tuple-element.48.own_ref, f32[1,256]{1,0:T(1,128)S(1)} %get-tuple-element.35.occ_ref), custom_call_target="tpu_custom_call" | custom-call | tf_op jit(solution)/shard_map/early/pallas_call | solution.py:348
  38.4 2.2 %collective-permute-done.11.got_b_ref = f32[4,128]{1,0:T(4,128)S(1)} collective-permute-done((f32[4,128]{1,0:T(4,128)S(1)}, f32[4,128]{1,0:T(4,128)S(1)}, u32[]{:S(2)}, u32[]{:S(2)}) %collective-permute-start.11) | collective-permute-done | bytes 2080 | tf_op jit(solution)/shard_map/ppermute | solution.py:30
  40.6 0.8 %collective-permute-done.10.got_a_ref = f32[4,128]{1,0:T(4,128)S(1)} collective-permute-done((f32[4,128]{1,0:T(4,128)S(1)}, f32[4,128]{1,0:T(4,128)S(1)}, u32[]{:S(2)}, u32[]{:S(2)}) %collective-permute-start.10) | collective-permute-done | bytes 2080 | tf_op jit(solution)/shard_map/ppermute | solution.py:30
  41.4 0.6 %finish.1 = (f32[3,2,128]{2,1,0:T(2,128)}, f32[3,2,128]{2,1,0:T(2,128)}) custom-call(f32[16,128]{1,0:T(8,128)S(1)} %fusion.mid_ref, f32[4,128]{1,0:T(4,128)S(1)} %collective-permute-done.10.got_a_ref, f32[4,128]{1,0:T(4,128)S(1)} %collective-permute-done.11.got_b_ref, f32[8,128]{1,0:T(8,128)S(1)} %get-tuple-element.48.own_ref, ...), custom_call_target="tpu_custom_call" | custom-call | tf_op jit(solution)/shard_map/finish/pallas_call | solution.py:348
  (13 shorter events, 0.1 us)
Async XLA Ops:
  1.4 4.9 %collective-permute-start = (f32[4,128]{1,0:T(4,128)S(1)}, f32[4,128]{1,0:T(4,128)S(1)}, u32[]{:S(2)}, u32[]{:S(2)}) collective-permute-start(f32[4,128]{1,0:T(4,128)S(1)} %get-tuple-element.33), channel_id=1, source_target_pairs={{0,3},{1,2},{2,1},{3,0},{4,7},{5,6},{6,5},{7,4},{8,11},{9,10},{10,... | collective-permute-start | bytes 6152 | tf_op jit(solution)/shard_map/ppermute | solution.py:30
  3.7 3.6 %collective-permute-start.1 = (f32[4,128]{1,0:T(4,128)S(1)}, f32[4,128]{1,0:T(4,128)S(1)}, u32[]{:S(2)}, u32[]{:S(2)}) collective-permute-start(f32[4,128]{1,0:T(4,128)S(1)} %get-tuple-element.34), channel_id=1, source_target_pairs={{0,1},{1,0},{2,3},{3,2},{4,5},{5,4},{6,7},{7,6},{8,9},{9,8},{10,11... | collective-permute-start | bytes 6152 | tf_op jit(solution)/shard_map/ppermute | solution.py:30
  7.3 5.1 %collective-permute-start.3 = (f32[16,128]{1,0:T(8,128)S(1)}, f32[16,128]{1,0:T(8,128)S(1)}, u32[]{:S(2)}, u32[]{:S(2)}) collective-permute-start(f32[16,128]{1,0:T(8,128)S(1)} %pad_maximum_fusion), channel_id=1, source_target_pairs={{0,4},{4,0},{8,12},{12,8},{16,20},{20,16},{24,28},{28,24},{32,36},... | collective-permute-start | bytes 24584 | tf_op jit(solution)/shard_map/ppermute | solution.py:30
  7.4 6.3 %collective-permute-start.2 = (f32[16,128]{1,0:T(8,128)S(1)}, f32[16,128]{1,0:T(8,128)S(1)}, u32[]{:S(2)}, u32[]{:S(2)}) collective-permute-start(f32[16,128]{1,0:T(8,128)S(1)} %pad_maximum_fusion), channel_id=1, source_target_pairs={{0,60},{4,8},{8,4},{12,16},{16,12},{20,24},{24,20},{28,32},{32,28}... | collective-permute-start | bytes 24584 | tf_op jit(solution)/shard_map/ppermute | solution.py:30
  13.8 5.2 %collective-permute-start.5 = (f32[48,128]{1,0:T(8,128)S(1)}, f32[48,128]{1,0:T(8,128)S(1)}, u32[]{:S(2)}, u32[]{:S(2)}) collective-permute-start(f32[48,128]{1,0:T(8,128)S(1)} %concatenate.8.plane_ref), channel_id=1, source_target_pairs={{0,192},{64,128},{128,64},{192,0},{1,193},{65,129},{129,65},{193,1... | collective-permute-start | bytes 73736 | tf_op jit(solution)/shard_map/ppermute | solution.py:30
  16.9 3.8 %collective-permute-start.4 = (f32[48,128]{1,0:T(8,128)S(1)}, f32[48,128]{1,0:T(8,128)S(1)}, u32[]{:S(2)}, u32[]{:S(2)}) collective-permute-start(f32[48,128]{1,0:T(8,128)S(1)} %concatenate.8.plane_ref), channel_id=1, source_target_pairs={{0,64},{64,0},{128,192},{192,128},{1,65},{65,1},{129,193},{193,129... | collective-permute-start | bytes 73736 | tf_op jit(solution)/shard_map/ppermute | solution.py:30
  26.1 3.8 %collective-permute-start.6 = (bf16[48,128]{1,0:T(8,128)(2,1)S(1)}, bf16[48,128]{1,0:T(8,128)(2,1)S(1)}, u32[]{:S(2)}, u32[]{:S(2)}) collective-permute-start(bf16[48,128]{1,0:T(8,128)(2,1)S(1)} %get-tuple-element.51), channel_id=1, source_target_pairs={{0,64},{64,0},{128,192},{192,128},{1,65},{65,1},{129,193},{193,129... | collective-permute-start | bytes 36872 | tf_op jit(solution)/shard_map/ppermute | solution.py:30
  26.3 4.9 %collective-permute-start.7 = (bf16[48,128]{1,0:T(8,128)(2,1)S(1)}, bf16[48,128]{1,0:T(8,128)(2,1)S(1)}, u32[]{:S(2)}, u32[]{:S(2)}) collective-permute-start(bf16[48,128]{1,0:T(8,128)(2,1)S(1)} %get-tuple-element.52), channel_id=1, source_target_pairs={{0,192},{64,128},{128,64},{192,0},{1,193},{65,129},{129,65},{193,1... | collective-permute-start | bytes 36872 | tf_op jit(solution)/shard_map/ppermute | solution.py:30
  31.3 1.9 %collective-permute-start.8 = (f32[16,128]{1,0:T(8,128)S(1)}, f32[16,128]{1,0:T(8,128)S(1)}, u32[]{:S(2)}, u32[]{:S(2)}) collective-permute-start(f32[16,128]{1,0:T(8,128)S(1)} %get-tuple-element.62), channel_id=1, source_target_pairs={{0,4},{4,0},{8,12},{12,8},{16,20},{20,16},{24,28},{28,24},{32,36},... | collective-permute-start | bytes 24584 | tf_op jit(solution)/shard_map/ppermute | solution.py:30
  31.4 4.4 %collective-permute-start.9 = (f32[16,128]{1,0:T(8,128)S(1)}, f32[16,128]{1,0:T(8,128)S(1)}, u32[]{:S(2)}, u32[]{:S(2)}) collective-permute-start(f32[16,128]{1,0:T(8,128)S(1)} %get-tuple-element.63), channel_id=1, source_target_pairs={{0,60},{4,8},{8,4},{12,16},{16,12},{20,24},{24,20},{28,32},{32,28}... | collective-permute-start | bytes 24584 | tf_op jit(solution)/shard_map/ppermute | solution.py:30
  35.8 4.9 %collective-permute-start.11 = (f32[4,128]{1,0:T(4,128)S(1)}, f32[4,128]{1,0:T(4,128)S(1)}, u32[]{:S(2)}, u32[]{:S(2)}) collective-permute-start(f32[4,128]{1,0:T(4,128)S(1)} %get-tuple-element.66), channel_id=1, source_target_pairs={{0,3},{1,2},{2,1},{3,0},{4,7},{5,6},{6,5},{7,4},{8,11},{9,10},{10,... | collective-permute-start | bytes 6152 | tf_op jit(solution)/shard_map/ppermute | solution.py:30
  37.9 3.6 %collective-permute-start.10 = (f32[4,128]{1,0:T(4,128)S(1)}, f32[4,128]{1,0:T(4,128)S(1)}, u32[]{:S(2)}, u32[]{:S(2)}) collective-permute-start(f32[4,128]{1,0:T(4,128)S(1)} %get-tuple-element.67), channel_id=1, source_target_pairs={{0,1},{1,0},{2,3},{3,2},{4,5},{5,4},{6,7},{7,6},{8,9},{9,8},{10,11... | collective-permute-start | bytes 6152 | tf_op jit(solution)/shard_map/ppermute | solution.py:30

commit v5 on v4

--- a/solution.py
+++ b/solution.py
@@ -17,6 +17,7 @@
 CH = 64
 NB = 8
 GROUP = 8
+EDGES_LIMIT = 40 << 20
 F32 = jnp.float32
 BF16 = jnp.bfloat16
 
@@ -116,7 +117,7 @@
         slot = code % CAP
         off_ref[r] = off
         slot_ref[r] = slot
-        cell = off // 3 * 4 + off % 3 + r
+        cell = (off // 3 % 3 * 3 + off // 9) * 4 + off % 3 + r
         slot_rows = jnp.concatenate([slot.astype(F32), jnp.zeros((CAP - K, CAP), F32)], axis=0).T
         for k in range(K):
             lanes = slice(k * W + r * CAP, k * W + (r + 1) * CAP)
@@ -126,10 +127,10 @@
 
 def edges_kernel(
     plane_ref, got_a_ref, got_b_ref, occ_ref, web_ref, w1_ref, w2_ref, wnt_ref, wc_ref, w2t_ref, wn_ref, embt_ref, off_ref, slot_ref, cell_ref, pick_ref,
-    mid_ref, send_a_ref, send_b_ref, own_ref,
-    pos_s, d_s, kd_s, ey_s, eyb_s, exu_s, ds_s, feat_s, q_s, qb_s, m_s, mb_s, gr_s, t_s, ts_s, g_s, a_s,
+    send_a_ref, send_b_ref, g_s, energy_ref,
+    pos_s, d_s, kd_s, ey_s, eyb_s, exu_s, ds_s, feat_s, q_s, qb_s, m_s, mb_s, gr_s, t_s, ts_s, a_s,
 ):
-    even = lax.axis_index("gx") % 2 == 0
+    even = lax.axis_index("gy") % 2 == 0
     pos_s[0:48] = jnp.where(even, got_b_ref[...], got_a_ref[...])
     pos_s[48:96] = plane_ref[...]
     pos_s[96:144] = jnp.where(even, got_a_ref[...], got_b_ref[...])
@@ -138,8 +139,9 @@
     offs = [[off_ref[r, h * 8:(h + 1) * 8, :] for h in range(2)] for r in range(R)]
     slots = [[slot_ref[r, h * 8:(h + 1) * 8, :] for h in range(2)] for r in range(R)]
     for col in range(9):
+        place = col % 3 * 3 + col // 3
         for zz in range(4):
-            rows = [rows8(pos_s[col * 16 + zz * 4 + q:col * 16 + zz * 4 + q + 1, :], CAP) for q in range(4)]
+            rows = [rows8(pos_s[place * 16 + zz * 4 + q:place * 16 + zz * 4 + q + 1, :], CAP) for q in range(4)]
             for r in range(R):
                 dz = zz - r
                 if not 0 <= dz <= 2:
@@ -320,30 +322,41 @@
         gz = e[3] + SQRT3 * (y * e[5] + x * e[6]) + z * (2.0 * e[8] + gs2)
         for c, g in enumerate((gx, gy, gz)):
             g_s[r, c * K:(c + 1) * K, :] = g
-            own_ref[r * 4 + c:r * 4 + c + 1, :] = jnp.sum(g, axis=0, keepdims=True)
-        own_ref[r * 4 + 3:r * 4 + 4, :] = energy[:, cols]
-
-    sub = lax.broadcasted_iota(jnp.int32, (16, CAP), 0)
-    comp = sub % 4
+    energy_ref[...] = energy
+
+    scatter_inputs(g_s, cell_ref, a_s, ((0, 0), (96, 48)))
+    out = jnp.dot(a_s[...], pick_ref[...], preferred_element_type=F32)
+    send_a_ref[...] = jnp.where(even, out[48:96], out[0:48]).astype(BF16)
+    send_b_ref[...] = jnp.where(even, out[0:48], out[48:96]).astype(BF16)
+
+
+def scatter_inputs(g_ref, cell_ref, a_ref, blocks):
+    comp = lax.broadcasted_iota(jnp.int32, (16, CAP), 0) % 4
     for k in range(K):
         for r in range(R):
             lanes = slice(k * W + r * CAP, k * W + (r + 1) * CAP)
-            gx, gy, gz = (jnp.broadcast_to(g_s[r, c * K + k:c * K + k + 1, :], (16, CAP)) for c in range(3))
+            gx, gy, gz = (jnp.broadcast_to(g_ref[r, c * K + k:c * K + k + 1, :], (16, CAP)) for c in range(3))
             mixed = jnp.where(comp == 0, gx, jnp.where(comp == 1, gy, jnp.where(comp == 2, gz, 0.0)))
             mixed = (-mixed).astype(BF16)
-            for j in range(9):
-                a_s[j * 16:(j + 1) * 16, lanes] = cell_ref[j * 16:(j + 1) * 16, lanes] * mixed
-    out = jnp.dot(a_s[...], pick_ref[...], preferred_element_type=F32)
-    mid_ref[...] = out[48:96]
-    send_a_ref[...] = jnp.where(even, out[96:144], out[0:48]).astype(BF16)
-    send_b_ref[...] = jnp.where(even, out[0:48], out[96:144]).astype(BF16)
+            for take, put in blocks:
+                for j in range(0, 48, 16):
+                    a_ref[put + j:put + j + 16, lanes] = cell_ref[take + j:take + j + 16, lanes] * mixed
+
+
+def near_kernel(g_ref, energy_ref, cell_ref, pick_ref, mid_ref, own_ref, a_s):
+    scatter_inputs(g_ref, cell_ref, a_s, ((48, 0),))
+    mid_ref[...] = jnp.dot(a_s[...], pick_ref[...], preferred_element_type=F32)
+    for r in range(R):
+        for c in range(3):
+            own_ref[r * 4 + c:r * 4 + c + 1, :] = jnp.sum(g_ref[r, c * K:(c + 1) * K, :], axis=0, keepdims=True)
+        own_ref[r * 4 + 3:r * 4 + 4, :] = energy_ref[:, r * CAP:(r + 1) * CAP]
 
 
 VMEM = pl.BlockSpec(memory_space=pltpu.VMEM)
 SMEM = pl.BlockSpec(memory_space=pltpu.SMEM)
 
 
-def call(kernel, name, args, outs, near, far=0, smem=0, scratch=()):
+def call(kernel, name, args, outs, near, far=0, smem=0, scratch=(), limit=None):
     args = args[:near] + tuple(pltpu.with_memory_space_constraint(a, pltpu.VMEM) for a in args[near:])
     return pl.pallas_call(
         kernel,
@@ -351,6 +364,7 @@
         out_specs=[VMEM] * len(outs),
         out_shape=[(pltpu.VMEM if i < len(outs) - far else jax.ShapeDtypeStruct)(*out) for i, out in enumerate(outs)],
         scratch_shapes=list(scratch),
+        compiler_params=pltpu.CompilerParams(vmem_limit_bytes=limit),
         name=name,
     )(*args)
 
@@ -386,11 +400,16 @@
         pltpu.VMEM((3 * CH, K * W), BF16),
         pltpu.VMEM((R, 9, 8 * K, CAP), F32),
         pltpu.VMEM((R, 8 * K, CAP), F32),
-        pltpu.VMEM((R, 3 * K, CAP), F32),
-        pltpu.VMEM((144, K * W), BF16),
+        pltpu.VMEM((96, K * W), BF16),
     ]
-    outs = [((48, CAP), F32), ((48, CAP), BF16), ((48, CAP), BF16), ((8, CAP), F32)]
-    return call(edges_kernel, "edges", (plane, got_a, got_b, *prepared), outs, 0, scratch=scratch)
+    outs = [((48, CAP), BF16), ((48, CAP), BF16), ((R, 3 * K, CAP), F32), ((1, W), F32)]
+    return call(edges_kernel, "edges", (plane, got_a, got_b, *prepared), outs, 0, scratch=scratch, limit=EDGES_LIMIT)
+
+
+def near(gradient, energy, prepared):
+    outs = [((48, CAP), F32), ((4 * R, CAP), F32)]
+    scratch = [pltpu.VMEM((48, K * W), BF16)]
+    return call(near_kernel, "near", (gradient, energy, *prepared[-2:]), outs, 0, scratch=scratch, limit=EDGES_LIMIT)
 
 
 def early(mine, keep, own, prepared):
@@ -406,7 +425,7 @@
 def shards(
     frac, velocity, force_old, species, cell_count, neighbours, embed, w_radial_in, w_radial_out, w_node, w_energy
 ):
-    even_y = lax.axis_index("gy") % 2 == 0
+    even_x = lax.axis_index("gx") % 2 == 0
     even_z = lax.axis_index("gz") % 2 == 0
     vectors = (3, R, CAP)
     count = cell_count.reshape(R)
@@ -422,18 +441,19 @@
     column = jnp.concatenate(
         [jnp.where(even_z, got_b, got_a), mine, jnp.where(even_z, got_a, got_b)], axis=0
     )
-    got_a, got_b = swap(column, "gy", False), swap(column, "gy", True)
+    got_a, got_b = swap(column, "gx", False), swap(column, "gx", True)
     plane = jnp.concatenate(
-        [jnp.where(even_y, got_b, got_a), column, jnp.where(even_y, got_a, got_b)], axis=0
-    )
-    got_a, got_b = swap(plane, "gx", False), swap(plane, "gx", True)
-
-    plane, send_a, send_b, own = edges(plane, got_a, got_b, prepared)
+        [jnp.where(even_x, got_b, got_a), column, jnp.where(even_x, got_a, got_b)], axis=0
+    )
+    got_a, got_b = swap(plane, "gy", False), swap(plane, "gy", True)
+
+    send_a, send_b, gradient, energy = edges(plane, got_a, got_b, prepared)
+    plane, own = near(gradient, energy, prepared)
     speed, gain, next_frac, energy = early(mine, keep, own, prepared)
-    plane = plane + swap(send_a, "gx", False).astype(F32) + swap(send_b, "gx", True).astype(F32)
+    plane = plane + swap(send_a, "gy", False).astype(F32) + swap(send_b, "gy", True).astype(F32)
     lower, column, upper = plane[0:16], plane[16:32], plane[32:48]
-    send_a, send_b = jnp.where(even_y, upper, lower), jnp.where(even_y, lower, upper)
-    column = column + swap(send_a, "gy", False) + swap(send_b, "gy", True)
+    send_a, send_b = jnp.where(even_x, upper, lower), jnp.where(even_x, lower, upper)
+    column = column + swap(send_a, "gx", False) + swap(send_b, "gx", True)
     send_a = jnp.where(even_z, column[12:16], column[0:4])
     send_b = jnp.where(even_z, column[0:4], column[12:16])
     got_a, got_b = swap(send_a, "gz", False), swap(send_b, "gz", True)

time: 42.2 us -> 40.5 us (0.960)
  waiting for transfers between devices: 16 us -> 12.9 us
  starting transfers between devices: 16 us -> 17.1 us
    ppermute x12, waiting for transfers between devices: 16 us -> 12.9 us  [swap(): return lax.ppermute(array, axis, pairs)]
    ppermute x12, starting transfers between devices: 16 us -> 17.1 us  [swap(): return lax.ppermute(array, axis, pairs)]
    pallas_call x5 -> x6, Pallas kernels: 9.19 us -> 9.45 us  [call(): pl.pallas_call(kernel, in_specs=[SMEM] * smem + [VMEM] * (len(args) - sme...]
  transfers between devices with their start and end apart: 12 -> 12, of which waited for: 9 -> 9; matrix products, arithmetic and copies ran while one was open for 0% -> 0% of each run, Pallas kernels for 6% -> 7%
where the time goes in v5:
time: 40.5 us; the launch traced here: 40.3 us
  starting transfers between devices  17.1 us (42%)
  waiting for transfers between devices  12.9 us (32%)
  Pallas kernels  9.45 us (23%)
  between operations  0.7 us (2%)
    ppermute x12, starting transfers between devices, swap(): return lax.ppermute(array, axis, pairs)  17.1 us
    ppermute x12, waiting for transfers between devices, swap(): return lax.ppermute(array, axis, pairs)  12.9 us
    pallas_call x6, Pallas kernels, call(): pl.pallas_call(kernel, in_specs=[SMEM] * smem + [VMEM] * (len(args) - sme...  9.45 us
  transfers between devices with their start and end apart: 12, of which 9 were waited for; matrix products, arithmetic and copies ran while one was open for 0% of the time, Pallas kernels for 7%

profile of v5, /device:TPU:6, one launch (start us, length us, event | category | flops | bytes accessed | tf_op | source)
XLA Modules:
  0.0 40.3 jit_solution(10242622005544176425)
XLA Ops:
  0.6 0.8 %begin.1 = (f32[4,128]{1,0:T(4,128)S(1)}, f32[4,128]{1,0:T(4,128)S(1)}, f32[8,128]{1,0:T(8,128)S(1)}, f32[8,128]{1,0:T(8,128)S(1)}) custom-call(f32[3,2,128]{2,1,0:T(2,128)} %bitcast.20, f32[3,2,128]{2,1,0:T(2,128)} %bitcast.21, f32[3,2,128]{2,1,0:T(2,128)} %bitcast.22, s32[2,128]{1,0:T(2,128)} %bitcast.23), custom_call_target="tpu_custom_call" | custom-call | tf_op jit(solution)/shard_map/begin/pallas_call | solution.py:361
  1.4 2.3 %collective-permute-start = (f32[4,128]{1,0:T(4,128)S(1)}, f32[4,128]{1,0:T(4,128)S(1)}, u32[]{:S(2)}, u32[]{:S(2)}) collective-permute-start(f32[4,128]{1,0:T(4,128)S(1)} %get-tuple-element.35), channel_id=1, source_target_pairs={{0,3},{1,2},{2,1},{3,0},{4,7},{5,6},{6,5},{7,4},{8,11},{9,10},{10,... | collective-permute-start | bytes 6152 | tf_op jit(solution)/shard_map/ppermute | solution.py:31
  3.7 2.6 %collective-permute-done = f32[4,128]{1,0:T(4,128)S(1)} collective-permute-done((f32[4,128]{1,0:T(4,128)S(1)}, f32[4,128]{1,0:T(4,128)S(1)}, u32[]{:S(2)}, u32[]{:S(2)}) %collective-permute-start) | collective-permute-done | bytes 2080 | tf_op jit(solution)/shard_map/ppermute | solution.py:31
  6.3 1.0 %collective-permute-done.1 = f32[4,128]{1,0:T(4,128)S(1)} collective-permute-done((f32[4,128]{1,0:T(4,128)S(1)}, f32[4,128]{1,0:T(4,128)S(1)}, u32[]{:S(2)}, u32[]{:S(2)}) %collective-permute-start.1) | collective-permute-done | bytes 2080 | tf_op jit(solution)/shard_map/ppermute | solution.py:31
  7.3 0.7 %collective-permute-start.3 = (f32[16,128]{1,0:T(8,128)S(1)}, f32[16,128]{1,0:T(8,128)S(1)}, u32[]{:S(2)}, u32[]{:S(2)}) collective-permute-start(f32[16,128]{1,0:T(8,128)S(1)} %pad_maximum_fusion), channel_id=1, source_target_pairs={{0,64},{64,0},{128,192},{192,128},{1,65},{65,1},{129,193},{193,129... | collective-permute-start | bytes 24584 | tf_op jit(solution)/shard_map/ppermute | solution.py:31
  7.9 2.2 %collective-permute-start.2 = (f32[16,128]{1,0:T(8,128)S(1)}, f32[16,128]{1,0:T(8,128)S(1)}, u32[]{:S(2)}, u32[]{:S(2)}) collective-permute-start(f32[16,128]{1,0:T(8,128)S(1)} %pad_maximum_fusion), channel_id=1, source_target_pairs={{0,192},{64,128},{128,64},{192,0},{1,193},{65,129},{129,65},{193,1... | collective-permute-start | bytes 24584 | tf_op jit(solution)/shard_map/ppermute | solution.py:31
  10.1 0.9 %collective-permute-done.3 = f32[16,128]{1,0:T(8,128)S(1)} collective-permute-done((f32[16,128]{1,0:T(8,128)S(1)}, f32[16,128]{1,0:T(8,128)S(1)}, u32[]{:S(2)}, u32[]{:S(2)}) %collective-permute-start.3) | collective-permute-done | bytes 8224 | tf_op jit(solution)/shard_map/ppermute | solution.py:31
  11.0 1.8 %collective-permute-done.2 = f32[16,128]{1,0:T(8,128)S(1)} collective-permute-done((f32[16,128]{1,0:T(8,128)S(1)}, f32[16,128]{1,0:T(8,128)S(1)}, u32[]{:S(2)}, u32[]{:S(2)}) %collective-permute-start.2) | collective-permute-done | bytes 8224 | tf_op jit(solution)/shard_map/ppermute | solution.py:31
  12.8 0.1 concatenate.8.plane_ref
  12.9 2.8 %collective-permute-start.5 = (f32[48,128]{1,0:T(8,128)S(1)}, f32[48,128]{1,0:T(8,128)S(1)}, u32[]{:S(2)}, u32[]{:S(2)}) collective-permute-start(f32[48,128]{1,0:T(8,128)S(1)} %concatenate.8.plane_ref), channel_id=1, source_target_pairs={{0,60},{4,8},{8,4},{12,16},{16,12},{20,24},{24,20},{28,32},{32,28}... | collective-permute-start | bytes 73736 | tf_op jit(solution)/shard_map/ppermute | solution.py:31
  15.7 1.9 %prepare.1 = (f32[1,256]{1,0:T(1,128)S(1)}, f32[64,128]{1,0:T(8,128)S(1)}, bf16[8,64]{1,0:T(8,128)(2,1)S(1)}, bf16[64,192]{1,0:T(8,128)(2,1)S(1)}, bf16[64,256]{...) custom-call(s32[2]{0:T(128)} %bitcast.24, ...), custom_call_target="tpu_custom_call" | custom-call | tf_op jit(solution)/shard_map/prepare/pallas_call | solution.py:361
  17.6 5.2 %edges.1 = (bf16[48,128]{1,0:T(8,128)(2,1)S(1)}, bf16[48,128]{1,0:T(8,128)(2,1)S(1)}, f32[2,48,128]{2,1,0:T(8,128)S(1)}, f32[1,256]{1,0:T(1,128)S(1)}) custom-call(f32[48,128]{1,0:T(8,128)S(1)} %concatenate.8.plane_ref, f32[48,128]{1,0:T(8,128)S(1)} %collective-permute-done.4.got_a_ref, f32[48,128]{1,0:T(8,128)S(1)} %collective-permute-done.5.got_b_ref, ...), custom_call_target="tpu_custom_call" | custom-call | tf_op jit(solution)/shard_map/edges/pallas_call | solution.py:361
  22.9 0.6 %collective-permute-start.6 = (bf16[48,128]{1,0:T(8,128)(2,1)S(1)}, bf16[48,128]{1,0:T(8,128)(2,1)S(1)}, u32[]{:S(2)}, u32[]{:S(2)}) collective-permute-start(bf16[48,128]{1,0:T(8,128)(2,1)S(1)} %get-tuple-element.55), channel_id=1, source_target_pairs={{0,4},{4,0},{8,12},{12,8},{16,20},{20,16},{24,28},{28,24},{32,36},... | collective-permute-start | bytes 36872 | tf_op jit(solution)/shard_map/ppermute | solution.py:31
  23.4 4.1 %collective-permute-start.7 = (bf16[48,128]{1,0:T(8,128)(2,1)S(1)}, bf16[48,128]{1,0:T(8,128)(2,1)S(1)}, u32[]{:S(2)}, u32[]{:S(2)}) collective-permute-start(bf16[48,128]{1,0:T(8,128)(2,1)S(1)} %get-tuple-element.56), channel_id=1, source_target_pairs={{0,60},{4,8},{8,4},{12,16},{16,12},{20,24},{24,20},{28,32},{32,28}... | collective-permute-start | bytes 36872 | tf_op jit(solution)/shard_map/ppermute | solution.py:31
  27.5 0.4 %near.1 = (f32[48,128]{1,0:T(8,128)S(1)}, f32[8,128]{1,0:T(8,128)S(1)}) custom-call(f32[2,48,128]{2,1,0:T(8,128)S(1)} %get-tuple-element.50.g_ref, f32[1,256]{1,0:T(1,128)S(1)} %get-tuple-element.51.energy_ref, bf16[144,4096]{1,0:T(8,128)(2,1)S(1)} %get-tuple-element.48.cell_ref, bf16[4096,128]{1,0:T(8,128)(2,1)S(1)} %get-tuple-element.49.pick_ref), custom_call_target="tpu_custom_call" | custom-call | tf_op jit(solution)/shard_map/near/pallas_call | solution.py:361
  28.0 1.0 %collective-permute-done.7 = bf16[48,128]{1,0:T(8,128)(2,1)S(1)} collective-permute-done((bf16[48,128]{1,0:T(8,128)(2,1)S(1)}, bf16[48,128]{1,0:T(8,128)(2,1)S(1)}, u32[]{:S(2)}, u32[]{:S(2)}) %collective-permute-start.7) | collective-permute-done | bytes 12320 | tf_op jit(solution)/shard_map/ppermute | solution.py:31
  29.1 2.3 %collective-permute-start.9 = (f32[16,128]{1,0:T(8,128)S(1)}, f32[16,128]{1,0:T(8,128)S(1)}, u32[]{:S(2)}, u32[]{:S(2)}) collective-permute-start(f32[16,128]{1,0:T(8,128)S(1)} %get-tuple-element.67), channel_id=1, source_target_pairs={{0,192},{64,128},{128,64},{192,0},{1,193},{65,129},{129,65},{193,1... | collective-permute-start | bytes 24584 | tf_op jit(solution)/shard_map/ppermute | solution.py:31
  31.3 1.4 %collective-permute-done.8 = f32[16,128]{1,0:T(8,128)S(1)} collective-permute-done((f32[16,128]{1,0:T(8,128)S(1)}, f32[16,128]{1,0:T(8,128)S(1)}, u32[]{:S(2)}, u32[]{:S(2)}) %collective-permute-start.8) | collective-permute-done | bytes 8224 | tf_op jit(solution)/shard_map/ppermute | solution.py:31
  32.7 1.3 %collective-permute-done.9 = f32[16,128]{1,0:T(8,128)S(1)} collective-permute-done((f32[16,128]{1,0:T(8,128)S(1)}, f32[16,128]{1,0:T(8,128)S(1)}, u32[]{:S(2)}, u32[]{:S(2)}) %collective-permute-start.9) | collective-permute-done | bytes 8224 | tf_op jit(solution)/shard_map/ppermute | solution.py:31
  34.0 2.1 %collective-permute-start.11 = (f32[4,128]{1,0:T(4,128)S(1)}, f32[4,128]{1,0:T(4,128)S(1)}, u32[]{:S(2)}, u32[]{:S(2)}) collective-permute-start(f32[4,128]{1,0:T(4,128)S(1)} %get-tuple-element.70), channel_id=1, source_target_pairs={{0,3},{1,2},{2,1},{3,0},{4,7},{5,6},{6,5},{7,4},{8,11},{9,10},{10,... | collective-permute-start | bytes 6152 | tf_op jit(solution)/shard_map/ppermute | solution.py:31
  36.1 0.6 %early.1 = (f32[8,128]{1,0:T(8,128)S(1)}, f32[8,128]{1,0:T(8,128)S(1)}, f32[3,2,128]{2,1,0:T(2,128)}, f32[2,128]{1,0:T(2,128)}) custom-call(f32[8,128]{1,0:T(8,128)S(1)} %get-tuple-element.33.mine_ref, f32[8,128]{1,0:T(8,128)S(1)} %get-tuple-element.34.keep_ref, f32[8,128]{1,0:T(8,128)S(1)} %get-tuple-element.52.own_ref, f32[1,256]{1,0:T(1,128)S(1)} %get-tuple-element.37.occ_ref), custom_call_target="tpu_custom_call" | custom-call | tf_op jit(solution)/shard_map/early/pallas_call | solution.py:361
  36.7 2.2 %collective-permute-done.11.got_b_ref = f32[4,128]{1,0:T(4,128)S(1)} collective-permute-done((f32[4,128]{1,0:T(4,128)S(1)}, f32[4,128]{1,0:T(4,128)S(1)}, u32[]{:S(2)}, u32[]{:S(2)}) %collective-permute-start.11) | collective-permute-done | bytes 2080 | tf_op jit(solution)/shard_map/ppermute | solution.py:31
  38.9 0.8 %collective-permute-done.10.got_a_ref = f32[4,128]{1,0:T(4,128)S(1)} collective-permute-done((f32[4,128]{1,0:T(4,128)S(1)}, f32[4,128]{1,0:T(4,128)S(1)}, u32[]{:S(2)}, u32[]{:S(2)}) %collective-permute-start.10) | collective-permute-done | bytes 2080 | tf_op jit(solution)/shard_map/ppermute | solution.py:31
  39.7 0.6 %finish.1 = (f32[3,2,128]{2,1,0:T(2,128)}, f32[3,2,128]{2,1,0:T(2,128)}) custom-call(f32[16,128]{1,0:T(8,128)S(1)} %fusion.mid_ref, f32[4,128]{1,0:T(4,128)S(1)} %collective-permute-done.10.got_a_ref, f32[4,128]{1,0:T(4,128)S(1)} %collective-permute-done.11.got_b_ref, f32[8,128]{1,0:T(8,128)S(1)} %get-tuple-element.52.own_ref, ...), custom_call_target="tpu_custom_call" | custom-call | tf_op jit(solution)/shard_map/finish/pallas_call | solution.py:361
  (14 shorter events, 0.2 us)
Async XLA Ops:
  1.4 4.9 %collective-permute-start = (f32[4,128]{1,0:T(4,128)S(1)}, f32[4,128]{1,0:T(4,128)S(1)}, u32[]{:S(2)}, u32[]{:S(2)}) collective-permute-start(f32[4,128]{1,0:T(4,128)S(1)} %get-tuple-element.35), channel_id=1, source_target_pairs={{0,3},{1,2},{2,1},{3,0},{4,7},{5,6},{6,5},{7,4},{8,11},{9,10},{10,... | collective-permute-start | bytes 6152 | tf_op jit(solution)/shard_map/ppermute | solution.py:31
  3.7 3.6 %collective-permute-start.1 = (f32[4,128]{1,0:T(4,128)S(1)}, f32[4,128]{1,0:T(4,128)S(1)}, u32[]{:S(2)}, u32[]{:S(2)}) collective-permute-start(f32[4,128]{1,0:T(4,128)S(1)} %get-tuple-element.36), channel_id=1, source_target_pairs={{0,1},{1,0},{2,3},{3,2},{4,5},{5,4},{6,7},{7,6},{8,9},{9,8},{10,11... | collective-permute-start | bytes 6152 | tf_op jit(solution)/shard_map/ppermute | solution.py:31
  7.3 3.7 %collective-permute-start.3 = (f32[16,128]{1,0:T(8,128)S(1)}, f32[16,128]{1,0:T(8,128)S(1)}, u32[]{:S(2)}, u32[]{:S(2)}) collective-permute-start(f32[16,128]{1,0:T(8,128)S(1)} %pad_maximum_fusion), channel_id=1, source_target_pairs={{0,64},{64,0},{128,192},{192,128},{1,65},{65,1},{129,193},{193,129... | collective-permute-start | bytes 24584 | tf_op jit(solution)/shard_map/ppermute | solution.py:31
  7.9 4.9 %collective-permute-start.2 = (f32[16,128]{1,0:T(8,128)S(1)}, f32[16,128]{1,0:T(8,128)S(1)}, u32[]{:S(2)}, u32[]{:S(2)}) collective-permute-start(f32[16,128]{1,0:T(8,128)S(1)} %pad_maximum_fusion), channel_id=1, source_target_pairs={{0,192},{64,128},{128,64},{192,0},{1,193},{65,129},{129,65},{193,1... | collective-permute-start | bytes 24584 | tf_op jit(solution)/shard_map/ppermute | solution.py:31
  12.9 4.7 %collective-permute-start.5 = (f32[48,128]{1,0:T(8,128)S(1)}, f32[48,128]{1,0:T(8,128)S(1)}, u32[]{:S(2)}, u32[]{:S(2)}) collective-permute-start(f32[48,128]{1,0:T(8,128)S(1)} %concatenate.8.plane_ref), channel_id=1, source_target_pairs={{0,60},{4,8},{8,4},{12,16},{16,12},{20,24},{24,20},{28,32},{32,28}... | collective-permute-start | bytes 73736 | tf_op jit(solution)/shard_map/ppermute | solution.py:31
  15.7 1.9 %collective-permute-start.4 = (f32[48,128]{1,0:T(8,128)S(1)}, f32[48,128]{1,0:T(8,128)S(1)}, u32[]{:S(2)}, u32[]{:S(2)}) collective-permute-start(f32[48,128]{1,0:T(8,128)S(1)} %concatenate.8.plane_ref), channel_id=1, source_target_pairs={{0,4},{4,0},{8,12},{12,8},{16,20},{20,16},{24,28},{28,24},{32,36},... | collective-permute-start | bytes 73736 | tf_op jit(solution)/shard_map/ppermute | solution.py:31
  22.9 5.1 %collective-permute-start.6 = (bf16[48,128]{1,0:T(8,128)(2,1)S(1)}, bf16[48,128]{1,0:T(8,128)(2,1)S(1)}, u32[]{:S(2)}, u32[]{:S(2)}) collective-permute-start(bf16[48,128]{1,0:T(8,128)(2,1)S(1)} %get-tuple-element.55), channel_id=1, source_target_pairs={{0,4},{4,0},{8,12},{12,8},{16,20},{20,16},{24,28},{28,24},{32,36},... | collective-permute-start | bytes 36872 | tf_op jit(solution)/shard_map/ppermute | solution.py:31
  23.4 5.5 %collective-permute-start.7 = (bf16[48,128]{1,0:T(8,128)(2,1)S(1)}, bf16[48,128]{1,0:T(8,128)(2,1)S(1)}, u32[]{:S(2)}, u32[]{:S(2)}) collective-permute-start(bf16[48,128]{1,0:T(8,128)(2,1)S(1)} %get-tuple-element.56), channel_id=1, source_target_pairs={{0,60},{4,8},{8,4},{12,16},{16,12},{20,24},{24,20},{28,32},{32,28}... | collective-permute-start | bytes 36872 | tf_op jit(solution)/shard_map/ppermute | solution.py:31
  29.0 3.7 %collective-permute-start.8 = (f32[16,128]{1,0:T(8,128)S(1)}, f32[16,128]{1,0:T(8,128)S(1)}, u32[]{:S(2)}, u32[]{:S(2)}) collective-permute-start(f32[16,128]{1,0:T(8,128)S(1)} %get-tuple-element.66), channel_id=1, source_target_pairs={{0,64},{64,0},{128,192},{192,128},{1,65},{65,1},{129,193},{193,129... | collective-permute-start | bytes 24584 | tf_op jit(solution)/shard_map/ppermute | solution.py:31
  29.1 4.9 %collective-permute-start.9 = (f32[16,128]{1,0:T(8,128)S(1)}, f32[16,128]{1,0:T(8,128)S(1)}, u32[]{:S(2)}, u32[]{:S(2)}) collective-permute-start(f32[16,128]{1,0:T(8,128)S(1)} %get-tuple-element.67), channel_id=1, source_target_pairs={{0,192},{64,128},{128,64},{192,0},{1,193},{65,129},{129,65},{193,1... | collective-permute-start | bytes 24584 | tf_op jit(solution)/shard_map/ppermute | solution.py:31
  34.0 4.9 %collective-permute-start.11 = (f32[4,128]{1,0:T(4,128)S(1)}, f32[4,128]{1,0:T(4,128)S(1)}, u32[]{:S(2)}, u32[]{:S(2)}) collective-permute-start(f32[4,128]{1,0:T(4,128)S(1)} %get-tuple-element.70), channel_id=1, source_target_pairs={{0,3},{1,2},{2,1},{3,0},{4,7},{5,6},{6,5},{7,4},{8,11},{9,10},{10,... | collective-permute-start | bytes 6152 | tf_op jit(solution)/shard_map/ppermute | solution.py:31
  36.1 3.6 %collective-permute-start.10 = (f32[4,128]{1,0:T(4,128)S(1)}, f32[4,128]{1,0:T(4,128)S(1)}, u32[]{:S(2)}, u32[]{:S(2)}) collective-permute-start(f32[4,128]{1,0:T(4,128)S(1)} %get-tuple-element.71), channel_id=1, source_target_pairs={{0,1},{1,0},{2,3},{3,2},{4,5},{5,4},{6,7},{7,6},{8,9},{9,8},{10,11... | collective-permute-start | bytes 6152 | tf_op jit(solution)/shard_map/ppermute | solution.py:31

commit v6 on v5

--- a/solution.py
+++ b/solution.py
@@ -92,8 +92,9 @@
 
 def prepare_kernel(
     count_ref, codes_ref, emb_ref, w1_ref, w2_ref, wnt_ref, we_ref,
-    occ_ref, web_ref, w1c_ref, w2c_ref, wntc_ref, wc_ref, w2t_ref, wn_ref, embt_ref, off_ref, slot_ref, cell_ref, pick_ref,
+    side_ref, occ_ref, web_ref, w1c_ref, w2c_ref, wntc_ref, wc_ref, w2t_ref, wn_ref, embt_ref, off_ref, slot_ref, cell_ref, pick_ref,
 ):
+    side_ref[...] = jnp.where(lax.axis_index("gx") % 2 == 0, jnp.ones((16, CAP), F32), jnp.zeros((16, CAP), F32))
     slot_number = lax.broadcasted_iota(jnp.int32, (1, CAP), 1)
     for r in range(R):
         occ_ref[:, r * CAP:(r + 1) * CAP] = jnp.where(slot_number < count_ref[r], 1.0, 0.0)
@@ -125,35 +126,46 @@
             pick_ref[lanes, :] = jnp.where(slot_rows[:, k:k + 1] == slots, 1.0, 0.0).astype(BF16)
 
 
+def gather_plane(off_ref, slot_ref, table_ref, base, oy, acc):
+    offs = [[off_ref[r, h * 8:(h + 1) * 8, :] for h in range(2)] for r in range(R)]
+    slots = [[slot_ref[r, h * 8:(h + 1) * 8, :] for h in range(2)] for r in range(R)]
+    acc = list(acc)
+    for ox in range(3):
+        for zz in range(4):
+            at = base + ox * 16 + zz * 4
+            rows = [rows8(table_ref[at + q:at + q + 1, :], CAP) for q in range(4)]
+            for r in range(R):
+                oz = zz - r
+                if not 0 <= oz <= 2:
+                    continue
+                for h in range(2):
+                    hit = offs[r][h] == ox * 9 + oy * 3 + oz
+                    for q in range(4):
+                        got = jnp.take_along_axis(rows[q], slots[r][h], axis=1, mode="promise_in_bounds")
+                        n = (r * 2 + h) * 4 + q
+                        acc[n] = jnp.where(hit, got, acc[n])
+    return offs, acc
+
+
+def middle_kernel(plane_ref, off_ref, slot_ref, gathered_ref):
+    _, acc = gather_plane(off_ref, slot_ref, plane_ref, 0, 1, [jnp.zeros((8, CAP), F32)] * 16)
+    for n in range(16):
+        gathered_ref[n * 8:(n + 1) * 8, :] = acc[n]
+
+
 def edges_kernel(
-    plane_ref, got_a_ref, got_b_ref, occ_ref, web_ref, w1_ref, w2_ref, wnt_ref, wc_ref, w2t_ref, wn_ref, embt_ref, off_ref, slot_ref, cell_ref, pick_ref,
+    plane_ref, got_a_ref, got_b_ref, gathered_ref, occ_ref, web_ref, w1_ref, w2_ref, wnt_ref, wc_ref, w2t_ref, wn_ref, embt_ref, off_ref, slot_ref, cell_ref, pick_ref,
     send_a_ref, send_b_ref, g_s, energy_ref,
     pos_s, d_s, kd_s, ey_s, eyb_s, exu_s, ds_s, feat_s, q_s, qb_s, m_s, mb_s, gr_s, t_s, ts_s, a_s,
 ):
     even = lax.axis_index("gy") % 2 == 0
     pos_s[0:48] = jnp.where(even, got_b_ref[...], got_a_ref[...])
-    pos_s[48:96] = plane_ref[...]
-    pos_s[96:144] = jnp.where(even, got_a_ref[...], got_b_ref[...])
-
-    acc = [jnp.zeros((8, CAP), F32) for _ in range(16)]
-    offs = [[off_ref[r, h * 8:(h + 1) * 8, :] for h in range(2)] for r in range(R)]
-    slots = [[slot_ref[r, h * 8:(h + 1) * 8, :] for h in range(2)] for r in range(R)]
-    for col in range(9):
-        place = col % 3 * 3 + col // 3
-        for zz in range(4):
-            rows = [rows8(pos_s[place * 16 + zz * 4 + q:place * 16 + zz * 4 + q + 1, :], CAP) for q in range(4)]
-            for r in range(R):
-                dz = zz - r
-                if not 0 <= dz <= 2:
-                    continue
-                for h in range(2):
-                    hit = offs[r][h] == col * 3 + dz
-                    for q in range(4):
-                        got = jnp.take_along_axis(rows[q], slots[r][h], axis=1, mode="promise_in_bounds")
-                        at = (r * 2 + h) * 4 + q
-                        acc[at] = jnp.where(hit, got, acc[at])
-    for r in range(R):
-        own = [pos_s[64 + (1 + r) * 4 + c:64 + (1 + r) * 4 + c + 1, :] for c in range(3)]
+    pos_s[48:96] = jnp.where(even, got_a_ref[...], got_b_ref[...])
+    acc = [gathered_ref[at * 8:(at + 1) * 8, :] for at in range(16)]
+    offs, acc = gather_plane(off_ref, slot_ref, pos_s, 0, 0, acc)
+    offs, acc = gather_plane(off_ref, slot_ref, pos_s, 48, 2, acc)
+    for r in range(R):
+        own = [plane_ref[16 + (1 + r) * 4 + c:16 + (1 + r) * 4 + c + 1, :] for c in range(3)]
         for h in range(2):
             off = offs[r][h]
             shift = (off // 9 - 1, off // 3 % 3 - 1, off % 3 - 1)
@@ -230,7 +242,7 @@
         message_block(cb, 0)
 
     own_kind = jnp.concatenate(
-        [jnp.broadcast_to(pos_s[64 + (1 + r) * 4 + 3:64 + (1 + r) * 4 + 4, :], (16, CAP)) for r in range(R)], axis=1
+        [jnp.broadcast_to(plane_ref[16 + (1 + r) * 4 + 3:16 + (1 + r) * 4 + 4, :], (16, CAP)) for r in range(R)], axis=1
     )
     own_feat = jnp.dot(
         embt_ref[...], jnp.where(own_kind == kinds16, 1.0, 0.0).astype(BF16), preferred_element_type=F32
@@ -376,16 +388,21 @@
 
 def prepare(count, codes, embed, w1, w2, wnt, we):
     outs = [
-        ((1, W), F32), ((CH, CAP), F32), ((NB, CH), BF16), ((CH, 3 * CH), BF16), ((CH, 4 * CH), BF16),
+        ((16, CAP), F32), ((1, W), F32), ((CH, CAP), F32), ((NB, CH), BF16), ((CH, 3 * CH), BF16), ((CH, 4 * CH), BF16),
         ((2 * CH, NB + 16), BF16), ((3 * CH, CH), BF16), ((4 * CH, CH), BF16), ((CH, 16), BF16),
         ((R, K, CAP), jnp.int32), ((R, K, CAP), jnp.int32), ((144, K * W), BF16), ((K * W, CAP), BF16),
     ]
     return call(prepare_kernel, "prepare", (count, codes, embed, w1, w2, wnt, we), outs, 7, smem=1)
 
 
-def edges(plane, got_a, got_b, prepared):
+def middle(plane, prepared):
+    outs = [((16 * 8, CAP), F32)]
+    return call(middle_kernel, "middle", (plane, *prepared[-4:-2]), outs, 0, limit=EDGES_LIMIT)[0]
+
+
+def edges(plane, got_a, got_b, gathered, prepared):
     scratch = [
-        pltpu.VMEM((144, CAP), F32),
+        pltpu.VMEM((96, CAP), F32),
         pltpu.VMEM((R, 3 * K, CAP), F32),
         pltpu.VMEM((R, K, CAP), F32),
         pltpu.VMEM((9, 8 * K, W), F32),
@@ -403,7 +420,7 @@
         pltpu.VMEM((96, K * W), BF16),
     ]
     outs = [((48, CAP), BF16), ((48, CAP), BF16), ((R, 3 * K, CAP), F32), ((1, W), F32)]
-    return call(edges_kernel, "edges", (plane, got_a, got_b, *prepared), outs, 0, scratch=scratch, limit=EDGES_LIMIT)
+    return call(edges_kernel, "edges", (plane, got_a, got_b, gathered, *prepared), outs, 0, scratch=scratch, limit=EDGES_LIMIT)
 
 
 def near(gradient, energy, prepared):
@@ -433,7 +450,7 @@
     send_a, send_b, mine, keep = begin(
         frac.reshape(vectors), velocity.reshape(vectors), force_old.reshape(vectors), species.reshape(R, CAP)
     )
-    prepared = prepare(
+    side, *prepared = prepare(
         count, neighbours.reshape(K * R, CAP), embed, w_radial_in, w_radial_out, wnt, w_energy.reshape(1, CH)
     )
 
@@ -443,11 +460,12 @@
     )
     got_a, got_b = swap(column, "gx", False), swap(column, "gx", True)
     plane = jnp.concatenate(
-        [jnp.where(even_x, got_b, got_a), column, jnp.where(even_x, got_a, got_b)], axis=0
-    )
+        [jnp.where(side > 0.5, got_b, got_a), column, jnp.where(side > 0.5, got_a, got_b)], axis=0
+    )
+    gathered = middle(plane, prepared)
     got_a, got_b = swap(plane, "gy", False), swap(plane, "gy", True)
 
-    send_a, send_b, gradient, energy = edges(plane, got_a, got_b, prepared)
+    send_a, send_b, gradient, energy = edges(plane, got_a, got_b, gathered, prepared)
     plane, own = near(gradient, energy, prepared)
     speed, gain, next_frac, energy = early(mine, keep, own, prepared)
     plane = plane + swap(send_a, "gy", False).astype(F32) + swap(send_b, "gy", True).astype(F32)

time: 40.5 us -> 40.3 us (level)
  waiting for transfers between devices: 12.9 us -> 12.3 us
    ppermute x12, waiting for transfers between devices: 12.9 us -> 12.3 us  [swap(): return lax.ppermute(array, axis, pairs)]
    pallas_call x6 -> x7, Pallas kernels: 9.45 us -> 9.57 us  [call(): pl.pallas_call(kernel, in_specs=[SMEM] * smem + [VMEM] * (len(args) - sme...]
  transfers between devices with their start and end apart: 12 -> 12, of which waited for: 9 -> 9; matrix products, arithmetic and copies ran while one was open for 0% -> 0% of each run, Pallas kernels for 7% -> 8%
where the time goes in v6:
time: 40.3 us; the launch traced here: 40.1 us
  starting transfers between devices  17.4 us (43%)
  waiting for transfers between devices  12.3 us (31%)
  Pallas kernels  9.57 us (24%)
  between operations  0.71 us (2%)
    ppermute x12, starting transfers between devices, swap(): return lax.ppermute(array, axis, pairs)  17.4 us
    ppermute x12, waiting for transfers between devices, swap(): return lax.ppermute(array, axis, pairs)  12.3 us
    pallas_call x7, Pallas kernels, call(): pl.pallas_call(kernel, in_specs=[SMEM] * smem + [VMEM] * (len(args) - sme...  9.57 us
  transfers between devices with their start and end apart: 12, of which 9 were waited for; matrix products, arithmetic and copies ran while one was open for 0% of the time, Pallas kernels for 8%

profile of v6, /device:TPU:6, one launch (start us, length us, event | category | flops | bytes accessed | tf_op | source)
XLA Modules:
  0.0 40.1 jit_solution(11701203483636056605)
XLA Ops:
  0.6 0.8 %begin.1 = (f32[4,128]{1,0:T(4,128)S(1)}, f32[4,128]{1,0:T(4,128)S(1)}, f32[8,128]{1,0:T(8,128)S(1)}, f32[8,128]{1,0:T(8,128)S(1)}) custom-call(f32[3,2,128]{2,1,0:T(2,128)} %bitcast.20, f32[3,2,128]{2,1,0:T(2,128)} %bitcast.21, f32[3,2,128]{2,1,0:T(2,128)} %bitcast.22, s32[2,128]{1,0:T(2,128)} %bitcast.23), custom_call_target="tpu_custom_call" | custom-call | tf_op jit(solution)/shard_map/begin/pallas_call | solution.py:373
  1.4 2.3 %collective-permute-start = (f32[4,128]{1,0:T(4,128)S(1)}, f32[4,128]{1,0:T(4,128)S(1)}, u32[]{:S(2)}, u32[]{:S(2)}) collective-permute-start(f32[4,128]{1,0:T(4,128)S(1)} %get-tuple-element.37), channel_id=1, source_target_pairs={{0,3},{1,2},{2,1},{3,0},{4,7},{5,6},{6,5},{7,4},{8,11},{9,10},{10,... | collective-permute-start | bytes 6152 | tf_op jit(solution)/shard_map/ppermute | solution.py:31
  3.7 2.6 %collective-permute-done = f32[4,128]{1,0:T(4,128)S(1)} collective-permute-done((f32[4,128]{1,0:T(4,128)S(1)}, f32[4,128]{1,0:T(4,128)S(1)}, u32[]{:S(2)}, u32[]{:S(2)}) %collective-permute-start) | collective-permute-done | bytes 2080 | tf_op jit(solution)/shard_map/ppermute | solution.py:31
  6.3 1.0 %collective-permute-done.1 = f32[4,128]{1,0:T(4,128)S(1)} collective-permute-done((f32[4,128]{1,0:T(4,128)S(1)}, f32[4,128]{1,0:T(4,128)S(1)}, u32[]{:S(2)}, u32[]{:S(2)}) %collective-permute-start.1) | collective-permute-done | bytes 2080 | tf_op jit(solution)/shard_map/ppermute | solution.py:31
  7.3 0.7 %collective-permute-start.3 = (f32[16,128]{1,0:T(8,128)S(1)}, f32[16,128]{1,0:T(8,128)S(1)}, u32[]{:S(2)}, u32[]{:S(2)}) collective-permute-start(f32[16,128]{1,0:T(8,128)S(1)} %pad_maximum_fusion), channel_id=1, source_target_pairs={{0,64},{64,0},{128,192},{192,128},{1,65},{65,1},{129,193},{193,129... | collective-permute-start | bytes 24584 | tf_op jit(solution)/shard_map/ppermute | solution.py:31
  7.9 2.2 %collective-permute-start.2 = (f32[16,128]{1,0:T(8,128)S(1)}, f32[16,128]{1,0:T(8,128)S(1)}, u32[]{:S(2)}, u32[]{:S(2)}) collective-permute-start(f32[16,128]{1,0:T(8,128)S(1)} %pad_maximum_fusion), channel_id=1, source_target_pairs={{0,192},{64,128},{128,64},{192,0},{1,193},{65,129},{129,65},{193,1... | collective-permute-start | bytes 24584 | tf_op jit(solution)/shard_map/ppermute | solution.py:31
  10.1 1.9 %prepare.1 = (f32[16,128]{1,0:T(8,128)S(1)}, f32[1,256]{1,0:T(1,128)S(1)}, f32[64,128]{1,0:T(8,128)S(1)}, bf16[8,64]{1,0:T(8,128)(2,1)S(1)}, bf16[64,192]{1,0:T(...) custom-call(s32[2]{0:T(128)} %bitcast.24, ...), custom_call_target="tpu_custom_call" | custom-call | tf_op jit(solution)/shard_map/prepare/pallas_call | solution.py:373
  12.0 0.8 %collective-permute-done.2 = f32[16,128]{1,0:T(8,128)S(1)} collective-permute-done((f32[16,128]{1,0:T(8,128)S(1)}, f32[16,128]{1,0:T(8,128)S(1)}, u32[]{:S(2)}, u32[]{:S(2)}) %collective-permute-start.2) | collective-permute-done | bytes 8224 | tf_op jit(solution)/shard_map/ppermute | solution.py:31
  12.8 0.1 concatenate.8.plane_ref
  12.9 2.9 %collective-permute-start.5 = (f32[48,128]{1,0:T(8,128)S(1)}, f32[48,128]{1,0:T(8,128)S(1)}, u32[]{:S(2)}, u32[]{:S(2)}) collective-permute-start(f32[48,128]{1,0:T(8,128)S(1)} %concatenate.8.plane_ref), channel_id=1, source_target_pairs={{0,60},{4,8},{8,4},{12,16},{16,12},{20,24},{24,20},{28,32},{32,28}... | collective-permute-start | bytes 73736 | tf_op jit(solution)/shard_map/ppermute | solution.py:31
  15.9 0.3 middle.1.gathered_ref
  16.2 1.3 %collective-permute-done.5.got_b_ref = f32[48,128]{1,0:T(8,128)S(1)} collective-permute-done((f32[48,128]{1,0:T(8,128)S(1)}, f32[48,128]{1,0:T(8,128)S(1)}, u32[]{:S(2)}, u32[]{:S(2)}) %collective-permute-start.5) | collective-permute-done | bytes 24608 | tf_op jit(solution)/shard_map/ppermute | solution.py:31
  17.5 5.0 %edges.1 = (bf16[48,128]{1,0:T(8,128)(2,1)S(1)}, bf16[48,128]{1,0:T(8,128)(2,1)S(1)}, f32[2,48,128]{2,1,0:T(8,128)S(1)}, f32[1,256]{1,0:T(1,128)S(1)}) custom-call(f32[48,128]{1,0:T(8,128)S(1)} %concatenate.8.plane_ref, f32[48,128]{1,0:T(8,128)S(1)} %collective-permute-done.4.got_a_ref, f32[48,128]{1,0:T(8,128)S(1)} %collective-permute-done.5.got_b_ref, ...), custom_call_target="tpu_custom_call" | custom-call | tf_op jit(solution)/shard_map/edges/pallas_call | solution.py:373
  22.6 4.8 %collective-permute-start.7 = (bf16[48,128]{1,0:T(8,128)(2,1)S(1)}, bf16[48,128]{1,0:T(8,128)(2,1)S(1)}, u32[]{:S(2)}, u32[]{:S(2)}) collective-permute-start(bf16[48,128]{1,0:T(8,128)(2,1)S(1)} %get-tuple-element.58), channel_id=1, source_target_pairs={{0,60},{4,8},{8,4},{12,16},{16,12},{20,24},{24,20},{28,32},{32,28}... | collective-permute-start | bytes 36872 | tf_op jit(solution)/shard_map/ppermute | solution.py:31
  27.4 0.4 %near.1 = (f32[48,128]{1,0:T(8,128)S(1)}, f32[8,128]{1,0:T(8,128)S(1)}) custom-call(f32[2,48,128]{2,1,0:T(8,128)S(1)} %get-tuple-element.52.g_ref, f32[1,256]{1,0:T(1,128)S(1)} %get-tuple-element.53.energy_ref, bf16[144,4096]{1,0:T(8,128)(2,1)S(1)} %get-tuple-element.50.cell_ref, bf16[4096,128]{1,0:T(8,128)(2,1)S(1)} %get-tuple-element.51.pick_ref), custom_call_target="tpu_custom_call" | custom-call | tf_op jit(solution)/shard_map/near/pallas_call | solution.py:373
  27.8 1.0 %collective-permute-done.7 = bf16[48,128]{1,0:T(8,128)(2,1)S(1)} collective-permute-done((bf16[48,128]{1,0:T(8,128)(2,1)S(1)}, bf16[48,128]{1,0:T(8,128)(2,1)S(1)}, u32[]{:S(2)}, u32[]{:S(2)}) %collective-permute-start.7) | collective-permute-done | bytes 12320 | tf_op jit(solution)/shard_map/ppermute | solution.py:31
  28.9 2.3 %collective-permute-start.9 = (f32[16,128]{1,0:T(8,128)S(1)}, f32[16,128]{1,0:T(8,128)S(1)}, u32[]{:S(2)}, u32[]{:S(2)}) collective-permute-start(f32[16,128]{1,0:T(8,128)S(1)} %get-tuple-element.71), channel_id=1, source_target_pairs={{0,192},{64,128},{128,64},{192,0},{1,193},{65,129},{129,65},{193,1... | collective-permute-start | bytes 24584 | tf_op jit(solution)/shard_map/ppermute | solution.py:31
  31.1 1.4 %collective-permute-done.8 = f32[16,128]{1,0:T(8,128)S(1)} collective-permute-done((f32[16,128]{1,0:T(8,128)S(1)}, f32[16,128]{1,0:T(8,128)S(1)}, u32[]{:S(2)}, u32[]{:S(2)}) %collective-permute-start.8) | collective-permute-done | bytes 8224 | tf_op jit(solution)/shard_map/ppermute | solution.py:31
  32.5 1.3 %collective-permute-done.9 = f32[16,128]{1,0:T(8,128)S(1)} collective-permute-done((f32[16,128]{1,0:T(8,128)S(1)}, f32[16,128]{1,0:T(8,128)S(1)}, u32[]{:S(2)}, u32[]{:S(2)}) %collective-permute-start.9) | collective-permute-done | bytes 8224 | tf_op jit(solution)/shard_map/ppermute | solution.py:31
  33.8 2.1 %collective-permute-start.11 = (f32[4,128]{1,0:T(4,128)S(1)}, f32[4,128]{1,0:T(4,128)S(1)}, u32[]{:S(2)}, u32[]{:S(2)}) collective-permute-start(f32[4,128]{1,0:T(4,128)S(1)} %get-tuple-element.72), channel_id=1, source_target_pairs={{0,3},{1,2},{2,1},{3,0},{4,7},{5,6},{6,5},{7,4},{8,11},{9,10},{10,... | collective-permute-start | bytes 6152 | tf_op jit(solution)/shard_map/ppermute | solution.py:31
  35.9 0.6 %early.1 = (f32[8,128]{1,0:T(8,128)S(1)}, f32[8,128]{1,0:T(8,128)S(1)}, f32[3,2,128]{2,1,0:T(2,128)}, f32[2,128]{1,0:T(2,128)}) custom-call(f32[8,128]{1,0:T(8,128)S(1)} %get-tuple-element.34.mine_ref, f32[8,128]{1,0:T(8,128)S(1)} %get-tuple-element.35.keep_ref, f32[8,128]{1,0:T(8,128)S(1)} %get-tuple-element.54.own_ref, f32[1,256]{1,0:T(1,128)S(1)} %get-tuple-element.41.occ_ref), custom_call_target="tpu_custom_call" | custom-call | tf_op jit(solution)/shard_map/early/pallas_call | solution.py:373
  36.5 2.2 %collective-permute-done.11.got_b_ref = f32[4,128]{1,0:T(4,128)S(1)} collective-permute-done((f32[4,128]{1,0:T(4,128)S(1)}, f32[4,128]{1,0:T(4,128)S(1)}, u32[]{:S(2)}, u32[]{:S(2)}) %collective-permute-start.11) | collective-permute-done | bytes 2080 | tf_op jit(solution)/shard_map/ppermute | solution.py:31
  38.7 0.8 %collective-permute-done.10.got_a_ref = f32[4,128]{1,0:T(4,128)S(1)} collective-permute-done((f32[4,128]{1,0:T(4,128)S(1)}, f32[4,128]{1,0:T(4,128)S(1)}, u32[]{:S(2)}, u32[]{:S(2)}) %collective-permute-start.10) | collective-permute-done | bytes 2080 | tf_op jit(solution)/shard_map/ppermute | solution.py:31
  39.5 0.6 %finish.1 = (f32[3,2,128]{2,1,0:T(2,128)}, f32[3,2,128]{2,1,0:T(2,128)}) custom-call(f32[16,128]{1,0:T(8,128)S(1)} %fusion.mid_ref, f32[4,128]{1,0:T(4,128)S(1)} %collective-permute-done.10.got_a_ref, f32[4,128]{1,0:T(4,128)S(1)} %collective-permute-done.11.got_b_ref, f32[8,128]{1,0:T(8,128)S(1)} %get-tuple-element.54.own_ref, ...), custom_call_target="tpu_custom_call" | custom-call | tf_op jit(solution)/shard_map/finish/pallas_call | solution.py:373
  (16 shorter events, 0.3 us)
Async XLA Ops:
  1.4 4.9 %collective-permute-start = (f32[4,128]{1,0:T(4,128)S(1)}, f32[4,128]{1,0:T(4,128)S(1)}, u32[]{:S(2)}, u32[]{:S(2)}) collective-permute-start(f32[4,128]{1,0:T(4,128)S(1)} %get-tuple-element.37), channel_id=1, source_target_pairs={{0,3},{1,2},{2,1},{3,0},{4,7},{5,6},{6,5},{7,4},{8,11},{9,10},{10,... | collective-permute-start | bytes 6152 | tf_op jit(solution)/shard_map/ppermute | solution.py:31
  3.7 3.6 %collective-permute-start.1 = (f32[4,128]{1,0:T(4,128)S(1)}, f32[4,128]{1,0:T(4,128)S(1)}, u32[]{:S(2)}, u32[]{:S(2)}) collective-permute-start(f32[4,128]{1,0:T(4,128)S(1)} %get-tuple-element.38), channel_id=1, source_target_pairs={{0,1},{1,0},{2,3},{3,2},{4,5},{5,4},{6,7},{7,6},{8,9},{9,8},{10,11... | collective-permute-start | bytes 6152 | tf_op jit(solution)/shard_map/ppermute | solution.py:31
  7.3 4.8 %collective-permute-start.3 = (f32[16,128]{1,0:T(8,128)S(1)}, f32[16,128]{1,0:T(8,128)S(1)}, u32[]{:S(2)}, u32[]{:S(2)}) collective-permute-start(f32[16,128]{1,0:T(8,128)S(1)} %pad_maximum_fusion), channel_id=1, source_target_pairs={{0,64},{64,0},{128,192},{192,128},{1,65},{65,1},{129,193},{193,129... | collective-permute-start | bytes 24584 | tf_op jit(solution)/shard_map/ppermute | solution.py:31
  7.9 4.9 %collective-permute-start.2 = (f32[16,128]{1,0:T(8,128)S(1)}, f32[16,128]{1,0:T(8,128)S(1)}, u32[]{:S(2)}, u32[]{:S(2)}) collective-permute-start(f32[16,128]{1,0:T(8,128)S(1)} %pad_maximum_fusion), channel_id=1, source_target_pairs={{0,192},{64,128},{128,64},{192,0},{1,193},{65,129},{129,65},{193,1... | collective-permute-start | bytes 24584 | tf_op jit(solution)/shard_map/ppermute | solution.py:31
  12.9 4.5 %collective-permute-start.5 = (f32[48,128]{1,0:T(8,128)S(1)}, f32[48,128]{1,0:T(8,128)S(1)}, u32[]{:S(2)}, u32[]{:S(2)}) collective-permute-start(f32[48,128]{1,0:T(8,128)S(1)} %concatenate.8.plane_ref), channel_id=1, source_target_pairs={{0,60},{4,8},{8,4},{12,16},{16,12},{20,24},{24,20},{28,32},{32,28}... | collective-permute-start | bytes 73736 | tf_op jit(solution)/shard_map/ppermute | solution.py:31
  15.9 1.6 %collective-permute-start.4 = (f32[48,128]{1,0:T(8,128)S(1)}, f32[48,128]{1,0:T(8,128)S(1)}, u32[]{:S(2)}, u32[]{:S(2)}) collective-permute-start(f32[48,128]{1,0:T(8,128)S(1)} %concatenate.8.plane_ref), channel_id=1, source_target_pairs={{0,4},{4,0},{8,12},{12,8},{16,20},{20,16},{24,28},{28,24},{32,36},... | collective-permute-start | bytes 73736 | tf_op jit(solution)/shard_map/ppermute | solution.py:31
  22.5 5.3 %collective-permute-start.6 = (bf16[48,128]{1,0:T(8,128)(2,1)S(1)}, bf16[48,128]{1,0:T(8,128)(2,1)S(1)}, u32[]{:S(2)}, u32[]{:S(2)}) collective-permute-start(bf16[48,128]{1,0:T(8,128)(2,1)S(1)} %get-tuple-element.57), channel_id=1, source_target_pairs={{0,4},{4,0},{8,12},{12,8},{16,20},{20,16},{24,28},{28,24},{32,36},... | collective-permute-start | bytes 36872 | tf_op jit(solution)/shard_map/ppermute | solution.py:31
  22.6 6.2 %collective-permute-start.7 = (bf16[48,128]{1,0:T(8,128)(2,1)S(1)}, bf16[48,128]{1,0:T(8,128)(2,1)S(1)}, u32[]{:S(2)}, u32[]{:S(2)}) collective-permute-start(bf16[48,128]{1,0:T(8,128)(2,1)S(1)} %get-tuple-element.58), channel_id=1, source_target_pairs={{0,60},{4,8},{8,4},{12,16},{16,12},{20,24},{24,20},{28,32},{32,28}... | collective-permute-start | bytes 36872 | tf_op jit(solution)/shard_map/ppermute | solution.py:31
  28.8 3.7 %collective-permute-start.8 = (f32[16,128]{1,0:T(8,128)S(1)}, f32[16,128]{1,0:T(8,128)S(1)}, u32[]{:S(2)}, u32[]{:S(2)}) collective-permute-start(f32[16,128]{1,0:T(8,128)S(1)} %get-tuple-element.70), channel_id=1, source_target_pairs={{0,64},{64,0},{128,192},{192,128},{1,65},{65,1},{129,193},{193,129... | collective-permute-start | bytes 24584 | tf_op jit(solution)/shard_map/ppermute | solution.py:31
  28.9 4.9 %collective-permute-start.9 = (f32[16,128]{1,0:T(8,128)S(1)}, f32[16,128]{1,0:T(8,128)S(1)}, u32[]{:S(2)}, u32[]{:S(2)}) collective-permute-start(f32[16,128]{1,0:T(8,128)S(1)} %get-tuple-element.71), channel_id=1, source_target_pairs={{0,192},{64,128},{128,64},{192,0},{1,193},{65,129},{129,65},{193,1... | collective-permute-start | bytes 24584 | tf_op jit(solution)/shard_map/ppermute | solution.py:31
  33.8 4.9 %collective-permute-start.11 = (f32[4,128]{1,0:T(4,128)S(1)}, f32[4,128]{1,0:T(4,128)S(1)}, u32[]{:S(2)}, u32[]{:S(2)}) collective-permute-start(f32[4,128]{1,0:T(4,128)S(1)} %get-tuple-element.72), channel_id=1, source_target_pairs={{0,3},{1,2},{2,1},{3,0},{4,7},{5,6},{6,5},{7,4},{8,11},{9,10},{10,... | collective-permute-start | bytes 6152 | tf_op jit(solution)/shard_map/ppermute | solution.py:31
  35.9 3.6 %collective-permute-start.10 = (f32[4,128]{1,0:T(4,128)S(1)}, f32[4,128]{1,0:T(4,128)S(1)}, u32[]{:S(2)}, u32[]{:S(2)}) collective-permute-start(f32[4,128]{1,0:T(4,128)S(1)} %get-tuple-element.73), channel_id=1, source_target_pairs={{0,1},{1,0},{2,3},{3,2},{4,5},{5,4},{6,7},{7,6},{8,9},{9,8},{10,11... | collective-permute-start | bytes 6152 | tf_op jit(solution)/shard_map/ppermute | solution.py:31

commit v7 on v6

--- a/solution.py
+++ b/solution.py
@@ -468,10 +468,16 @@
     send_a, send_b, gradient, energy = edges(plane, got_a, got_b, gathered, prepared)
     plane, own = near(gradient, energy, prepared)
     speed, gain, next_frac, energy = early(mine, keep, own, prepared)
-    plane = plane + swap(send_a, "gy", False).astype(F32) + swap(send_b, "gy", True).astype(F32)
+    got_b, got_a = swap(send_b, "gy", True), swap(send_a, "gy", False)
+    plane = plane + got_b.astype(F32)
+    plane = lax.optimization_barrier(plane)
+    plane = plane + got_a.astype(F32)
     lower, column, upper = plane[0:16], plane[16:32], plane[32:48]
     send_a, send_b = jnp.where(even_x, upper, lower), jnp.where(even_x, lower, upper)
-    column = column + swap(send_a, "gx", False) + swap(send_b, "gx", True)
+    got_b, got_a = swap(send_b, "gx", True), swap(send_a, "gx", False)
+    column = column + got_b
+    column = lax.optimization_barrier(column)
+    column = column + got_a
     send_a = jnp.where(even_z, column[12:16], column[0:4])
     send_b = jnp.where(even_z, column[0:4], column[12:16])
     got_a, got_b = swap(send_a, "gz", False), swap(send_b, "gz", True)

time: 40.3 us -> 40.1 us (level)
  the two profiles are of different devices: /device:TPU:6 before, /device:TPU:128 now
where the time goes in v7:
time: 40.1 us; the launch traced here: 39.9 us
  waiting for transfers between devices  17.5 us (44%)
  starting transfers between devices  11.9 us (30%)
  Pallas kernels  9.57 us (24%)
  between operations  0.72 us (2%)
    ppermute x12, waiting for transfers between devices, swap(): return lax.ppermute(array, axis, pairs)  17.5 us
    ppermute x12, starting transfers between devices, swap(): return lax.ppermute(array, axis, pairs)  11.9 us
    pallas_call x7, Pallas kernels, call(): pl.pallas_call(kernel, in_specs=[SMEM] * smem + [VMEM] * (len(args) - sme...  9.57 us
  transfers between devices with their start and end apart: 12, of which 8 were waited for; matrix products, arithmetic and copies ran while one was open for 0% of the time, Pallas kernels for 8%

profile of v7, /device:TPU:128, one launch (start us, length us, event | category | flops | bytes accessed | tf_op | source)
XLA Modules:
  0.0 39.9 jit_solution(17969600788648216336)
XLA Ops:
  0.6 0.8 %begin.1 = (f32[4,128]{1,0:T(4,128)S(1)}, f32[4,128]{1,0:T(4,128)S(1)}, f32[8,128]{1,0:T(8,128)S(1)}, f32[8,128]{1,0:T(8,128)S(1)}) custom-call(f32[3,2,128]{2,1,0:T(2,128)} %bitcast.20, f32[3,2,128]{2,1,0:T(2,128)} %bitcast.21, f32[3,2,128]{2,1,0:T(2,128)} %bitcast.22, s32[2,128]{1,0:T(2,128)} %bitcast.23), custom_call_target="tpu_custom_call" | custom-call | tf_op jit(solution)/shard_map/begin/pallas_call | solution.py:373
  1.4 2.8 %collective-permute-start = (f32[4,128]{1,0:T(4,128)S(1)}, f32[4,128]{1,0:T(4,128)S(1)}, u32[]{:S(2)}, u32[]{:S(2)}) collective-permute-start(f32[4,128]{1,0:T(4,128)S(1)} %get-tuple-element.37), channel_id=1, source_target_pairs={{0,3},{1,2},{2,1},{3,0},{4,7},{5,6},{6,5},{7,4},{8,11},{9,10},{10,... | collective-permute-start | bytes 6152 | tf_op jit(solution)/shard_map/ppermute | solution.py:31
  4.2 0.2 collective-permute-start.1
  4.4 1.8 %collective-permute-done = f32[4,128]{1,0:T(4,128)S(1)} collective-permute-done((f32[4,128]{1,0:T(4,128)S(1)}, f32[4,128]{1,0:T(4,128)S(1)}, u32[]{:S(2)}, u32[]{:S(2)}) %collective-permute-start) | collective-permute-done | bytes 2080 | tf_op jit(solution)/shard_map/ppermute | solution.py:31
  6.3 1.5 %collective-permute-done.1 = f32[4,128]{1,0:T(4,128)S(1)} collective-permute-done((f32[4,128]{1,0:T(4,128)S(1)}, f32[4,128]{1,0:T(4,128)S(1)}, u32[]{:S(2)}, u32[]{:S(2)}) %collective-permute-start.1) | collective-permute-done | bytes 2080 | tf_op jit(solution)/shard_map/ppermute | solution.py:31
  7.8 1.7 %collective-permute-start.3 = (f32[16,128]{1,0:T(8,128)S(1)}, f32[16,128]{1,0:T(8,128)S(1)}, u32[]{:S(2)}, u32[]{:S(2)}) collective-permute-start(f32[16,128]{1,0:T(8,128)S(1)} %pad_maximum_fusion), channel_id=1, source_target_pairs={{0,64},{64,0},{128,192},{192,128},{1,65},{65,1},{129,193},{193,129... | collective-permute-start | bytes 24584 | tf_op jit(solution)/shard_map/ppermute | solution.py:31
  9.5 2.2 %collective-permute-start.2 = (f32[16,128]{1,0:T(8,128)S(1)}, f32[16,128]{1,0:T(8,128)S(1)}, u32[]{:S(2)}, u32[]{:S(2)}) collective-permute-start(f32[16,128]{1,0:T(8,128)S(1)} %pad_maximum_fusion), channel_id=1, source_target_pairs={{0,192},{64,128},{128,64},{192,0},{1,193},{65,129},{129,65},{193,1... | collective-permute-start | bytes 24584 | tf_op jit(solution)/shard_map/ppermute | solution.py:31
  11.7 1.9 %prepare.1 = (f32[16,128]{1,0:T(8,128)S(1)}, f32[1,256]{1,0:T(1,128)S(1)}, f32[64,128]{1,0:T(8,128)S(1)}, bf16[8,64]{1,0:T(8,128)(2,1)S(1)}, bf16[64,192]{1,0:T(...) custom-call(s32[2]{0:T(128)} %bitcast.24, ...), custom_call_target="tpu_custom_call" | custom-call | tf_op jit(solution)/shard_map/prepare/pallas_call | solution.py:373
  13.6 0.8 %collective-permute-done.2 = f32[16,128]{1,0:T(8,128)S(1)} collective-permute-done((f32[16,128]{1,0:T(8,128)S(1)}, f32[16,128]{1,0:T(8,128)S(1)}, u32[]{:S(2)}, u32[]{:S(2)}) %collective-permute-start.2) | collective-permute-done | bytes 8224 | tf_op jit(solution)/shard_map/ppermute | solution.py:31
  14.4 0.1 concatenate.8.plane_ref
  14.6 1.1 %collective-permute-start.4 = (f32[48,128]{1,0:T(8,128)S(1)}, f32[48,128]{1,0:T(8,128)S(1)}, u32[]{:S(2)}, u32[]{:S(2)}) collective-permute-start(f32[48,128]{1,0:T(8,128)S(1)} %concatenate.8.plane_ref), channel_id=1, source_target_pairs={{0,4},{4,0},{8,12},{12,8},{16,20},{20,16},{24,28},{28,24},{32,36},... | collective-permute-start | bytes 73736 | tf_op jit(solution)/shard_map/ppermute | solution.py:31
  15.7 0.3 middle.1.gathered_ref
  16.0 3.0 %collective-permute-done.5.got_b_ref = f32[48,128]{1,0:T(8,128)S(1)} collective-permute-done((f32[48,128]{1,0:T(8,128)S(1)}, f32[48,128]{1,0:T(8,128)S(1)}, u32[]{:S(2)}, u32[]{:S(2)}) %collective-permute-start.5) | collective-permute-done | bytes 24608 | tf_op jit(solution)/shard_map/ppermute | solution.py:31
  19.0 5.0 %edges.1 = (bf16[48,128]{1,0:T(8,128)(2,1)S(1)}, bf16[48,128]{1,0:T(8,128)(2,1)S(1)}, f32[2,48,128]{2,1,0:T(8,128)S(1)}, f32[1,256]{1,0:T(1,128)S(1)}) custom-call(f32[48,128]{1,0:T(8,128)S(1)} %concatenate.8.plane_ref, f32[48,128]{1,0:T(8,128)S(1)} %collective-permute-done.4.got_a_ref, f32[48,128]{1,0:T(8,128)S(1)} %collective-permute-done.5.got_b_ref, ...), custom_call_target="tpu_custom_call" | custom-call | tf_op jit(solution)/shard_map/edges/pallas_call | solution.py:373
  24.0 0.1 collective-permute-start.6
  24.3 0.4 %near.1 = (f32[48,128]{1,0:T(8,128)S(1)}, f32[8,128]{1,0:T(8,128)S(1)}) custom-call(f32[2,48,128]{2,1,0:T(8,128)S(1)} %get-tuple-element.52.g_ref, f32[1,256]{1,0:T(1,128)S(1)} %get-tuple-element.53.energy_ref, bf16[144,4096]{1,0:T(8,128)(2,1)S(1)} %get-tuple-element.50.cell_ref, bf16[4096,128]{1,0:T(8,128)(2,1)S(1)} %get-tuple-element.51.pick_ref), custom_call_target="tpu_custom_call" | custom-call | tf_op jit(solution)/shard_map/near/pallas_call | solution.py:373
  24.7 3.8 %collective-permute-done.6 = bf16[48,128]{1,0:T(8,128)(2,1)S(1)} collective-permute-done((bf16[48,128]{1,0:T(8,128)(2,1)S(1)}, bf16[48,128]{1,0:T(8,128)(2,1)S(1)}, u32[]{:S(2)}, u32[]{:S(2)}) %collective-permute-start.6) | collective-permute-done | bytes 12320 | tf_op jit(solution)/shard_map/ppermute | solution.py:31
  28.5 2.3 %collective-permute-start.8 = (f32[16,128]{1,0:T(8,128)S(1)}, f32[16,128]{1,0:T(8,128)S(1)}, u32[]{:S(2)}, u32[]{:S(2)}) collective-permute-start(f32[16,128]{1,0:T(8,128)S(1)} %get-tuple-element.71), channel_id=1, source_target_pairs={{0,192},{64,128},{128,64},{192,0},{1,193},{65,129},{129,65},{193,1... | collective-permute-start | bytes 24584 | tf_op jit(solution)/shard_map/ppermute | solution.py:31
  30.8 2.7 %collective-permute-done.8 = f32[16,128]{1,0:T(8,128)S(1)} collective-permute-done((f32[16,128]{1,0:T(8,128)S(1)}, f32[16,128]{1,0:T(8,128)S(1)}, u32[]{:S(2)}, u32[]{:S(2)}) %collective-permute-start.8) | collective-permute-done | bytes 8224 | tf_op jit(solution)/shard_map/ppermute | solution.py:31
  33.4 1.0 %collective-permute-done.9 = f32[16,128]{1,0:T(8,128)S(1)} collective-permute-done((f32[16,128]{1,0:T(8,128)S(1)}, f32[16,128]{1,0:T(8,128)S(1)}, u32[]{:S(2)}, u32[]{:S(2)}) %collective-permute-start.9) | collective-permute-done | bytes 8224 | tf_op jit(solution)/shard_map/ppermute | solution.py:31
  34.4 1.3 %collective-permute-start.11 = (f32[4,128]{1,0:T(4,128)S(1)}, f32[4,128]{1,0:T(4,128)S(1)}, u32[]{:S(2)}, u32[]{:S(2)}) collective-permute-start(f32[4,128]{1,0:T(4,128)S(1)} %get-tuple-element.72), channel_id=1, source_target_pairs={{0,3},{1,2},{2,1},{3,0},{4,7},{5,6},{6,5},{7,4},{8,11},{9,10},{10,... | collective-permute-start | bytes 6152 | tf_op jit(solution)/shard_map/ppermute | solution.py:31
  35.7 0.6 %early.1 = (f32[8,128]{1,0:T(8,128)S(1)}, f32[8,128]{1,0:T(8,128)S(1)}, f32[3,2,128]{2,1,0:T(2,128)}, f32[2,128]{1,0:T(2,128)}) custom-call(f32[8,128]{1,0:T(8,128)S(1)} %get-tuple-element.34.mine_ref, f32[8,128]{1,0:T(8,128)S(1)} %get-tuple-element.35.keep_ref, f32[8,128]{1,0:T(8,128)S(1)} %get-tuple-element.54.own_ref, f32[1,256]{1,0:T(1,128)S(1)} %get-tuple-element.41.occ_ref), custom_call_target="tpu_custom_call" | custom-call | tf_op jit(solution)/shard_map/early/pallas_call | solution.py:373
  36.3 3.0 %collective-permute-done.11.got_b_ref = f32[4,128]{1,0:T(4,128)S(1)} collective-permute-done((f32[4,128]{1,0:T(4,128)S(1)}, f32[4,128]{1,0:T(4,128)S(1)}, u32[]{:S(2)}, u32[]{:S(2)}) %collective-permute-start.11) | collective-permute-done | bytes 2080 | tf_op jit(solution)/shard_map/ppermute | solution.py:31
  39.3 0.6 %finish.1 = (f32[3,2,128]{2,1,0:T(2,128)}, f32[3,2,128]{2,1,0:T(2,128)}) custom-call(f32[16,128]{1,0:T(8,128)S(1)} %add.24.mid_ref, f32[4,128]{1,0:T(4,128)S(1)} %collective-permute-done.10.got_a_ref, f32[4,128]{1,0:T(4,128)S(1)} %collective-permute-done.11.got_b_ref, f32[8,128]{1,0:T(8,128)S(1)} %get-tuple-element.54.own_ref, ...), custom_call_target="tpu_custom_call" | custom-call | tf_op jit(solution)/shard_map/finish/pallas_call | solution.py:373
  (18 shorter events, 0.3 us)
Async XLA Ops:
  1.4 4.9 %collective-permute-start = (f32[4,128]{1,0:T(4,128)S(1)}, f32[4,128]{1,0:T(4,128)S(1)}, u32[]{:S(2)}, u32[]{:S(2)}) collective-permute-start(f32[4,128]{1,0:T(4,128)S(1)} %get-tuple-element.37), channel_id=1, source_target_pairs={{0,3},{1,2},{2,1},{3,0},{4,7},{5,6},{6,5},{7,4},{8,11},{9,10},{10,... | collective-permute-start | bytes 6152 | tf_op jit(solution)/shard_map/ppermute | solution.py:31
  4.2 3.6 %collective-permute-start.1 = (f32[4,128]{1,0:T(4,128)S(1)}, f32[4,128]{1,0:T(4,128)S(1)}, u32[]{:S(2)}, u32[]{:S(2)}) collective-permute-start(f32[4,128]{1,0:T(4,128)S(1)} %get-tuple-element.38), channel_id=1, source_target_pairs={{0,1},{1,0},{2,3},{3,2},{4,5},{5,4},{6,7},{7,6},{8,9},{9,8},{10,11... | collective-permute-start | bytes 6152 | tf_op jit(solution)/shard_map/ppermute | solution.py:31
  7.8 5.8 %collective-permute-start.3 = (f32[16,128]{1,0:T(8,128)S(1)}, f32[16,128]{1,0:T(8,128)S(1)}, u32[]{:S(2)}, u32[]{:S(2)}) collective-permute-start(f32[16,128]{1,0:T(8,128)S(1)} %pad_maximum_fusion), channel_id=1, source_target_pairs={{0,64},{64,0},{128,192},{192,128},{1,65},{65,1},{129,193},{193,129... | collective-permute-start | bytes 24584 | tf_op jit(solution)/shard_map/ppermute | solution.py:31
  9.5 4.9 %collective-permute-start.2 = (f32[16,128]{1,0:T(8,128)S(1)}, f32[16,128]{1,0:T(8,128)S(1)}, u32[]{:S(2)}, u32[]{:S(2)}) collective-permute-start(f32[16,128]{1,0:T(8,128)S(1)} %pad_maximum_fusion), channel_id=1, source_target_pairs={{0,192},{64,128},{128,64},{192,0},{1,193},{65,129},{129,65},{193,1... | collective-permute-start | bytes 24584 | tf_op jit(solution)/shard_map/ppermute | solution.py:31
  14.5 4.5 %collective-permute-start.5 = (f32[48,128]{1,0:T(8,128)S(1)}, f32[48,128]{1,0:T(8,128)S(1)}, u32[]{:S(2)}, u32[]{:S(2)}) collective-permute-start(f32[48,128]{1,0:T(8,128)S(1)} %concatenate.8.plane_ref), channel_id=1, source_target_pairs={{0,60},{4,8},{8,4},{12,16},{16,12},{20,24},{24,20},{28,32},{32,28}... | collective-permute-start | bytes 73736 | tf_op jit(solution)/shard_map/ppermute | solution.py:31
  14.6 4.5 %collective-permute-start.4 = (f32[48,128]{1,0:T(8,128)S(1)}, f32[48,128]{1,0:T(8,128)S(1)}, u32[]{:S(2)}, u32[]{:S(2)}) collective-permute-start(f32[48,128]{1,0:T(8,128)S(1)} %concatenate.8.plane_ref), channel_id=1, source_target_pairs={{0,4},{4,0},{8,12},{12,8},{16,20},{20,16},{24,28},{28,24},{32,36},... | collective-permute-start | bytes 73736 | tf_op jit(solution)/shard_map/ppermute | solution.py:31
  24.0 4.4 %collective-permute-start.6 = (bf16[48,128]{1,0:T(8,128)(2,1)S(1)}, bf16[48,128]{1,0:T(8,128)(2,1)S(1)}, u32[]{:S(2)}, u32[]{:S(2)}) collective-permute-start(bf16[48,128]{1,0:T(8,128)(2,1)S(1)} %get-tuple-element.57), channel_id=1, source_target_pairs={{0,60},{4,8},{8,4},{12,16},{16,12},{20,24},{24,20},{28,32},{32,28}... | collective-permute-start | bytes 36872 | tf_op jit(solution)/shard_map/ppermute | solution.py:31
  24.2 4.3 %collective-permute-start.7 = (bf16[48,128]{1,0:T(8,128)(2,1)S(1)}, bf16[48,128]{1,0:T(8,128)(2,1)S(1)}, u32[]{:S(2)}, u32[]{:S(2)}) collective-permute-start(bf16[48,128]{1,0:T(8,128)(2,1)S(1)} %get-tuple-element.58), channel_id=1, source_target_pairs={{0,4},{4,0},{8,12},{12,8},{16,20},{20,16},{24,28},{28,24},{32,36},... | collective-permute-start | bytes 36872 | tf_op jit(solution)/shard_map/ppermute | solution.py:31
  28.5 4.9 %collective-permute-start.8 = (f32[16,128]{1,0:T(8,128)S(1)}, f32[16,128]{1,0:T(8,128)S(1)}, u32[]{:S(2)}, u32[]{:S(2)}) collective-permute-start(f32[16,128]{1,0:T(8,128)S(1)} %get-tuple-element.71), channel_id=1, source_target_pairs={{0,192},{64,128},{128,64},{192,0},{1,193},{65,129},{129,65},{193,1... | collective-permute-start | bytes 24584 | tf_op jit(solution)/shard_map/ppermute | solution.py:31
  30.8 3.7 %collective-permute-start.9 = (f32[16,128]{1,0:T(8,128)S(1)}, f32[16,128]{1,0:T(8,128)S(1)}, u32[]{:S(2)}, u32[]{:S(2)}) collective-permute-start(f32[16,128]{1,0:T(8,128)S(1)} %get-tuple-element.70), channel_id=1, source_target_pairs={{0,64},{64,0},{128,192},{192,128},{1,65},{65,1},{129,193},{193,129... | collective-permute-start | bytes 24584 | tf_op jit(solution)/shard_map/ppermute | solution.py:31
  34.4 4.9 %collective-permute-start.11 = (f32[4,128]{1,0:T(4,128)S(1)}, f32[4,128]{1,0:T(4,128)S(1)}, u32[]{:S(2)}, u32[]{:S(2)}) collective-permute-start(f32[4,128]{1,0:T(4,128)S(1)} %get-tuple-element.72), channel_id=1, source_target_pairs={{0,3},{1,2},{2,1},{3,0},{4,7},{5,6},{6,5},{7,4},{8,11},{9,10},{10,... | collective-permute-start | bytes 6152 | tf_op jit(solution)/shard_map/ppermute | solution.py:31
  35.7 3.6 %collective-permute-start.10 = (f32[4,128]{1,0:T(4,128)S(1)}, f32[4,128]{1,0:T(4,128)S(1)}, u32[]{:S(2)}, u32[]{:S(2)}) collective-permute-start(f32[4,128]{1,0:T(4,128)S(1)} %get-tuple-element.73), channel_id=1, source_target_pairs={{0,1},{1,0},{2,3},{3,2},{4,5},{5,4},{6,7},{7,6},{8,9},{9,8},{10,11... | collective-permute-start | bytes 6152 | tf_op jit(solution)/shard_map/ppermute | solution.py:31

commit v8 on v7

--- a/solution.py
+++ b/solution.py
@@ -94,7 +94,7 @@
     count_ref, codes_ref, emb_ref, w1_ref, w2_ref, wnt_ref, we_ref,
     side_ref, occ_ref, web_ref, w1c_ref, w2c_ref, wntc_ref, wc_ref, w2t_ref, wn_ref, embt_ref, off_ref, slot_ref, cell_ref, pick_ref,
 ):
-    side_ref[...] = jnp.where(lax.axis_index("gx") % 2 == 0, jnp.ones((16, CAP), F32), jnp.zeros((16, CAP), F32))
+    side_ref[...] = jnp.where(lax.axis_index("gz") % 2 == 0, jnp.ones((4, CAP), F32), jnp.zeros((4, CAP), F32))
     slot_number = lax.broadcasted_iota(jnp.int32, (1, CAP), 1)
     for r in range(R):
         occ_ref[:, r * CAP:(r + 1) * CAP] = jnp.where(slot_number < count_ref[r], 1.0, 0.0)
@@ -388,7 +388,7 @@
 
 def prepare(count, codes, embed, w1, w2, wnt, we):
     outs = [
-        ((16, CAP), F32), ((1, W), F32), ((CH, CAP), F32), ((NB, CH), BF16), ((CH, 3 * CH), BF16), ((CH, 4 * CH), BF16),
+        ((4, CAP), F32), ((1, W), F32), ((CH, CAP), F32), ((NB, CH), BF16), ((CH, 3 * CH), BF16), ((CH, 4 * CH), BF16),
         ((2 * CH, NB + 16), BF16), ((3 * CH, CH), BF16), ((4 * CH, CH), BF16), ((CH, 16), BF16),
         ((R, K, CAP), jnp.int32), ((R, K, CAP), jnp.int32), ((144, K * W), BF16), ((K * W, CAP), BF16),
     ]
@@ -456,11 +456,12 @@
 
     got_a, got_b = swap(send_a, "gz", False), swap(send_b, "gz", True)
     column = jnp.concatenate(
-        [jnp.where(even_z, got_b, got_a), mine, jnp.where(even_z, got_a, got_b)], axis=0
+        [jnp.where(side > 0.5, got_b, got_a), mine, jnp.where(side > 0.5, got_a, got_b)], axis=0
     )
     got_a, got_b = swap(column, "gx", False), swap(column, "gx", True)
+    low, high = lax.optimization_barrier((jnp.where(even_x, got_b, 0.0), jnp.where(even_x, 0.0, got_b)))
     plane = jnp.concatenate(
-        [jnp.where(side > 0.5, got_b, got_a), column, jnp.where(side > 0.5, got_a, got_b)], axis=0
+        [jnp.where(even_x, low, got_a), column, jnp.where(even_x, got_a, high)], axis=0
     )
     gathered = middle(plane, prepared)
     got_a, got_b = swap(plane, "gy", False), swap(plane, "gy", True)

time: 40.1 us -> 39.4 us (0.983)
  starting transfers between devices: 11.9 us -> 10.3 us
  waiting for transfers between devices: 17.5 us -> 18.4 us
    ppermute x12, starting transfers between devices: 11.9 us -> 10.3 us  [swap(): return lax.ppermute(array, axis, pairs)]
    ppermute x12, waiting for transfers between devices: 17.5 us -> 18.4 us  [swap(): return lax.ppermute(array, axis, pairs)]
  transfers between devices with their start and end apart: 12 -> 12, of which waited for: 8 -> 7; matrix products, arithmetic and copies ran while one was open for 0% -> 0% of each run, Pallas kernels for 8% -> 8%
where the time goes in v8:
time: 39.4 us; the launch traced here: 39.2 us
  waiting for transfers between devices  18.4 us (47%)
  starting transfers between devices  10.3 us (26%)
  Pallas kernels  9.63 us (24%)
  between operations  0.74 us (2%)
    ppermute x12, waiting for transfers between devices, swap(): return lax.ppermute(array, axis, pairs)  18.4 us
    ppermute x12, starting transfers between devices, swap(): return lax.ppermute(array, axis, pairs)  10.3 us
    pallas_call x7, Pallas kernels, call(): pl.pallas_call(kernel, in_specs=[SMEM] * smem + [VMEM] * (len(args) - sme...  9.63 us
  transfers between devices with their start and end apart: 12, of which 7 were waited for; matrix products, arithmetic and copies ran while one was open for 0% of the time, Pallas kernels for 8%

profile of v8, /device:TPU:128, one launch (start us, length us, event | category | flops | bytes accessed | tf_op | source)
XLA Modules:
  0.0 39.2 jit_solution(2002871380249553013)
XLA Ops:
  0.6 0.8 %begin.1 = (f32[4,128]{1,0:T(4,128)S(1)}, f32[4,128]{1,0:T(4,128)S(1)}, f32[8,128]{1,0:T(8,128)S(1)}, f32[8,128]{1,0:T(8,128)S(1)}) custom-call(f32[3,2,128]{2,1,0:T(2,128)} %bitcast.20, f32[3,2,128]{2,1,0:T(2,128)} %bitcast.21, f32[3,2,128]{2,1,0:T(2,128)} %bitcast.22, s32[2,128]{1,0:T(2,128)} %bitcast.23), custom_call_target="tpu_custom_call" | custom-call | tf_op jit(solution)/shard_map/begin/pallas_call | solution.py:373
  1.4 2.8 %collective-permute-start = (f32[4,128]{1,0:T(4,128)S(1)}, f32[4,128]{1,0:T(4,128)S(1)}, u32[]{:S(2)}, u32[]{:S(2)}) collective-permute-start(f32[4,128]{1,0:T(4,128)S(1)} %get-tuple-element.39), channel_id=1, source_target_pairs={{0,3},{1,2},{2,1},{3,0},{4,7},{5,6},{6,5},{7,4},{8,11},{9,10},{10,... | collective-permute-start | bytes 6152 | tf_op jit(solution)/shard_map/ppermute | solution.py:31
  4.2 0.2 collective-permute-start.1
  4.4 1.9 %prepare.1 = (f32[4,128]{1,0:T(4,128)S(1)}, f32[1,256]{1,0:T(1,128)S(1)}, f32[64,128]{1,0:T(8,128)S(1)}, bf16[8,64]{1,0:T(8,128)(2,1)S(1)}, bf16[64,192]{1,0:T(8...) custom-call(s32[2]{0:T(128)} %bitcast.24, ...), custom_call_target="tpu_custom_call" | custom-call | tf_op jit(solution)/shard_map/prepare/pallas_call | solution.py:373
  6.4 1.4 %collective-permute-done.1 = f32[4,128]{1,0:T(4,128)S(1)} collective-permute-done((f32[4,128]{1,0:T(4,128)S(1)}, f32[4,128]{1,0:T(4,128)S(1)}, u32[]{:S(2)}, u32[]{:S(2)}) %collective-permute-start.1) | collective-permute-done | bytes 2080 | tf_op jit(solution)/shard_map/ppermute | solution.py:31
  7.8 3.1 %collective-permute-start.2 = (f32[16,128]{1,0:T(8,128)S(1)}, f32[16,128]{1,0:T(8,128)S(1)}, u32[]{:S(2)}, u32[]{:S(2)}) collective-permute-start(f32[16,128]{1,0:T(8,128)S(1)} %pad_maximum_fusion), channel_id=1, source_target_pairs={{0,192},{64,128},{128,64},{192,0},{1,193},{65,129},{129,65},{193,1... | collective-permute-start | bytes 24584 | tf_op jit(solution)/shard_map/ppermute | solution.py:31
  10.9 0.1 collective-permute-start.3
  11.1 1.7 %collective-permute-done.2 = f32[16,128]{1,0:T(8,128)S(1)} collective-permute-done((f32[16,128]{1,0:T(8,128)S(1)}, f32[16,128]{1,0:T(8,128)S(1)}, u32[]{:S(2)}, u32[]{:S(2)}) %collective-permute-start.2) | collective-permute-done | bytes 8224 | tf_op jit(solution)/shard_map/ppermute | solution.py:31
  12.8 1.8 %collective-permute-done.3 = f32[16,128]{1,0:T(8,128)S(1)} collective-permute-done((f32[16,128]{1,0:T(8,128)S(1)}, f32[16,128]{1,0:T(8,128)S(1)}, u32[]{:S(2)}, u32[]{:S(2)}) %collective-permute-start.3) | collective-permute-done | bytes 8224 | tf_op jit(solution)/shard_map/ppermute | solution.py:31
  14.6 0.1 concatenate.8.plane_ref
  14.8 1.1 %collective-permute-start.4 = (f32[48,128]{1,0:T(8,128)S(1)}, f32[48,128]{1,0:T(8,128)S(1)}, u32[]{:S(2)}, u32[]{:S(2)}) collective-permute-start(f32[48,128]{1,0:T(8,128)S(1)} %concatenate.8.plane_ref), channel_id=1, source_target_pairs={{0,4},{4,0},{8,12},{12,8},{16,20},{20,16},{24,28},{28,24},{32,36},... | collective-permute-start | bytes 73736 | tf_op jit(solution)/shard_map/ppermute | solution.py:31
  15.9 0.3 middle.1.gathered_ref
  16.3 3.0 %collective-permute-done.5.got_b_ref = f32[48,128]{1,0:T(8,128)S(1)} collective-permute-done((f32[48,128]{1,0:T(8,128)S(1)}, f32[48,128]{1,0:T(8,128)S(1)}, u32[]{:S(2)}, u32[]{:S(2)}) %collective-permute-start.5) | collective-permute-done | bytes 24608 | tf_op jit(solution)/shard_map/ppermute | solution.py:31
  19.3 5.1 %edges.1 = (bf16[48,128]{1,0:T(8,128)(2,1)S(1)}, bf16[48,128]{1,0:T(8,128)(2,1)S(1)}, f32[2,48,128]{2,1,0:T(8,128)S(1)}, f32[1,256]{1,0:T(1,128)S(1)}) custom-call(f32[48,128]{1,0:T(8,128)S(1)} %concatenate.8.plane_ref, f32[48,128]{1,0:T(8,128)S(1)} %collective-permute-done.4.got_a_ref, f32[48,128]{1,0:T(8,128)S(1)} %collective-permute-done.5.got_b_ref, ...), custom_call_target="tpu_custom_call" | custom-call | tf_op jit(solution)/shard_map/edges/pallas_call | solution.py:373
  24.3 0.1 collective-permute-start.6
  24.4 0.1 collective-permute-start.7
  24.5 0.4 %near.1 = (f32[48,128]{1,0:T(8,128)S(1)}, f32[8,128]{1,0:T(8,128)S(1)}) custom-call(f32[2,48,128]{2,1,0:T(8,128)S(1)} %get-tuple-element.56.g_ref, f32[1,256]{1,0:T(1,128)S(1)} %get-tuple-element.57.energy_ref, bf16[144,4096]{1,0:T(8,128)(2,1)S(1)} %get-tuple-element.54.cell_ref, bf16[4096,128]{1,0:T(8,128)(2,1)S(1)} %get-tuple-element.55.pick_ref), custom_call_target="tpu_custom_call" | custom-call | tf_op jit(solution)/shard_map/near/pallas_call | solution.py:373
  25.0 3.8 %collective-permute-done.6 = bf16[48,128]{1,0:T(8,128)(2,1)S(1)} collective-permute-done((bf16[48,128]{1,0:T(8,128)(2,1)S(1)}, bf16[48,128]{1,0:T(8,128)(2,1)S(1)}, u32[]{:S(2)}, u32[]{:S(2)}) %collective-permute-start.6) | collective-permute-done | bytes 12320 | tf_op jit(solution)/shard_map/ppermute | solution.py:31
  28.8 1.3 %collective-permute-start.8 = (f32[16,128]{1,0:T(8,128)S(1)}, f32[16,128]{1,0:T(8,128)S(1)}, u32[]{:S(2)}, u32[]{:S(2)}) collective-permute-start(f32[16,128]{1,0:T(8,128)S(1)} %get-tuple-element.75), channel_id=1, source_target_pairs={{0,192},{64,128},{128,64},{192,0},{1,193},{65,129},{129,65},{193,1... | collective-permute-start | bytes 24584 | tf_op jit(solution)/shard_map/ppermute | solution.py:31
  30.1 3.6 %collective-permute-done.8 = f32[16,128]{1,0:T(8,128)S(1)} collective-permute-done((f32[16,128]{1,0:T(8,128)S(1)}, f32[16,128]{1,0:T(8,128)S(1)}, u32[]{:S(2)}, u32[]{:S(2)}) %collective-permute-start.8) | collective-permute-done | bytes 8224 | tf_op jit(solution)/shard_map/ppermute | solution.py:31
  33.8 1.3 %collective-permute-start.11 = (f32[4,128]{1,0:T(4,128)S(1)}, f32[4,128]{1,0:T(4,128)S(1)}, u32[]{:S(2)}, u32[]{:S(2)}) collective-permute-start(f32[4,128]{1,0:T(4,128)S(1)} %get-tuple-element.76), channel_id=1, source_target_pairs={{0,3},{1,2},{2,1},{3,0},{4,7},{5,6},{6,5},{7,4},{8,11},{9,10},{10,... | collective-permute-start | bytes 6152 | tf_op jit(solution)/shard_map/ppermute | solution.py:31
  35.1 0.6 %early.1 = (f32[8,128]{1,0:T(8,128)S(1)}, f32[8,128]{1,0:T(8,128)S(1)}, f32[3,2,128]{2,1,0:T(2,128)}, f32[2,128]{1,0:T(2,128)}) custom-call(f32[8,128]{1,0:T(8,128)S(1)} %get-tuple-element.36.mine_ref, f32[8,128]{1,0:T(8,128)S(1)} %get-tuple-element.37.keep_ref, f32[8,128]{1,0:T(8,128)S(1)} %get-tuple-element.58.own_ref, f32[1,256]{1,0:T(1,128)S(1)} %get-tuple-element.45.occ_ref), custom_call_target="tpu_custom_call" | custom-call | tf_op jit(solution)/shard_map/early/pallas_call | solution.py:373
  35.6 3.0 %collective-permute-done.11.got_b_ref = f32[4,128]{1,0:T(4,128)S(1)} collective-permute-done((f32[4,128]{1,0:T(4,128)S(1)}, f32[4,128]{1,0:T(4,128)S(1)}, u32[]{:S(2)}, u32[]{:S(2)}) %collective-permute-start.11) | collective-permute-done | bytes 2080 | tf_op jit(solution)/shard_map/ppermute | solution.py:31
  38.6 0.6 %finish.1 = (f32[3,2,128]{2,1,0:T(2,128)}, f32[3,2,128]{2,1,0:T(2,128)}) custom-call(f32[16,128]{1,0:T(8,128)S(1)} %add.23.mid_ref, f32[4,128]{1,0:T(4,128)S(1)} %collective-permute-done.10.got_a_ref, f32[4,128]{1,0:T(4,128)S(1)} %collective-permute-done.11.got_b_ref, f32[8,128]{1,0:T(8,128)S(1)} %get-tuple-element.58.own_ref, ...), custom_call_target="tpu_custom_call" | custom-call | tf_op jit(solution)/shard_map/finish/pallas_call | solution.py:373
  (19 shorter events, 0.2 us)
Async XLA Ops:
  1.4 5.0 %collective-permute-start = (f32[4,128]{1,0:T(4,128)S(1)}, f32[4,128]{1,0:T(4,128)S(1)}, u32[]{:S(2)}, u32[]{:S(2)}) collective-permute-start(f32[4,128]{1,0:T(4,128)S(1)} %get-tuple-element.39), channel_id=1, source_target_pairs={{0,3},{1,2},{2,1},{3,0},{4,7},{5,6},{6,5},{7,4},{8,11},{9,10},{10,... | collective-permute-start | bytes 6152 | tf_op jit(solution)/shard_map/ppermute | solution.py:31
  4.2 3.6 %collective-permute-start.1 = (f32[4,128]{1,0:T(4,128)S(1)}, f32[4,128]{1,0:T(4,128)S(1)}, u32[]{:S(2)}, u32[]{:S(2)}) collective-permute-start(f32[4,128]{1,0:T(4,128)S(1)} %get-tuple-element.40), channel_id=1, source_target_pairs={{0,1},{1,0},{2,3},{3,2},{4,5},{5,4},{6,7},{7,6},{8,9},{9,8},{10,11... | collective-permute-start | bytes 6152 | tf_op jit(solution)/shard_map/ppermute | solution.py:31
  7.8 4.9 %collective-permute-start.2 = (f32[16,128]{1,0:T(8,128)S(1)}, f32[16,128]{1,0:T(8,128)S(1)}, u32[]{:S(2)}, u32[]{:S(2)}) collective-permute-start(f32[16,128]{1,0:T(8,128)S(1)} %pad_maximum_fusion), channel_id=1, source_target_pairs={{0,192},{64,128},{128,64},{192,0},{1,193},{65,129},{129,65},{193,1... | collective-permute-start | bytes 24584 | tf_op jit(solution)/shard_map/ppermute | solution.py:31
  10.9 3.7 %collective-permute-start.3 = (f32[16,128]{1,0:T(8,128)S(1)}, f32[16,128]{1,0:T(8,128)S(1)}, u32[]{:S(2)}, u32[]{:S(2)}) collective-permute-start(f32[16,128]{1,0:T(8,128)S(1)} %pad_maximum_fusion), channel_id=1, source_target_pairs={{0,64},{64,0},{128,192},{192,128},{1,65},{65,1},{129,193},{193,129... | collective-permute-start | bytes 24584 | tf_op jit(solution)/shard_map/ppermute | solution.py:31
  14.7 4.5 %collective-permute-start.5 = (f32[48,128]{1,0:T(8,128)S(1)}, f32[48,128]{1,0:T(8,128)S(1)}, u32[]{:S(2)}, u32[]{:S(2)}) collective-permute-start(f32[48,128]{1,0:T(8,128)S(1)} %concatenate.8.plane_ref), channel_id=1, source_target_pairs={{0,60},{4,8},{8,4},{12,16},{16,12},{20,24},{24,20},{28,32},{32,28}... | collective-permute-start | bytes 73736 | tf_op jit(solution)/shard_map/ppermute | solution.py:31
  14.8 4.5 %collective-permute-start.4 = (f32[48,128]{1,0:T(8,128)S(1)}, f32[48,128]{1,0:T(8,128)S(1)}, u32[]{:S(2)}, u32[]{:S(2)}) collective-permute-start(f32[48,128]{1,0:T(8,128)S(1)} %concatenate.8.plane_ref), channel_id=1, source_target_pairs={{0,4},{4,0},{8,12},{12,8},{16,20},{20,16},{24,28},{28,24},{32,36},... | collective-permute-start | bytes 73736 | tf_op jit(solution)/shard_map/ppermute | solution.py:31
  24.3 4.4 %collective-permute-start.6 = (bf16[48,128]{1,0:T(8,128)(2,1)S(1)}, bf16[48,128]{1,0:T(8,128)(2,1)S(1)}, u32[]{:S(2)}, u32[]{:S(2)}) collective-permute-start(bf16[48,128]{1,0:T(8,128)(2,1)S(1)} %get-tuple-element.61), channel_id=1, source_target_pairs={{0,60},{4,8},{8,4},{12,16},{16,12},{20,24},{24,20},{28,32},{32,28}... | collective-permute-start | bytes 36872 | tf_op jit(solution)/shard_map/ppermute | solution.py:31
  24.4 4.3 %collective-permute-start.7 = (bf16[48,128]{1,0:T(8,128)(2,1)S(1)}, bf16[48,128]{1,0:T(8,128)(2,1)S(1)}, u32[]{:S(2)}, u32[]{:S(2)}) collective-permute-start(bf16[48,128]{1,0:T(8,128)(2,1)S(1)} %get-tuple-element.62), channel_id=1, source_target_pairs={{0,4},{4,0},{8,12},{12,8},{16,20},{20,16},{24,28},{28,24},{32,36},... | collective-permute-start | bytes 36872 | tf_op jit(solution)/shard_map/ppermute | solution.py:31
  28.8 4.9 %collective-permute-start.8 = (f32[16,128]{1,0:T(8,128)S(1)}, f32[16,128]{1,0:T(8,128)S(1)}, u32[]{:S(2)}, u32[]{:S(2)}) collective-permute-start(f32[16,128]{1,0:T(8,128)S(1)} %get-tuple-element.75), channel_id=1, source_target_pairs={{0,192},{64,128},{128,64},{192,0},{1,193},{65,129},{129,65},{193,1... | collective-permute-start | bytes 24584 | tf_op jit(solution)/shard_map/ppermute | solution.py:31
  30.1 3.7 %collective-permute-start.9 = (f32[16,128]{1,0:T(8,128)S(1)}, f32[16,128]{1,0:T(8,128)S(1)}, u32[]{:S(2)}, u32[]{:S(2)}) collective-permute-start(f32[16,128]{1,0:T(8,128)S(1)} %get-tuple-element.74), channel_id=1, source_target_pairs={{0,64},{64,0},{128,192},{192,128},{1,65},{65,1},{129,193},{193,129... | collective-permute-start | bytes 24584 | tf_op jit(solution)/shard_map/ppermute | solution.py:31
  33.8 4.9 %collective-permute-start.11 = (f32[4,128]{1,0:T(4,128)S(1)}, f32[4,128]{1,0:T(4,128)S(1)}, u32[]{:S(2)}, u32[]{:S(2)}) collective-permute-start(f32[4,128]{1,0:T(4,128)S(1)} %get-tuple-element.76), channel_id=1, source_target_pairs={{0,3},{1,2},{2,1},{3,0},{4,7},{5,6},{6,5},{7,4},{8,11},{9,10},{10,... | collective-permute-start | bytes 6152 | tf_op jit(solution)/shard_map/ppermute | solution.py:31
  35.1 3.6 %collective-permute-start.10 = (f32[4,128]{1,0:T(4,128)S(1)}, f32[4,128]{1,0:T(4,128)S(1)}, u32[]{:S(2)}, u32[]{:S(2)}) collective-permute-start(f32[4,128]{1,0:T(4,128)S(1)} %get-tuple-element.77), channel_id=1, source_target_pairs={{0,1},{1,0},{2,3},{3,2},{4,5},{5,4},{6,7},{7,6},{8,9},{9,8},{10,11... | collective-permute-start | bytes 6152 | tf_op jit(solution)/shard_map/ppermute | solution.py:31
